TPU v7x, 256 devices: a whole 4x4x8 slice. The times are simulated.
256 devices in a mesh: cols: 8 (over x, z_hi), sites: 32 (over y, z_lo, core).
Axes of the slice: x: 4, y: 4, z: 8 (z_hi: 2, z_lo: 4; z = z_hi * 4 + z_lo), core: 2. Of those that a mesh axis runs over, the one named last changes fastest.
Arguments:
- right_vectors: float32 [2, 16, 8, 32, 256, 32], P(None, None, None, None, ('cols', 'sites')), may hold values from -6 to 6
- left_vectors: bfloat16 [2, 64, 512, 512], P(None, None, 'sites'), may hold values from -0.01171875 to 0.01171875
- vacancy: int32 [512, 512], P('sites'), may hold values 0 or 1
Outputs:
- gamma_moments: float32 [2, 4, 64, 16, 8], P(None, None, None, None, 'cols')
All inputs are finite; a program needn't handle non-finite values. No bound on the sum of `vacancy` on one device may be relied on, other than what follows from the above.
Results may differ from a plain program's by a relative error of at most 0.0029.
Values sent between devices are 32-bit elements; how exact they have to be, the bound alone decides.
No kernel may reach another device: no remote copies, remote signals or barrier semaphores. Data moves between devices by JAX's collectives and lax.ppermute only.
A program may use at most 64 MiB of HBM per device.

v0:
```python
import jax
import jax.numpy as jnp
from jax import lax
from jax.experimental import pallas as pl
from jax.experimental.pallas import tpu as pltpu
from jax.sharding import PartitionSpec as P

MOM = 4
HALO = 4
ONSITE_MASS = 0.3
SECOND_HOP = 0.2
BAND_SCALE = 4.5
LANES = 128
SUB = 8
F32 = jnp.float32


def pack_kernel(in_ref, out_ref):
    slabs = out_ref.shape[0]
    for slab in range(slabs):
        parts = [in_ref[q * SUB : (q + 1) * SUB, slab, :] for q in range(4)]
        out_ref[slab] = jnp.concatenate(parts, axis=1)


def pack(pieces):
    rg, groups, slabs, width = pieces.shape
    return pl.pallas_call(
        pack_kernel,
        grid=(groups,),
        in_specs=[pl.BlockSpec((rg, None, slabs, width), lambda k: (0, k, 0, 0))],
        out_specs=pl.BlockSpec((slabs, SUB, LANES), lambda k: (k, 0, 0)),
        out_shape=jax.ShapeDtypeStruct((groups * slabs, SUB, LANES), F32),
        name="pack",
    )(pieces)


def shift_right_of(tiles, is_last):
    rolled = [pltpu.roll(t, LANES - 1, 1) for t in tiles]
    following = rolled[1:] + [jnp.zeros_like(rolled[0])]
    return [jnp.where(is_last, b, a) for a, b in zip(rolled, following)]


def shift_left_of(tiles, is_first):
    rolled = [pltpu.roll(t, 1, 1) for t in tiles]
    before = [jnp.zeros_like(rolled[0])] + rolled[:-1]
    return [jnp.where(is_first, b, a) for a, b in zip(rolled, before)]


def regroup(pieces, low_half, even_block):
    a = [None] * 4
    for p in (0, 1):
        a[p] = jnp.where(low_half, pieces[p], pltpu.roll(pieces[p + 2], 64, 1))
        a[p + 2] = jnp.where(low_half, pltpu.roll(pieces[p], 64, 1), pieces[p + 2])
    b = [None] * 4
    for p in (0, 2):
        b[p] = jnp.where(even_block, a[p], pltpu.roll(a[p + 1], 32, 1))
        b[p + 1] = jnp.where(even_block, pltpu.roll(a[p], 96, 1), a[p + 1])
    return b


def moments_kernel(recv_ref, lo_ref, hi_ref, pres_ref, left_ref, out_ref, field, mrow):
    rows = left_ref.shape[0]
    ext = rows + 2 * HALO
    width = left_ref.shape[2]
    tiles = width // LANES
    lane = lax.broadcasted_iota(jnp.int32, (SUB, LANES), 1)
    low_half = lane < 64
    even_block = (lane // 32) % 2 == 0
    is_first = lane == 0
    is_last = lane == LANES - 1
    even_lane = lane % 2 == 0
    plus = jnp.where(even_lane, 1.0, -1.0).astype(F32)

    def load(ref, lead):
        return [ref[(*lead, slice(None), pl.ds(t * LANES, LANES))] for t in range(tiles)]

    def store(ref, lead, values):
        for t in range(tiles):
            ref[(*lead, slice(None), pl.ds(t * LANES, LANES))] = values[t]

    def unpack_row(src, src_row, e):
        pres = load(pres_ref, (e,))
        for t in range(tiles):
            pieces = [src[src_row * 16 + t * 4 + p] for p in range(4)]
            for q, value in enumerate(regroup(pieces, low_half, even_block)):
                field[0, e, q // 2, q % 2, :, pl.ds(t * LANES, LANES)] = value * pres[t]

    @pl.loop(0, HALO)
    def _(i):
        unpack_row(lo_ref, i, i)
        unpack_row(hi_ref, i, rows + HALO + i)

    @pl.loop(0, rows)
    def _(i):
        unpack_row(recv_ref, i, i + HALO)

    def row(level, e, parity, half):
        sign = plus if parity == 0 else -plus
        up_mask = even_lane if parity == 0 else jnp.logical_not(even_lane)
        c = [load(field, (level, e, r, half)) for r in (0, 1)]
        u = [load(field, (level, e + 1, r, half)) for r in (0, 1)]
        l = [load(field, (level, e - 1, r, half)) for r in (0, 1)]
        pres = load(pres_ref, (e,))
        f = [[sign * a for a in c[r]] for r in (0, 1)]
        d = [[sign * (a + b) for a, b in zip(u[r], l[r])] for r in (0, 1)]
        fr = [shift_right_of(f[r], is_last) for r in (0, 1)]
        fl = [shift_left_of(f[r], is_first) for r in (0, 1)]
        T = range(tiles)
        if level == 0:
            right = [
                [-c[1][t] - SECOND_HOP * d[0][t] - 2 * SECOND_HOP * fr[0][t] for t in T],
                [c[0][t] - SECOND_HOP * d[1][t] - 2 * SECOND_HOP * fr[1][t] for t in T],
            ]
            left = [
                [c[1][t] - SECOND_HOP * d[0][t] - 2 * SECOND_HOP * fl[0][t] for t in T],
                [-c[0][t] - SECOND_HOP * d[1][t] - 2 * SECOND_HOP * fl[1][t] for t in T],
            ]
        else:
            right = [
                [c[0][t] - SECOND_HOP * (d[1][t] + fr[1][t]) for t in T],
                [c[1][t] + SECOND_HOP * (d[0][t] + fr[0][t]) for t in T],
            ]
            left = [
                [c[0][t] + SECOND_HOP * (d[1][t] + fl[1][t]) for t in T],
                [c[1][t] - SECOND_HOP * (d[0][t] + fl[0][t]) for t in T],
            ]
        result = []
        for r in (0, 1):
            a = shift_right_of(right[r], is_last)
            b = shift_left_of(left[r], is_first)
            total = [a[t] + b[t] for t in T]
            if level > 0:
                vert = [jnp.where(up_mask, u[r][t], l[r][t]) for t in T]
                total = [total[t] + (ONSITE_MASS * f[r][t] + vert[t]) for t in T]
                scale = 1.0 / BAND_SCALE if level == 1 else 2.0 / BAND_SCALE
                total = [total[t] * (scale * pres[t]) for t in T]
                if level > 1:
                    old = load(field, (level - 1, e, r, half))
                    total = [total[t] - old[t] for t in T]
            else:
                total = [total[t] * pres[t] for t in T]
            result.append(total)
        return result

    for level in range(MOM):
        reach = HALO - 1 - level
        first = HALO - reach
        @pl.loop(0, (rows + 2 * reach) // 2)
        def _(i, level=level, first=first):
            for k in (0, 1):
                e = first + 2 * i + k
                for half in (0, 1):
                    values = row(level, e, (first + k) % 2, half)
                    if level < MOM - 1:
                        for r in (0, 1):
                            store(field, (level + 1, e, r, half), values[r])
                    else:
                        for r in (0, 1):
                            store(mrow, (e - HALO, r, half), values[r])

    acc = jnp.zeros((2 * left_ref.shape[1] // 2, left_ref.shape[1]), F32)

    def product(y, acc):
        stacked = []
        for r in (0, 1):
            for m in range(MOM):
                for half in (0, 1):
                    if m < MOM - 1:
                        stacked.append(field[m + 1, y + HALO, r, half])
                    else:
                        stacked.append(mrow[y, r, half])
        rhs = jnp.concatenate(stacked, axis=0).astype(jnp.bfloat16)
        return acc + lax.dot_general(
            rhs, left_ref[y], (((1,), (1,)), ((), ())), preferred_element_type=F32
        )

    acc = lax.fori_loop(0, rows, product, jnp.zeros((2 * MOM * 2 * SUB, left_ref.shape[1]), F32))
    half_rows = MOM * 2 * SUB
    top, bottom = acc[:half_rows], acc[half_rows:]
    lane_out = lax.broadcasted_iota(jnp.int32, top.shape, 1)
    out_ref[...] = pltpu.roll(bottom, 64, 1) + jnp.where(lane_out < 64, top, -top)


def moments(recv, lo, hi, pres, left):
    rows, n2, width = left.shape
    ext = rows + 2 * HALO
    vm = pl.BlockSpec(memory_space=pltpu.VMEM)
    return pl.pallas_call(
        moments_kernel,
        in_specs=[vm] * 5,
        out_specs=vm,
        out_shape=jax.ShapeDtypeStruct((MOM * 2 * SUB, n2), F32),
        scratch_shapes=[
            pltpu.VMEM((MOM, ext, 2, 2, SUB, width), F32),
            pltpu.VMEM((rows, 2, 2, SUB, width), F32),
        ],
        compiler_params=pltpu.CompilerParams(vmem_limit_bytes=40 * 2**20),
        name="moments",
    )(recv, lo, hi, pres, left)


def per_device(right_vectors, left_vectors, vacancy):
    parts, width_group, groups, slabs, _, piece = right_vectors.shape
    count = lax.axis_size("sites")
    up = [(i, (i + 1) % count) for i in range(count)]
    down = [((i + 1) % count, i) for i in range(count)]
    n_left, rows, width = left_vectors.shape[1:]

    present = vacancy.astype(F32)
    pres_ext = jnp.concatenate(
        [
            lax.ppermute(present[rows - HALO :], "sites", up),
            present,
            lax.ppermute(present[:HALO], "sites", down),
        ],
        axis=0,
    )
    pres_ext = jnp.broadcast_to(pres_ext[:, None, :], (rows + 2 * HALO, SUB, width))
    left = jnp.swapaxes(left_vectors.reshape(2 * n_left, rows, width), 0, 1)

    packed = pack(right_vectors.reshape(parts * width_group, groups, slabs, piece))
    recv = lax.all_to_all(packed, ("cols", "sites"), 0, 0, tiled=True)
    edge = HALO * width // piece
    lo = lax.ppermute(recv[recv.shape[0] - edge :], "sites", up)
    hi = lax.ppermute(recv[:edge], "sites", down)
    total = moments(recv, lo, hi, pres_ext, left)
    step = 1
    while step < count:
        total = total + lax.ppermute(total, "sites", [(i, i ^ step) for i in range(count)])
        step *= 2
    out = total.reshape(MOM, width_group, 2, n_left)
    return jnp.transpose(out, (2, 0, 3, 1))[..., None]


def solution(mesh):
    return jax.shard_map(
        per_device,
        mesh=mesh,
        in_specs=(
            P(None, None, None, None, ("cols", "sites"), None),
            P(None, None, "sites", None),
            P("sites", None),
        ),
        out_specs=P(None, None, None, None, "cols"),
        check_vma=False,
    )
```

profile of v0, /device:TPU:2, one launch (start us, length us, event | category | flops | bytes accessed | tf_op | source)
XLA Modules:
  0.0 100.5 jit_solution(7352883156500880876)
XLA Ops:
  0.0 6.9 %pack.1 = f32[256,8,128]{2,1,0:T(8,128)} custom-call(f32[32,8,32,32]{3,2,1,0:T(8,128)} %bitcast.8), custom_call_target="tpu_custom_call" | custom-call | tf_op jit(solution)/shard_map/pack/pallas_call | solution.py:27
  6.9 14.7 %all-to-all-start = ((f32[256,8,128]{2,1,0:T(8,128)}), f32[256,8,128]{2,1,0:T(8,128)S(1)}, u32[]{:S(2)}, u32[]{:S(2)}) async-start(f32[256,8,128]{2,1,0:T(8,128)} %pack.1), calls=%async_computation | async-start | bytes 2097152 | tf_op jit(solution)/shard_map/all_to_all | solution.py:222
  21.6 30.2 %all-to-all-done.recv_ref = f32[256,8,128]{2,1,0:T(8,128)S(1)} async-done(((f32[256,8,128]{2,1,0:T(8,128)}), f32[256,8,128]{2,1,0:T(8,128)S(1)}, u32[]{:S(2)}, u32[]{:S(2)}) %all-to-all-start) | async-done | bytes 1048608 | tf_op jit(solution)/shard_map/all_to_all | solution.py:222
  51.9 2.0 %collective-permute-start.1 = (f32[64,8,128]{2,1,0:T(8,128)S(1)}, f32[64,8,128]{2,1,0:T(8,128)S(1)}, u32[]{:S(2)}, u32[]{:S(2)}) collective-permute-start(f32[64,8,128]{2,1,0:T(8,128)S(1)} %get-tuple-element.5), channel_id=1, source_target_pairs={{1,0},{2,1},{3,2},{4,3},{5,4},{6,5},{7,6},{8,7},{9,8},{10,9},{11,1... | collective-permute-start | bytes 786440 | tf_op jit(solution)/shard_map/ppermute | solution.py:225
  53.8 0.0 collective-permute-start
  53.8 1.3 %collective-permute-start.2 = (f32[4,512]{1,0:T(4,128)S(1)}, f32[4,512]{1,0:T(4,128)S(1)}, u32[]{:S(2)}, u32[]{:S(2)}) collective-permute-start(f32[4,512]{1,0:T(4,128)S(1)} %get-tuple-element.7), channel_id=1, source_target_pairs={{0,1},{1,2},{2,3},{3,4},{4,5},{5,6},{6,7},{7,8},{8,9},{9,10},{10,1... | collective-permute-start | bytes 24584 | tf_op jit(solution)/shard_map/ppermute | solution.py:212
  55.1 4.5 %collective-permute-start.3 = (f32[4,512]{1,0:T(4,128)S(1)}, f32[4,512]{1,0:T(4,128)S(1)}, u32[]{:S(2)}, u32[]{:S(2)}) collective-permute-start(f32[4,512]{1,0:T(4,128)S(1)} %get-tuple-element.8), channel_id=1, source_target_pairs={{1,0},{2,1},{3,2},{4,3},{5,4},{6,5},{7,6},{8,7},{9,8},{10,9},{11,1... | collective-permute-start | bytes 24584 | tf_op jit(solution)/shard_map/ppermute | solution.py:214
  59.6 1.2 %copy.4 = bf16[2,64,16,512]{3,1,0,2:T(8,128)(2,1)S(1)} copy(bf16[2,64,16,512]{3,2,1,0:T(8,128)(2,1)S(1)} %copy-done) | data formatting | bytes 4194304 | tf_op args[1]
  60.7 3.0 %collective-permute-done.2 = f32[4,512]{1,0:T(4,128)S(1)} collective-permute-done((f32[4,512]{1,0:T(4,128)S(1)}, f32[4,512]{1,0:T(4,128)S(1)}, u32[]{:S(2)}, u32[]{:S(2)}) %collective-permute-start.2) | collective-permute-done | bytes 8224 | tf_op jit(solution)/shard_map/ppermute | solution.py:212
  63.7 0.0 collective-permute-done.1.hi_ref
  63.7 0.0 collective-permute-done.lo_ref
  63.8 16.6 %moments.1 = f32[64,128]{1,0:T(8,128)S(1)} custom-call(f32[256,8,128]{2,1,0:T(8,128)S(1)} %all-to-all-done.recv_ref, f32[64,8,128]{2,1,0:T(8,128)S(1)} %collective-permute-done.lo_ref, f32[64,8,128]{2,1,0:T(8,128)S(1)} %collective-permute-done.1.hi_ref, f32[24,8,512]{2,1,0:T(8,128)S(1)} %broadcast_in_dim.4.pres_ref, bf16[16,128,512]{2,1,0:T(8,128)(2,1)S(1)} %bitcast.7), custom_call_target="tpu_custom_call" | custom-call | tf_op jit(solution)/shard_map/moments/pallas_call | solution.py:188
  80.4 0.1 collective-permute-start.4
  80.5 1.2 %collective-permute-done.4 = f32[64,128]{1,0:T(8,128)S(1)} collective-permute-done((f32[64,128]{1,0:T(8,128)S(1)}, f32[64,128]{1,0:T(8,128)S(1)}, u32[]{:S(2)}, u32[]{:S(2)}) %collective-permute-start.4) | collective-permute-done | bytes 32800 | tf_op jit(solution)/shard_map/ppermute | solution.py:229
  81.7 0.0 collective-permute-start.5
  81.7 3.9 %collective-permute-done.5 = f32[64,128]{1,0:T(8,128)S(1)} collective-permute-done((f32[64,128]{1,0:T(8,128)S(1)}, f32[64,128]{1,0:T(8,128)S(1)}, u32[]{:S(2)}, u32[]{:S(2)}) %collective-permute-start.5) | collective-permute-done | bytes 32800 | tf_op jit(solution)/shard_map/ppermute | solution.py:229
  85.6 0.3 collective-permute-start.6
  85.9 4.5 %collective-permute-done.6 = f32[64,128]{1,0:T(8,128)S(1)} collective-permute-done((f32[64,128]{1,0:T(8,128)S(1)}, f32[64,128]{1,0:T(8,128)S(1)}, u32[]{:S(2)}, u32[]{:S(2)}) %collective-permute-start.6) | collective-permute-done | bytes 32800 | tf_op jit(solution)/shard_map/ppermute | solution.py:229
  90.5 0.5 collective-permute-start.7
  91.0 3.4 %collective-permute-done.7 = f32[64,128]{1,0:T(8,128)S(1)} collective-permute-done((f32[64,128]{1,0:T(8,128)S(1)}, f32[64,128]{1,0:T(8,128)S(1)}, u32[]{:S(2)}, u32[]{:S(2)}) %collective-permute-start.7) | collective-permute-done | bytes 32800 | tf_op jit(solution)/shard_map/ppermute | solution.py:229
  94.4 0.0 collective-permute-start.8
  94.4 5.4 %collective-permute-done.8 = f32[64,128]{1,0:T(8,128)S(1)} collective-permute-done((f32[64,128]{1,0:T(8,128)S(1)}, f32[64,128]{1,0:T(8,128)S(1)}, u32[]{:S(2)}, u32[]{:S(2)}) %collective-permute-start.8) | collective-permute-done | bytes 32800 | tf_op jit(solution)/shard_map/ppermute | solution.py:229
  99.8 0.1 reshape.12
  99.9 0.6 copy.5
  (15 shorter events, 0.1 us)
Async XLA Ops:
  0.0 21.6 %copy-start.1 = (s32[16,512]{1,0:T(8,128)S(1)}, s32[16,512]{1,0:T(8,128)}, u32[]{:S(2)}) copy-start(s32[16,512]{1,0:T(8,128)} %param.5) | copy-start | bytes 98308
  6.9 52.7 %copy-start = (bf16[2,64,16,512]{3,2,1,0:T(8,128)(2,1)S(1)}, bf16[2,64,16,512]{3,2,1,0:T(8,128)(2,1)}, u32[]{:S(2)}) copy-start(bf16[2,64,16,512]{3,2,1,0:T(8,128)(2,1)} %param.4) | copy-start | bytes 6291460
  6.9 44.9 %all-to-all-start = ((f32[256,8,128]{2,1,0:T(8,128)}), f32[256,8,128]{2,1,0:T(8,128)S(1)}, u32[]{:S(2)}, u32[]{:S(2)}) async-start(f32[256,8,128]{2,1,0:T(8,128)} %pack.1), calls=%async_computation | async-start | bytes 2097152 | tf_op jit(solution)/shard_map/all_to_all | solution.py:222
  51.9 11.9 %collective-permute-start.1 = (f32[64,8,128]{2,1,0:T(8,128)S(1)}, f32[64,8,128]{2,1,0:T(8,128)S(1)}, u32[]{:S(2)}, u32[]{:S(2)}) collective-permute-start(f32[64,8,128]{2,1,0:T(8,128)S(1)} %get-tuple-element.5), channel_id=1, source_target_pairs={{1,0},{2,1},{3,2},{4,3},{5,4},{6,5},{7,6},{8,7},{9,8},{10,9},{11,1... | collective-permute-start | bytes 786440 | tf_op jit(solution)/shard_map/ppermute | solution.py:225
  53.8 9.9 %collective-permute-start = (f32[64,8,128]{2,1,0:T(8,128)S(1)}, f32[64,8,128]{2,1,0:T(8,128)S(1)}, u32[]{:S(2)}, u32[]{:S(2)}) collective-permute-start(f32[64,8,128]{2,1,0:T(8,128)S(1)} %get-tuple-element.6), channel_id=1, source_target_pairs={{0,1},{1,2},{2,3},{3,4},{4,5},{5,6},{6,7},{7,8},{8,9},{9,10},{10,1... | collective-permute-start | bytes 786440 | tf_op jit(solution)/shard_map/ppermute | solution.py:224
  53.8 9.9 %collective-permute-start.2 = (f32[4,512]{1,0:T(4,128)S(1)}, f32[4,512]{1,0:T(4,128)S(1)}, u32[]{:S(2)}, u32[]{:S(2)}) collective-permute-start(f32[4,512]{1,0:T(4,128)S(1)} %get-tuple-element.7), channel_id=1, source_target_pairs={{0,1},{1,2},{2,3},{3,4},{4,5},{5,6},{6,7},{7,8},{8,9},{9,10},{10,1... | collective-permute-start | bytes 24584 | tf_op jit(solution)/shard_map/ppermute | solution.py:212
  55.1 8.6 %collective-permute-start.3 = (f32[4,512]{1,0:T(4,128)S(1)}, f32[4,512]{1,0:T(4,128)S(1)}, u32[]{:S(2)}, u32[]{:S(2)}) collective-permute-start(f32[4,512]{1,0:T(4,128)S(1)} %get-tuple-element.8), channel_id=1, source_target_pairs={{1,0},{2,1},{3,2},{4,3},{5,4},{6,5},{7,6},{8,7},{9,8},{10,9},{11,1... | collective-permute-start | bytes 24584 | tf_op jit(solution)/shard_map/ppermute | solution.py:214
  80.4 1.3 %collective-permute-start.4 = (f32[64,128]{1,0:T(8,128)S(1)}, f32[64,128]{1,0:T(8,128)S(1)}, u32[]{:S(2)}, u32[]{:S(2)}) collective-permute-start(f32[64,128]{1,0:T(8,128)S(1)} %moments.1), channel_id=1, source_target_pairs={{0,1},{1,0},{2,3},{3,2},{4,5},{5,4},{6,7},{7,6},{8,9},{9,8},{10,11... | collective-permute-start | bytes 98312 | tf_op jit(solution)/shard_map/ppermute | solution.py:229
  81.7 3.9 %collective-permute-start.5 = (f32[64,128]{1,0:T(8,128)S(1)}, f32[64,128]{1,0:T(8,128)S(1)}, u32[]{:S(2)}, u32[]{:S(2)}) collective-permute-start(f32[64,128]{1,0:T(8,128)S(1)} %add.15), channel_id=1, source_target_pairs={{0,2},{1,3},{2,0},{3,1},{4,6},{5,7},{6,4},{7,5},{8,10},{9,11},{10,... | collective-permute-start | bytes 98312 | tf_op jit(solution)/shard_map/ppermute | solution.py:229
  85.6 4.8 %collective-permute-start.6 = (f32[64,128]{1,0:T(8,128)S(1)}, f32[64,128]{1,0:T(8,128)S(1)}, u32[]{:S(2)}, u32[]{:S(2)}) collective-permute-start(f32[64,128]{1,0:T(8,128)S(1)} %add.16), channel_id=1, source_target_pairs={{0,4},{1,5},{2,6},{3,7},{4,0},{5,1},{6,2},{7,3},{8,12},{9,13},{10,... | collective-permute-start | bytes 98312 | tf_op jit(solution)/shard_map/ppermute | solution.py:229
  90.5 3.9 %collective-permute-start.7 = (f32[64,128]{1,0:T(8,128)S(1)}, f32[64,128]{1,0:T(8,128)S(1)}, u32[]{:S(2)}, u32[]{:S(2)}) collective-permute-start(f32[64,128]{1,0:T(8,128)S(1)} %add.17), channel_id=1, source_target_pairs={{0,8},{1,9},{2,10},{3,11},{4,12},{5,13},{6,14},{7,15},{8,0},{9,1},... | collective-permute-start | bytes 98312 | tf_op jit(solution)/shard_map/ppermute | solution.py:229
  94.4 5.4 %collective-permute-start.8 = (f32[64,128]{1,0:T(8,128)S(1)}, f32[64,128]{1,0:T(8,128)S(1)}, u32[]{:S(2)}, u32[]{:S(2)}) collective-permute-start(f32[64,128]{1,0:T(8,128)S(1)} %add.18), channel_id=1, source_target_pairs={{0,16},{1,17},{2,18},{3,19},{4,20},{5,21},{6,22},{7,23},{8,24},{9,... | collective-permute-start | bytes 98312 | tf_op jit(solution)/shard_map/ppermute | solution.py:229
where the time goes:
time: 101 us
  waiting for transfers between devices  51.6 us (51%)
  Pallas kernels  23.5 us (23%)
  starting transfers between devices  23.3 us (23%)
  local copies, waits for them, and re-layouts  1.98 us (2%)
    all_to_all x1, waiting for transfers between devices, per_device(): recv = lax.all_to_all(packed, ('cols', 'sites'), 0, 0, tiled=True)  30.2 us
    ppermute x5, waiting for transfers between devices, per_device(): lax.ppermute(total, 'sites', [(i, i ^ step) for i in range(count)])  18.4 us
    pallas_call x1, Pallas kernels, moments(): pl.pallas_call(moments_kernel, in_specs=[vm] * 5, out_specs=vm, out_shape...  16.6 us
    all_to_all x1, starting transfers between devices, per_device(): recv = lax.all_to_all(packed, ('cols', 'sites'), 0, 0, tiled=True)  14.7 us
    pallas_call x1, Pallas kernels, pack(): pl.pallas_call(pack_kernel, grid=(groups,), in_specs=[pl.BlockSpec((rg, N...  6.92 us
    ppermute x1, starting transfers between devices, per_device(): lax.ppermute(present[:HALO], 'sites', down)  4.48 us
    ppermute x1, waiting for transfers between devices, per_device(): lax.ppermute(present[rows - HALO:], 'sites', up)  2.97 us
  transfers between devices with their start and end apart: 10, of which 7 were waited for; matrix products, arithmetic and copies ran while one was open for 1% of the time, Pallas kernels for 0%

commit v1 on v0

v1 whole, which is shorter than its diff:
```python
import jax
import jax.numpy as jnp
from jax import lax
from jax.experimental import pallas as pl
from jax.experimental.pallas import tpu as pltpu
from jax.sharding import PartitionSpec as P

MOM = 4
HALO = 4
ONSITE_MASS = 0.3
SECOND_HOP = 0.2
BAND_SCALE = 4.5
LANES = 128
SUB = 8
TILES = 4
F32 = jnp.float32


def pack_kernel(in_ref, out_ref):
    lane = lax.broadcasted_iota(jnp.int32, (SUB, LANES), 1)
    source = lane // 32 * 32 + lane % 8 * 4 + lane // 8 % 4
    slabs = out_ref.shape[0]
    for slab in range(slabs):
        parts = [in_ref[q * SUB : (q + 1) * SUB, slab, :] for q in range(4)]
        tile = jnp.concatenate(parts, axis=1)
        out_ref[slab] = jnp.take_along_axis(tile, source, axis=1)


def pack(pieces):
    rg, groups, slabs, width = pieces.shape
    return pl.pallas_call(
        pack_kernel,
        grid=(groups,),
        in_specs=[pl.BlockSpec((rg, None, slabs, width), lambda k: (0, k, 0, 0))],
        out_specs=pl.BlockSpec((slabs, SUB, LANES), lambda k: (k, 0, 0)),
        out_shape=jax.ShapeDtypeStruct((groups * slabs, SUB, LANES), F32),
        name="pack",
    )(pieces)


def regroup(pieces, block_bits):
    tiles = list(pieces)
    for bit, is_set in enumerate(block_bits):
        step = 1 << bit
        for p in range(16):
            if p & step:
                continue
            low, high = tiles[p], tiles[p | step]
            tiles[p] = jnp.where(is_set, pltpu.roll(high, SUB * step, 1), low)
            tiles[p | step] = jnp.where(is_set, high, pltpu.roll(low, LANES - SUB * step, 1))
    return tiles


def moments_kernel(recv_ref, lo_ref, hi_ref, pres_ref, left_ref, out_ref, field, presb):
    rows = left_ref.shape[0]
    lane = lax.broadcasted_iota(jnp.int32, (SUB, LANES), 1)
    block_bits = [(lane // SUB >> bit) % 2 == 1 for bit in range(4)]
    is_first = lane == 0
    is_last = lane == LANES - 1
    T = range(TILES)
    edge = HALO * 16

    def unpack_row(src, src_row, e, mask_rows):
        for t in T:
            presb[e, t] = jnp.broadcast_to(mask_rows[t], (SUB, LANES))
        pieces = [src[src_row * 16 + b] for b in range(16)]
        for v, value in enumerate(regroup(pieces, block_bits)):
            field[0, e, v // 8, v // 4 % 2, v % 4] = value * presb[e, v % 4]

    for i in range(HALO):
        for src, e in ((lo_ref, i), (hi_ref, rows + HALO + i)):
            at = [i * TILES + t for t in T]
            unpack_row(src, i, e, [src[edge + a // SUB, pl.ds(a % SUB, 1), :] for a in at])

    @pl.loop(0, rows)
    def _(i):
        unpack_row(recv_ref, i, i + HALO, [pres_ref[i, pl.ds(t, 1), :] for t in T])

    def ahead(tiles):
        wrapped = jnp.where(is_last, 0.0, pltpu.roll(tiles[0], LANES - 1, 1))
        return tiles[1:] + [wrapped]

    def behind(tiles):
        wrapped = jnp.where(is_first, 0.0, pltpu.roll(tiles[-1], 1, 1))
        return [wrapped] + tiles[:-1]

    def row(level, parity, below, centre, above, mask):
        c, d, nxt, prv, second = [], [], [], [], []
        for r in (0, 1):
            w = centre[r]
            diag = [above[r][t] + below[r][t] for t in T]
            fore, back = ahead(w), behind(w)
            if level == 0:
                a = ahead([2.0 * fore[t] - diag[t] for t in T])
                b = behind([2.0 * back[t] - diag[t] for t in T])
                second.append([a[t] + b[t] for t in T])
            else:
                a = ahead([fore[t] - diag[t] for t in T])
                b = behind([back[t] - diag[t] for t in T])
                second.append([a[t] - b[t] for t in T])
            nxt.append(fore)
            prv.append(back)
        result = []
        for r in (0, 1):
            values = []
            for t in T:
                sign = 1.0 if (parity + t) % 2 == 0 else -1.0
                if level == 0:
                    if r == 0:
                        along = prv[1][t] - nxt[1][t]
                    else:
                        along = nxt[0][t] - prv[0][t]
                    total = along - (SECOND_HOP * sign) * second[r][t]
                else:
                    vertical = above[r][t] if sign > 0 else below[r][t]
                    near = (nxt[r][t] + prv[r][t]) + vertical
                    turn = -sign if r == 0 else sign
                    total = near + (
                        (ONSITE_MASS * sign) * centre[r][t] + (SECOND_HOP * turn) * second[1 - r][t]
                    )
                values.append(total * mask[t])
            result.append(values)
        return result

    def load(level, e, half):
        return [[field[level, e, r, half, t] for t in T] for r in (0, 1)]

    for level in range(MOM):
        reach = HALO - 1 - level
        first = HALO - reach

        @pl.loop(0, (rows + 2 * reach) // 2)
        def _(i, level=level, first=first):
            e = first + 2 * i
            scale = (1.0, 1.0 / BAND_SCALE, 2.0 / BAND_SCALE, 2.0 / BAND_SCALE)[level]
            masks = []
            for k in (0, 1):
                mask = [presb[e + k, t] for t in T]
                masks.append(mask if level == 0 else [scale * m for m in mask])
            for half in (0, 1):
                window = [load(level, e + k, half) for k in (-1, 0, 1, 2)]
                for k in (0, 1):
                    values = row(level, (first + k) % 2, *window[k : k + 3], masks[k])
                    if level > 1:
                        old = load(level - 1, e + k, half)
                        values = [[values[r][t] - old[r][t] for t in T] for r in (0, 1)]
                    for r in (0, 1):
                        for t in T:
                            field[(level + 1) % MOM, e + k, r, half, t] = values[r][t]

    acc = None
    for y in range(rows):
        for t in T:
            rhs = jnp.concatenate(
                [field[(m + 1) % MOM, y + HALO, r, half, t] for r in (0, 1) for m in range(MOM) for half in (0, 1)],
                axis=0,
            ).astype(jnp.bfloat16)
            term = lax.dot_general(
                rhs,
                left_ref[y, :, t * LANES : (t + 1) * LANES],
                (((1,), (1,)), ((), ())),
                preferred_element_type=F32,
            )
            acc = term if acc is None else acc + term
    half_rows = MOM * 2 * SUB
    top, bottom = acc[:half_rows], acc[half_rows:]
    lane_out = lax.broadcasted_iota(jnp.int32, top.shape, 1)
    out_ref[...] = pltpu.roll(bottom, 64, 1) + jnp.where(lane_out < 64, top, -top)


def moments(recv, lo, hi, pres, left):
    rows, n2, width = left.shape
    ext = rows + 2 * HALO
    vm = pl.BlockSpec(memory_space=pltpu.VMEM)
    return pl.pallas_call(
        moments_kernel,
        in_specs=[vm] * 5,
        out_specs=vm,
        out_shape=jax.ShapeDtypeStruct((MOM * 2 * SUB, n2), F32),
        scratch_shapes=[
            pltpu.VMEM((MOM, ext, 2, 2, TILES, SUB, LANES), F32),
            pltpu.VMEM((ext, TILES, SUB, LANES), F32),
        ],
        compiler_params=pltpu.CompilerParams(vmem_limit_bytes=40 * 2**20),
        name="moments",
    )(recv, lo, hi, pres, left)


def per_device(right_vectors, left_vectors, vacancy):
    parts, width_group, groups, slabs, _, piece = right_vectors.shape
    count = lax.axis_size("sites")
    up = [(i, (i + 1) % count) for i in range(count)]
    down = [((i + 1) % count, i) for i in range(count)]
    n_left, rows, width = left_vectors.shape[1:]

    packed = pack(right_vectors.reshape(parts * width_group, groups, slabs, piece))
    packed, left_vectors = lax.optimization_barrier((packed, left_vectors))
    recv = lax.all_to_all(packed, ("cols", "sites"), 0, 0, tiled=True)

    site = lax.broadcasted_iota(jnp.int32, (width, width), 0)
    place = lax.broadcasted_iota(jnp.int32, (width, width), 1)
    to_place = (site % TILES * LANES + site // TILES == place).astype(jnp.bfloat16)
    left = left_vectors.reshape(2 * n_left * rows, width)
    left = jnp.dot(left, to_place, preferred_element_type=jnp.bfloat16)
    left = jnp.swapaxes(left.reshape(2 * n_left, rows, width), 0, 1)
    present = jnp.dot(vacancy.astype(jnp.bfloat16), to_place, preferred_element_type=F32)
    present = present.reshape(rows, TILES, LANES)
    recv, left, present = lax.optimization_barrier((recv, left, present))

    edge = HALO * width // piece
    low_mask = present[:HALO].reshape(-1, SUB, LANES)
    high_mask = present[rows - HALO :].reshape(-1, SUB, LANES)
    lo = lax.ppermute(jnp.concatenate([recv[recv.shape[0] - edge :], high_mask]), "sites", up)
    hi = lax.ppermute(jnp.concatenate([recv[:edge], low_mask]), "sites", down)
    total = moments(recv, lo, hi, present, left)
    step = 1
    while step < count:
        total = total + lax.ppermute(total, "sites", [(i, i ^ step) for i in range(count)])
        step *= 2
    out = total.reshape(MOM, width_group, 2, n_left)
    return jnp.transpose(out, (2, 0, 3, 1))[..., None]


def solution(mesh):
    return jax.shard_map(
        per_device,
        mesh=mesh,
        in_specs=(
            P(None, None, None, None, ("cols", "sites"), None),
            P(None, None, "sites", None),
            P("sites", None),
        ),
        out_specs=P(None, None, None, None, "cols"),
        check_vma=False,
    )
```

time: 101 us -> 97.4 us (0.964)
  matrix products: 0 us -> 5.05 us
  Pallas kernels: 23.5 us -> 19.4 us
  starting transfers between devices: 23.3 us -> 20.6 us
  local copies, waits for them, and re-layouts: 1.98 us -> 0.79 us
    all_to_all x1, waiting for transfers between devices: 30.2 us -> 25.1 us  [per_device(): recv = lax.all_to_all(packed, ('cols', 'sites'), 0, 0, tiled=True)]
    dot_general x0 -> x2, matrix products: none -> 5.05 us  [the longest x1 4.46 us: per_device(): left = jnp.dot(left, to_place, preferred_element_type=jnp.bfloat16)]
    pallas_call x1, Pallas kernels: 16.6 us -> 12.1 us  [moments(): pl.pallas_call(moments_kernel, in_specs=[vm] * 5, out_specs=vm, out_shape...]
    ppermute x4 -> x2, waiting for transfers between devices: 2.98 us -> 6.74 us  [the longest x1 6.74 us: per_device(): lax.ppermute(jnp.concatenate([recv[recv.shape[0] - edge:], high_mask]), '...]
    ppermute x4 -> x2, starting transfers between devices: 7.7 us -> 5.81 us  [the longest x1 4.32 us: per_device(): hi = lax.ppermute(jnp.concatenate([recv[:edge], low_mask]), 'sites', down)]
    unnamed x5 -> x2, local copies, waits for them, and re-layouts: 1.17 us -> 0.01 us
  transfers between devices with their start and end apart: 10 -> 8, of which waited for: 7 -> 7; matrix products, arithmetic and copies ran while one was open for 1% -> 5% of each run, Pallas kernels for 0% -> 0%
where the time goes in v1:
time: 97.4 us; the launch traced here: 97.1 us
  waiting for transfers between devices  51 us (52%)
  starting transfers between devices  20.6 us (21%)
  Pallas kernels  19.4 us (20%)
  matrix products  5.05 us (5%)
    all_to_all x1, waiting for transfers between devices, per_device(): recv = lax.all_to_all(packed, ('cols', 'sites'), 0, 0, tiled=True)  25.1 us
    ppermute x5, waiting for transfers between devices, per_device(): lax.ppermute(total, 'sites', [(i, i ^ step) for i in range(count)])  19.2 us
    all_to_all x1, starting transfers between devices, per_device(): recv = lax.all_to_all(packed, ('cols', 'sites'), 0, 0, tiled=True)  14.7 us
    pallas_call x1, Pallas kernels, moments(): pl.pallas_call(moments_kernel, in_specs=[vm] * 5, out_specs=vm, out_shape...  12.1 us
    pallas_call x1, Pallas kernels, pack(): pl.pallas_call(pack_kernel, grid=(groups,), in_specs=[pl.BlockSpec((rg, N...  7.29 us
    ppermute x1, waiting for transfers between devices, per_device(): lax.ppermute(jnp.concatenate([recv[recv.shape[0] - edge:], high_mask]), '...  6.74 us
    dot_general x1, matrix products, per_device(): left = jnp.dot(left, to_place, preferred_element_type=jnp.bfloat16)  4.46 us
    ppermute x1, starting transfers between devices, per_device(): hi = lax.ppermute(jnp.concatenate([recv[:edge], low_mask]), 'sites', down)  4.32 us
  transfers between devices with their start and end apart: 8, of which 7 were waited for; matrix products, arithmetic and copies ran while one was open for 5% of the time, Pallas kernels for 0%

profile of v1, /device:TPU:2, one launch (start us, length us, event | category | flops | bytes accessed | tf_op | source)
XLA Modules:
  0.0 97.1 jit_solution(12543892687673742700)
XLA Ops:
  0.0 7.3 %pack.1 = f32[256,8,128]{2,1,0:T(8,128)} custom-call(f32[32,8,32,32]{3,2,1,0:T(8,128)} %bitcast.14), custom_call_target="tpu_custom_call" | custom-call | tf_op jit(solution)/shard_map/pack/pallas_call | solution.py:31
  7.3 0.0 copy-start
  7.3 14.7 %all-to-all-start = ((f32[256,8,128]{2,1,0:T(8,128)}), f32[256,8,128]{2,1,0:T(8,128)S(1)}, u32[]{:S(2)}, u32[]{:S(2)}) async-start(f32[256,8,128]{2,1,0:T(8,128)} %pack.1), calls=%async_computation | async-start | bytes 2097152 | tf_op jit(solution)/shard_map/all_to_all | solution.py:198
  22.0 0.0 copy-done
  22.0 0.6 convolution_bitcast_fusion
  22.6 4.5 %fusion.2.left_ref = bf16[16,128,512]{2,1,0:T(8,128)(2,1)S(1)} fusion(bf16[128,16,512]{2,1,0:T(8,128)(2,1)} %bitcast.17, s32[512]{0:T(512)S(1)} %get-tuple-element.19, s32[512]{0:T(512)S(1)} %get-tuple-element.22, s32[512]{0:T(512)S(1)} %get-tuple-element.20, s32[512]{0:T(512)S(1)} %get-tuple-element.21, pred[512]{0:T(512)(128)(4,1)S(1)} %get-tuple-element.23, ...), kind=kOutput, calls=%fused_computation.2 | convolution fusion | flops 1075052544 | bytes 4203520 | tf_op jit(solution)/shard_map/dot_general | solution.py:204
  27.1 25.1 %all-to-all-done.recv_ref = f32[256,8,128]{2,1,0:T(8,128)S(1)} async-done(((f32[256,8,128]{2,1,0:T(8,128)}), f32[256,8,128]{2,1,0:T(8,128)S(1)}, u32[]{:S(2)}, u32[]{:S(2)}) %all-to-all-start) | async-done | bytes 1048608 | tf_op jit(solution)/shard_map/all_to_all | solution.py:198
  52.3 1.5 %collective-permute-start = (f32[66,8,128]{2,1,0:T(8,128)S(1)}, f32[66,8,128]{2,1,0:T(8,128)S(1)}, u32[]{:S(2)}, u32[]{:S(2)}) collective-permute-start(f32[66,8,128]{2,1,0:T(8,128)S(1)} %pad_maximum_fusion), channel_id=1, source_target_pairs={{0,1},{1,2},{2,3},{3,4},{4,5},{5,6},{6,7},{7,8},{8,9},{9,10},{10,1... | collective-permute-start | bytes 811016 | tf_op jit(solution)/shard_map/ppermute | solution.py:213
  53.8 4.3 %collective-permute-start.1 = (f32[66,8,128]{2,1,0:T(8,128)S(1)}, f32[66,8,128]{2,1,0:T(8,128)S(1)}, u32[]{:S(2)}, u32[]{:S(2)}) collective-permute-start(f32[66,8,128]{2,1,0:T(8,128)S(1)} %pad_maximum_fusion.1), channel_id=1, source_target_pairs={{1,0},{2,1},{3,2},{4,3},{5,4},{6,5},{7,6},{8,7},{9,8},{10,9},{11,1... | collective-permute-start | bytes 811016 | tf_op jit(solution)/shard_map/ppermute | solution.py:214
  58.1 6.7 %collective-permute-done.lo_ref = f32[66,8,128]{2,1,0:T(8,128)S(1)} collective-permute-done((f32[66,8,128]{2,1,0:T(8,128)S(1)}, f32[66,8,128]{2,1,0:T(8,128)S(1)}, u32[]{:S(2)}, u32[]{:S(2)}) %collective-permute-start) | collective-permute-done | bytes 270368 | tf_op jit(solution)/shard_map/ppermute | solution.py:213
  64.8 0.0 collective-permute-done.1.hi_ref
  64.8 12.1 %moments.1 = f32[64,128]{1,0:T(8,128)S(1)} custom-call(f32[256,8,128]{2,1,0:T(8,128)S(1)} %all-to-all-done.recv_ref, f32[66,8,128]{2,1,0:T(8,128)S(1)} %collective-permute-done.lo_ref, f32[66,8,128]{2,1,0:T(8,128)S(1)} %collective-permute-done.1.hi_ref, f32[16,4,128]{2,1,0:T(4,128)S(1)} %reshape.20.pres_ref, bf16[16,128,512]{2,1,0:T(8,128)(2,1)S(1)} %fusion.2.left_ref), custom_call_target="tpu_custom_call" | custom-call | tf_op jit(solution)/shard_map/moments/pallas_call | solution.py:175
  76.9 0.1 collective-permute-start.2
  77.0 1.2 %collective-permute-done.2 = f32[64,128]{1,0:T(8,128)S(1)} collective-permute-done((f32[64,128]{1,0:T(8,128)S(1)}, f32[64,128]{1,0:T(8,128)S(1)}, u32[]{:S(2)}, u32[]{:S(2)}) %collective-permute-start.2) | collective-permute-done | bytes 32800 | tf_op jit(solution)/shard_map/ppermute | solution.py:218
  78.2 0.0 collective-permute-start.3
  78.2 3.9 %collective-permute-done.3 = f32[64,128]{1,0:T(8,128)S(1)} collective-permute-done((f32[64,128]{1,0:T(8,128)S(1)}, f32[64,128]{1,0:T(8,128)S(1)}, u32[]{:S(2)}, u32[]{:S(2)}) %collective-permute-start.3) | collective-permute-done | bytes 32800 | tf_op jit(solution)/shard_map/ppermute | solution.py:218
  82.2 0.0 collective-permute-start.4
  82.2 4.8 %collective-permute-done.4 = f32[64,128]{1,0:T(8,128)S(1)} collective-permute-done((f32[64,128]{1,0:T(8,128)S(1)}, f32[64,128]{1,0:T(8,128)S(1)}, u32[]{:S(2)}, u32[]{:S(2)}) %collective-permute-start.4) | collective-permute-done | bytes 32800 | tf_op jit(solution)/shard_map/ppermute | solution.py:218
  87.0 0.0 collective-permute-start.5
  87.0 3.9 %collective-permute-done.5 = f32[64,128]{1,0:T(8,128)S(1)} collective-permute-done((f32[64,128]{1,0:T(8,128)S(1)}, f32[64,128]{1,0:T(8,128)S(1)}, u32[]{:S(2)}, u32[]{:S(2)}) %collective-permute-start.5) | collective-permute-done | bytes 32800 | tf_op jit(solution)/shard_map/ppermute | solution.py:218
  90.9 0.0 collective-permute-start.6
  90.9 5.4 %collective-permute-done.6 = f32[64,128]{1,0:T(8,128)S(1)} collective-permute-done((f32[64,128]{1,0:T(8,128)S(1)}, f32[64,128]{1,0:T(8,128)S(1)}, u32[]{:S(2)}, u32[]{:S(2)}) %collective-permute-start.6) | collective-permute-done | bytes 32800 | tf_op jit(solution)/shard_map/ppermute | solution.py:218
  96.3 0.1 reshape.23
  96.4 0.6 copy.5
  (13 shorter events, 0.1 us)
Async XLA Ops:
  7.3 14.7 %copy-start = (s32[16,512]{1,0:T(8,128)S(1)}, s32[16,512]{1,0:T(8,128)}, u32[]{:S(2)}) copy-start(s32[16,512]{1,0:T(8,128)} %param.5) | copy-start | bytes 98308
  7.3 44.9 %all-to-all-start = ((f32[256,8,128]{2,1,0:T(8,128)}), f32[256,8,128]{2,1,0:T(8,128)S(1)}, u32[]{:S(2)}, u32[]{:S(2)}) async-start(f32[256,8,128]{2,1,0:T(8,128)} %pack.1), calls=%async_computation | async-start | bytes 2097152 | tf_op jit(solution)/shard_map/all_to_all | solution.py:198
  52.3 12.6 %collective-permute-start = (f32[66,8,128]{2,1,0:T(8,128)S(1)}, f32[66,8,128]{2,1,0:T(8,128)S(1)}, u32[]{:S(2)}, u32[]{:S(2)}) collective-permute-start(f32[66,8,128]{2,1,0:T(8,128)S(1)} %pad_maximum_fusion), channel_id=1, source_target_pairs={{0,1},{1,2},{2,3},{3,4},{4,5},{5,6},{6,7},{7,8},{8,9},{9,10},{10,1... | collective-permute-start | bytes 811016 | tf_op jit(solution)/shard_map/ppermute | solution.py:213
  53.8 11.1 %collective-permute-start.1 = (f32[66,8,128]{2,1,0:T(8,128)S(1)}, f32[66,8,128]{2,1,0:T(8,128)S(1)}, u32[]{:S(2)}, u32[]{:S(2)}) collective-permute-start(f32[66,8,128]{2,1,0:T(8,128)S(1)} %pad_maximum_fusion.1), channel_id=1, source_target_pairs={{1,0},{2,1},{3,2},{4,3},{5,4},{6,5},{7,6},{8,7},{9,8},{10,9},{11,1... | collective-permute-start | bytes 811016 | tf_op jit(solution)/shard_map/ppermute | solution.py:214
  76.9 1.3 %collective-permute-start.2 = (f32[64,128]{1,0:T(8,128)S(1)}, f32[64,128]{1,0:T(8,128)S(1)}, u32[]{:S(2)}, u32[]{:S(2)}) collective-permute-start(f32[64,128]{1,0:T(8,128)S(1)} %moments.1), channel_id=1, source_target_pairs={{0,1},{1,0},{2,3},{3,2},{4,5},{5,4},{6,7},{7,6},{8,9},{9,8},{10,11... | collective-permute-start | bytes 98312 | tf_op jit(solution)/shard_map/ppermute | solution.py:218
  78.2 3.9 %collective-permute-start.3 = (f32[64,128]{1,0:T(8,128)S(1)}, f32[64,128]{1,0:T(8,128)S(1)}, u32[]{:S(2)}, u32[]{:S(2)}) collective-permute-start(f32[64,128]{1,0:T(8,128)S(1)} %add.33), channel_id=1, source_target_pairs={{0,2},{1,3},{2,0},{3,1},{4,6},{5,7},{6,4},{7,5},{8,10},{9,11},{10,... | collective-permute-start | bytes 98312 | tf_op jit(solution)/shard_map/ppermute | solution.py:218
  82.2 4.8 %collective-permute-start.4 = (f32[64,128]{1,0:T(8,128)S(1)}, f32[64,128]{1,0:T(8,128)S(1)}, u32[]{:S(2)}, u32[]{:S(2)}) collective-permute-start(f32[64,128]{1,0:T(8,128)S(1)} %add.34), channel_id=1, source_target_pairs={{0,4},{1,5},{2,6},{3,7},{4,0},{5,1},{6,2},{7,3},{8,12},{9,13},{10,... | collective-permute-start | bytes 98312 | tf_op jit(solution)/shard_map/ppermute | solution.py:218
  87.0 3.9 %collective-permute-start.5 = (f32[64,128]{1,0:T(8,128)S(1)}, f32[64,128]{1,0:T(8,128)S(1)}, u32[]{:S(2)}, u32[]{:S(2)}) collective-permute-start(f32[64,128]{1,0:T(8,128)S(1)} %add.35), channel_id=1, source_target_pairs={{0,8},{1,9},{2,10},{3,11},{4,12},{5,13},{6,14},{7,15},{8,0},{9,1},... | collective-permute-start | bytes 98312 | tf_op jit(solution)/shard_map/ppermute | solution.py:218
  90.9 5.4 %collective-permute-start.6 = (f32[64,128]{1,0:T(8,128)S(1)}, f32[64,128]{1,0:T(8,128)S(1)}, u32[]{:S(2)}, u32[]{:S(2)}) collective-permute-start(f32[64,128]{1,0:T(8,128)S(1)} %add.36), channel_id=1, source_target_pairs={{0,16},{1,17},{2,18},{3,19},{4,20},{5,21},{6,22},{7,23},{8,24},{9,... | collective-permute-start | bytes 98312 | tf_op jit(solution)/shard_map/ppermute | solution.py:218

commit v2 on v1

--- a/solution.py
+++ b/solution.py
@@ -12,49 +12,56 @@
 BAND_SCALE = 4.5
 LANES = 128
 SUB = 8
+GROUPSTEP = 2
 TILES = 4
 F32 = jnp.float32
 
 
-def pack_kernel(in_ref, out_ref):
+def pack_kernel(in_ref, out_ref, turned):
+    columns, groups, slabs, width = in_ref.shape
+    block = lax.broadcasted_iota(jnp.int32, (SUB, LANES), 1) // width
+    odd, high = block % 2 == 1, block >= 2
     lane = lax.broadcasted_iota(jnp.int32, (SUB, LANES), 1)
-    source = lane // 32 * 32 + lane % 8 * 4 + lane // 8 % 4
-    slabs = out_ref.shape[0]
-    for slab in range(slabs):
-        parts = [in_ref[q * SUB : (q + 1) * SUB, slab, :] for q in range(4)]
-        tile = jnp.concatenate(parts, axis=1)
-        out_ref[slab] = jnp.take_along_axis(tile, source, axis=1)
+    swapped = jnp.where(odd, lane - width, lane + width)
+    spots = [(k, base) for k in range(groups) for base in range(0, slabs, 4)]
+    for slot, (k, base) in enumerate(spots):
+        if base % 8 == 0:
+            octets = [jnp.swapaxes(in_ref[c : c + SUB, k, base : base + SUB, :], 0, 1) for c in range(0, columns, SUB)]
+        rows = [octets[c][base % 8 + s] for s in range(4) for c in range(columns // SUB)]
+        turned[slot] = jnp.concatenate(rows, axis=0).T
+    for slot, (k, base) in enumerate(spots):
+        v = [turned[slot, pl.ds(t, SUB, stride=TILES), :] for t in range(TILES)]
+        for p in (0, 2):
+            low, upper = v[p], v[p + 1]
+            moved = jnp.take_along_axis(jnp.where(odd, low, upper), swapped, axis=1)
+            v[p], v[p + 1] = jnp.where(odd, moved, low), jnp.where(odd, upper, moved)
+        for p in (0, 1):
+            low, upper = v[p], v[p + 2]
+            moved = pltpu.roll(jnp.where(high, low, upper), LANES // 2, 1)
+            v[p], v[p + 2] = jnp.where(high, moved, low), jnp.where(high, upper, moved)
+        for s in range(4):
+            out_ref[k, base + s] = v[s]
 
 
 def pack(pieces):
-    rg, groups, slabs, width = pieces.shape
-    return pl.pallas_call(
+    columns, groups, slabs, width = pieces.shape
+    step = GROUPSTEP
+    out = pl.pallas_call(
         pack_kernel,
-        grid=(groups,),
-        in_specs=[pl.BlockSpec((rg, None, slabs, width), lambda k: (0, k, 0, 0))],
-        out_specs=pl.BlockSpec((slabs, SUB, LANES), lambda k: (k, 0, 0)),
-        out_shape=jax.ShapeDtypeStruct((groups * slabs, SUB, LANES), F32),
+        grid=(groups // step,),
+        in_specs=[pl.BlockSpec((columns, step, slabs, width), lambda k: (0, k, 0, 0))],
+        out_specs=pl.BlockSpec((step, slabs, SUB, LANES), lambda k: (k, 0, 0, 0)),
+        out_shape=jax.ShapeDtypeStruct((groups, slabs, SUB, LANES), F32),
+        scratch_shapes=[pltpu.VMEM((step * slabs // 4, width, LANES), F32)],
+        compiler_params=pltpu.CompilerParams(vmem_limit_bytes=40 * 2**20),
         name="pack",
     )(pieces)
-
-
-def regroup(pieces, block_bits):
-    tiles = list(pieces)
-    for bit, is_set in enumerate(block_bits):
-        step = 1 << bit
-        for p in range(16):
-            if p & step:
-                continue
-            low, high = tiles[p], tiles[p | step]
-            tiles[p] = jnp.where(is_set, pltpu.roll(high, SUB * step, 1), low)
-            tiles[p | step] = jnp.where(is_set, high, pltpu.roll(low, LANES - SUB * step, 1))
-    return tiles
+    return out.reshape(groups * slabs, SUB, LANES)
 
 
 def moments_kernel(recv_ref, lo_ref, hi_ref, pres_ref, left_ref, out_ref, field, presb):
     rows = left_ref.shape[0]
     lane = lax.broadcasted_iota(jnp.int32, (SUB, LANES), 1)
-    block_bits = [(lane // SUB >> bit) % 2 == 1 for bit in range(4)]
     is_first = lane == 0
     is_last = lane == LANES - 1
     T = range(TILES)
@@ -63,18 +70,22 @@
     def unpack_row(src, src_row, e, mask_rows):
         for t in T:
             presb[e, t] = jnp.broadcast_to(mask_rows[t], (SUB, LANES))
-        pieces = [src[src_row * 16 + b] for b in range(16)]
-        for v, value in enumerate(regroup(pieces, block_bits)):
-            field[0, e, v // 8, v // 4 % 2, v % 4] = value * presb[e, v % 4]
+        turned = src[pl.ds(src_row * 16, 16)].reshape(LANES, LANES).T
+        for t in T:
+            for q in range(4):
+                at = (4 * t + q) * SUB
+                field[0, e, q // 2, q % 2, t] = turned[at : at + SUB] * presb[e, t]
 
     for i in range(HALO):
         for src, e in ((lo_ref, i), (hi_ref, rows + HALO + i)):
             at = [i * TILES + t for t in T]
             unpack_row(src, i, e, [src[edge + a // SUB, pl.ds(a % SUB, 1), :] for a in at])
 
-    @pl.loop(0, rows)
+    @pl.loop(0, rows // 4)
     def _(i):
-        unpack_row(recv_ref, i, i + HALO, [pres_ref[i, pl.ds(t, 1), :] for t in T])
+        for k in range(4):
+            y = 4 * i + k
+            unpack_row(recv_ref, y, y + HALO, [pres_ref[y, pl.ds(t, 1), :] for t in T])
 
     def ahead(tiles):
         wrapped = jnp.where(is_last, 0.0, pltpu.roll(tiles[0], LANES - 1, 1))

time: 97.4 us -> 91.1 us (0.935)
  Pallas kernels: 19.4 us -> 11 us
  local copies, waits for them, and re-layouts: 0.79 us -> 2.98 us
    pallas_call x1, Pallas kernels: 12.1 us -> 6.69 us  [moments(): pl.pallas_call(moments_kernel, in_specs=[vm] * 5, out_specs=vm, out_shape...]
    pallas_call x1, Pallas kernels: 7.29 us -> 4.34 us  [pack(): pl.pallas_call(pack_kernel, grid=(groups // step,), in_specs=[pl.BlockSpe...]
    unnamed x2 -> x4, local copies, waits for them, and re-layouts: 0.01 us -> 2.19 us
  transfers between devices with their start and end apart: 8 -> 8, of which waited for: 7 -> 7; matrix products, arithmetic and copies ran while one was open for 5% -> 6% of each run, Pallas kernels for 0% -> 0%
where the time goes in v2:
time: 91.1 us; the launch traced here: 90.9 us
  waiting for transfers between devices  51 us (56%)
  starting transfers between devices  20.6 us (23%)
  Pallas kernels  11 us (12%)
  matrix products  5.05 us (6%)
  local copies, waits for them, and re-layouts  2.98 us (3%)
    all_to_all x1, waiting for transfers between devices, per_device(): recv = lax.all_to_all(packed, ('cols', 'sites'), 0, 0, tiled=True)  25.1 us
    ppermute x5, waiting for transfers between devices, per_device(): lax.ppermute(total, 'sites', [(i, i ^ step) for i in range(count)])  19.2 us
    all_to_all x1, starting transfers between devices, per_device(): recv = lax.all_to_all(packed, ('cols', 'sites'), 0, 0, tiled=True)  14.7 us
    ppermute x1, waiting for transfers between devices, per_device(): lax.ppermute(jnp.concatenate([recv[recv.shape[0] - edge:], high_mask]), '...  6.74 us
    pallas_call x1, Pallas kernels, moments(): pl.pallas_call(moments_kernel, in_specs=[vm] * 5, out_specs=vm, out_shape...  6.69 us
    dot_general x1, matrix products, per_device(): left = jnp.dot(left, to_place, preferred_element_type=jnp.bfloat16)  4.46 us
    pallas_call x1, Pallas kernels, pack(): pl.pallas_call(pack_kernel, grid=(groups // step,), in_specs=[pl.BlockSpe...  4.34 us
    ppermute x1, starting transfers between devices, per_device(): hi = lax.ppermute(jnp.concatenate([recv[:edge], low_mask]), 'sites', down)  4.32 us
  transfers between devices with their start and end apart: 8, of which 7 were waited for; matrix products, arithmetic and copies ran while one was open for 6% of the time, Pallas kernels for 0%

profile of v2, /device:TPU:2, one launch (start us, length us, event | category | flops | bytes accessed | tf_op | source)
XLA Modules:
  0.0 90.9 jit_solution(2588238153319820282)
XLA Ops:
  0.0 2.2 %copy-done = f32[2,16,8,32,1,32]{5,4,3,2,1,0:T(1,128)S(1)} copy-done((f32[2,16,8,32,1,32]{5,4,3,2,1,0:T(1,128)S(1)}, f32[2,16,8,32,1,32]{5,4,3,2,1,0:T(1,128)}, u32[]{:S(2)}) %copy-start) | copy-done | bytes 1048600
  2.2 4.3 %pack.1 = f32[8,32,8,128]{3,2,1,0:T(8,128)} custom-call(f32[32,8,32,32]{3,2,1,0:T(8,128)S(1)} %bitcast.15), custom_call_target="tpu_custom_call" | custom-call | tf_op jit(solution)/shard_map/pack/pallas_call | solution.py:49
  6.5 14.7 %all-to-all-start = ((f32[256,8,128]{2,1,0:T(8,128)}), f32[256,8,128]{2,1,0:T(8,128)S(1)}, u32[]{:S(2)}, u32[]{:S(2)}) async-start(f32[256,8,128]{2,1,0:T(8,128)} %bitcast.1), calls=%async_computation | async-start | bytes 2097152 | tf_op jit(solution)/shard_map/all_to_all | solution.py:209
  21.3 0.0 copy-done.1
  21.3 0.6 convolution_bitcast_fusion
  21.9 4.5 %fusion.2.left_ref = bf16[16,128,512]{2,1,0:T(8,128)(2,1)S(1)} fusion(bf16[128,16,512]{2,1,0:T(8,128)(2,1)} %bitcast.18, s32[512]{0:T(512)S(1)} %get-tuple-element.19, s32[512]{0:T(512)S(1)} %get-tuple-element.22, s32[512]{0:T(512)S(1)} %get-tuple-element.20, s32[512]{0:T(512)S(1)} %get-tuple-element.21, pred[512]{0:T(512)(128)(4,1)S(1)} %get-tuple-element.23, ...), kind=kOutput, calls=%fused_computation.2 | convolution fusion | flops 1075052544 | bytes 4203520 | tf_op jit(solution)/shard_map/dot_general | solution.py:215
  26.4 25.1 %all-to-all-done.recv_ref = f32[256,8,128]{2,1,0:T(8,128)S(1)} async-done(((f32[256,8,128]{2,1,0:T(8,128)}), f32[256,8,128]{2,1,0:T(8,128)S(1)}, u32[]{:S(2)}, u32[]{:S(2)}) %all-to-all-start) | async-done | bytes 1048608 | tf_op jit(solution)/shard_map/all_to_all | solution.py:209
  51.5 1.5 %collective-permute-start = (f32[66,8,128]{2,1,0:T(8,128)S(1)}, f32[66,8,128]{2,1,0:T(8,128)S(1)}, u32[]{:S(2)}, u32[]{:S(2)}) collective-permute-start(f32[66,8,128]{2,1,0:T(8,128)S(1)} %pad_maximum_fusion), channel_id=1, source_target_pairs={{0,1},{1,2},{2,3},{3,4},{4,5},{5,6},{6,7},{7,8},{8,9},{9,10},{10,1... | collective-permute-start | bytes 811016 | tf_op jit(solution)/shard_map/ppermute | solution.py:224
  53.0 4.3 %collective-permute-start.1 = (f32[66,8,128]{2,1,0:T(8,128)S(1)}, f32[66,8,128]{2,1,0:T(8,128)S(1)}, u32[]{:S(2)}, u32[]{:S(2)}) collective-permute-start(f32[66,8,128]{2,1,0:T(8,128)S(1)} %pad_maximum_fusion.1), channel_id=1, source_target_pairs={{1,0},{2,1},{3,2},{4,3},{5,4},{6,5},{7,6},{8,7},{9,8},{10,9},{11,1... | collective-permute-start | bytes 811016 | tf_op jit(solution)/shard_map/ppermute | solution.py:225
  57.3 6.7 %collective-permute-done.lo_ref = f32[66,8,128]{2,1,0:T(8,128)S(1)} collective-permute-done((f32[66,8,128]{2,1,0:T(8,128)S(1)}, f32[66,8,128]{2,1,0:T(8,128)S(1)}, u32[]{:S(2)}, u32[]{:S(2)}) %collective-permute-start) | collective-permute-done | bytes 270368 | tf_op jit(solution)/shard_map/ppermute | solution.py:224
  64.1 0.0 collective-permute-done.1.hi_ref
  64.1 6.7 %moments.1 = f32[64,128]{1,0:T(8,128)S(1)} custom-call(f32[256,8,128]{2,1,0:T(8,128)S(1)} %all-to-all-done.recv_ref, f32[66,8,128]{2,1,0:T(8,128)S(1)} %collective-permute-done.lo_ref, f32[66,8,128]{2,1,0:T(8,128)S(1)} %collective-permute-done.1.hi_ref, f32[16,4,128]{2,1,0:T(4,128)S(1)} %reshape.24.pres_ref, bf16[16,128,512]{2,1,0:T(8,128)(2,1)S(1)} %fusion.2.left_ref), custom_call_target="tpu_custom_call" | custom-call | tf_op jit(solution)/shard_map/moments/pallas_call | solution.py:186
  70.8 0.1 collective-permute-start.2
  70.9 1.2 %collective-permute-done.2 = f32[64,128]{1,0:T(8,128)S(1)} collective-permute-done((f32[64,128]{1,0:T(8,128)S(1)}, f32[64,128]{1,0:T(8,128)S(1)}, u32[]{:S(2)}, u32[]{:S(2)}) %collective-permute-start.2) | collective-permute-done | bytes 32800 | tf_op jit(solution)/shard_map/ppermute | solution.py:229
  72.1 0.0 collective-permute-start.3
  72.1 3.9 %collective-permute-done.3 = f32[64,128]{1,0:T(8,128)S(1)} collective-permute-done((f32[64,128]{1,0:T(8,128)S(1)}, f32[64,128]{1,0:T(8,128)S(1)}, u32[]{:S(2)}, u32[]{:S(2)}) %collective-permute-start.3) | collective-permute-done | bytes 32800 | tf_op jit(solution)/shard_map/ppermute | solution.py:229
  76.0 0.0 collective-permute-start.4
  76.0 4.8 %collective-permute-done.4 = f32[64,128]{1,0:T(8,128)S(1)} collective-permute-done((f32[64,128]{1,0:T(8,128)S(1)}, f32[64,128]{1,0:T(8,128)S(1)}, u32[]{:S(2)}, u32[]{:S(2)}) %collective-permute-start.4) | collective-permute-done | bytes 32800 | tf_op jit(solution)/shard_map/ppermute | solution.py:229
  80.8 0.0 collective-permute-start.5
  80.8 3.9 %collective-permute-done.5 = f32[64,128]{1,0:T(8,128)S(1)} collective-permute-done((f32[64,128]{1,0:T(8,128)S(1)}, f32[64,128]{1,0:T(8,128)S(1)}, u32[]{:S(2)}, u32[]{:S(2)}) %collective-permute-start.5) | collective-permute-done | bytes 32800 | tf_op jit(solution)/shard_map/ppermute | solution.py:229
  84.7 0.0 collective-permute-start.6
  84.7 5.4 %collective-permute-done.6 = f32[64,128]{1,0:T(8,128)S(1)} collective-permute-done((f32[64,128]{1,0:T(8,128)S(1)}, f32[64,128]{1,0:T(8,128)S(1)}, u32[]{:S(2)}, u32[]{:S(2)}) %collective-permute-start.6) | collective-permute-done | bytes 32800 | tf_op jit(solution)/shard_map/ppermute | solution.py:229
  90.1 0.1 reshape.27
  90.2 0.6 copy.5
  (15 shorter events, 0.1 us)
Async XLA Ops:
  0.0 2.2 %copy-start = (f32[2,16,8,32,1,32]{5,4,3,2,1,0:T(1,128)S(1)}, f32[2,16,8,32,1,32]{5,4,3,2,1,0:T(1,128)}, u32[]{:S(2)}) copy-start(f32[2,16,8,32,1,32]{5,4,3,2,1,0:T(1,128)} %param.3) | copy-start | bytes 3145732
  6.5 14.7 %copy-start.1 = (s32[16,512]{1,0:T(8,128)S(1)}, s32[16,512]{1,0:T(8,128)}, u32[]{:S(2)}) copy-start(s32[16,512]{1,0:T(8,128)} %param.5) | copy-start | bytes 98308
  6.5 44.9 %all-to-all-start = ((f32[256,8,128]{2,1,0:T(8,128)}), f32[256,8,128]{2,1,0:T(8,128)S(1)}, u32[]{:S(2)}, u32[]{:S(2)}) async-start(f32[256,8,128]{2,1,0:T(8,128)} %bitcast.1), calls=%async_computation | async-start | bytes 2097152 | tf_op jit(solution)/shard_map/all_to_all | solution.py:209
  51.5 12.6 %collective-permute-start = (f32[66,8,128]{2,1,0:T(8,128)S(1)}, f32[66,8,128]{2,1,0:T(8,128)S(1)}, u32[]{:S(2)}, u32[]{:S(2)}) collective-permute-start(f32[66,8,128]{2,1,0:T(8,128)S(1)} %pad_maximum_fusion), channel_id=1, source_target_pairs={{0,1},{1,2},{2,3},{3,4},{4,5},{5,6},{6,7},{7,8},{8,9},{9,10},{10,1... | collective-permute-start | bytes 811016 | tf_op jit(solution)/shard_map/ppermute | solution.py:224
  53.0 11.1 %collective-permute-start.1 = (f32[66,8,128]{2,1,0:T(8,128)S(1)}, f32[66,8,128]{2,1,0:T(8,128)S(1)}, u32[]{:S(2)}, u32[]{:S(2)}) collective-permute-start(f32[66,8,128]{2,1,0:T(8,128)S(1)} %pad_maximum_fusion.1), channel_id=1, source_target_pairs={{1,0},{2,1},{3,2},{4,3},{5,4},{6,5},{7,6},{8,7},{9,8},{10,9},{11,1... | collective-permute-start | bytes 811016 | tf_op jit(solution)/shard_map/ppermute | solution.py:225
  70.8 1.3 %collective-permute-start.2 = (f32[64,128]{1,0:T(8,128)S(1)}, f32[64,128]{1,0:T(8,128)S(1)}, u32[]{:S(2)}, u32[]{:S(2)}) collective-permute-start(f32[64,128]{1,0:T(8,128)S(1)} %moments.1), channel_id=1, source_target_pairs={{0,1},{1,0},{2,3},{3,2},{4,5},{5,4},{6,7},{7,6},{8,9},{9,8},{10,11... | collective-permute-start | bytes 98312 | tf_op jit(solution)/shard_map/ppermute | solution.py:229
  72.1 3.9 %collective-permute-start.3 = (f32[64,128]{1,0:T(8,128)S(1)}, f32[64,128]{1,0:T(8,128)S(1)}, u32[]{:S(2)}, u32[]{:S(2)}) collective-permute-start(f32[64,128]{1,0:T(8,128)S(1)} %add.33), channel_id=1, source_target_pairs={{0,2},{1,3},{2,0},{3,1},{4,6},{5,7},{6,4},{7,5},{8,10},{9,11},{10,... | collective-permute-start | bytes 98312 | tf_op jit(solution)/shard_map/ppermute | solution.py:229
  76.0 4.8 %collective-permute-start.4 = (f32[64,128]{1,0:T(8,128)S(1)}, f32[64,128]{1,0:T(8,128)S(1)}, u32[]{:S(2)}, u32[]{:S(2)}) collective-permute-start(f32[64,128]{1,0:T(8,128)S(1)} %add.34), channel_id=1, source_target_pairs={{0,4},{1,5},{2,6},{3,7},{4,0},{5,1},{6,2},{7,3},{8,12},{9,13},{10,... | collective-permute-start | bytes 98312 | tf_op jit(solution)/shard_map/ppermute | solution.py:229
  80.8 3.9 %collective-permute-start.5 = (f32[64,128]{1,0:T(8,128)S(1)}, f32[64,128]{1,0:T(8,128)S(1)}, u32[]{:S(2)}, u32[]{:S(2)}) collective-permute-start(f32[64,128]{1,0:T(8,128)S(1)} %add.35), channel_id=1, source_target_pairs={{0,8},{1,9},{2,10},{3,11},{4,12},{5,13},{6,14},{7,15},{8,0},{9,1},... | collective-permute-start | bytes 98312 | tf_op jit(solution)/shard_map/ppermute | solution.py:229
  84.7 5.4 %collective-permute-start.6 = (f32[64,128]{1,0:T(8,128)S(1)}, f32[64,128]{1,0:T(8,128)S(1)}, u32[]{:S(2)}, u32[]{:S(2)}) collective-permute-start(f32[64,128]{1,0:T(8,128)S(1)} %add.36), channel_id=1, source_target_pairs={{0,16},{1,17},{2,18},{3,19},{4,20},{5,21},{6,22},{7,23},{8,24},{9,... | collective-permute-start | bytes 98312 | tf_op jit(solution)/shard_map/ppermute | solution.py:229

commit v3 on v2

v3 whole, which is shorter than its diff:
```python
import jax
import jax.numpy as jnp
from jax import lax
from jax.experimental import pallas as pl
from jax.experimental.pallas import tpu as pltpu
from jax.sharding import PartitionSpec as P

MOM = 4
HALO = 4
ONSITE_MASS = 0.3
SECOND_HOP = 0.2
BAND_SCALE = 4.5
LANES = 128
SUB = 8
TILES = 4
F32 = jnp.float32


def pack_kernel(in_ref, out_ref, turned):
    columns, groups, slabs, width = in_ref.shape
    block = lax.broadcasted_iota(jnp.int32, (SUB, LANES), 1) // width
    odd, high = block % 2 == 1, block >= 2
    lane = lax.broadcasted_iota(jnp.int32, (SUB, LANES), 1)
    swapped = jnp.where(odd, lane - width, lane + width)
    spots = [(k, base) for k in range(groups) for base in range(0, slabs, 4)]
    for slot, (k, base) in enumerate(spots):
        if base % 8 == 0:
            octets = [jnp.swapaxes(in_ref[c : c + SUB, k, base : base + SUB, :], 0, 1) for c in range(0, columns, SUB)]
        rows = [octets[c][base % 8 + s] for s in range(4) for c in range(columns // SUB)]
        turned[slot] = jnp.concatenate(rows, axis=0).T
    for slot, (k, base) in enumerate(spots):
        v = [turned[slot, pl.ds(t, SUB, stride=TILES), :] for t in range(TILES)]
        for p in (0, 2):
            low, upper = v[p], v[p + 1]
            moved = jnp.take_along_axis(jnp.where(odd, low, upper), swapped, axis=1)
            v[p], v[p + 1] = jnp.where(odd, moved, low), jnp.where(odd, upper, moved)
        for p in (0, 1):
            low, upper = v[p], v[p + 2]
            moved = pltpu.roll(jnp.where(high, low, upper), LANES // 2, 1)
            v[p], v[p + 2] = jnp.where(high, moved, low), jnp.where(high, upper, moved)
        for s in range(4):
            out_ref[k, base + s] = v[s]


def pack(pieces):
    columns, groups, slabs, width = pieces.shape
    step = 2
    out = pl.pallas_call(
        pack_kernel,
        grid=(groups // step,),
        in_specs=[pl.BlockSpec((columns, step, slabs, width), lambda k: (0, k, 0, 0))],
        out_specs=pl.BlockSpec((step, slabs, SUB, LANES), lambda k: (k, 0, 0, 0)),
        out_shape=jax.ShapeDtypeStruct((groups, slabs, SUB, LANES), F32),
        scratch_shapes=[pltpu.VMEM((step * slabs // 4, width, LANES), F32)],
        name="pack",
    )(pieces)
    return out.reshape(groups * slabs, SUB, LANES)


def wrap_masks():
    lane = lax.broadcasted_iota(jnp.int32, (SUB, LANES), 1)
    return lane == 0, lane == LANES - 1


def ahead(tiles, is_last):
    wrapped = jnp.where(is_last, 0.0, pltpu.roll(tiles[0], LANES - 1, 1))
    return tiles[1:] + [wrapped]


def behind(tiles, is_first):
    wrapped = jnp.where(is_first, 0.0, pltpu.roll(tiles[-1], 1, 1))
    return [wrapped] + tiles[:-1]


def stencil_row(level, parity, below, centre, above, old, mask, wraps):
    is_first, is_last = wraps
    T = range(TILES)
    nxt, prv, second = [], [], []
    for r in (0, 1):
        w = centre[r]
        diag = [above[r][t] + below[r][t] for t in T]
        fore, back = ahead(w, is_last), behind(w, is_first)
        if level == 0:
            a = ahead([2.0 * fore[t] - diag[t] for t in T], is_last)
            b = behind([2.0 * back[t] - diag[t] for t in T], is_first)
            second.append([a[t] + b[t] for t in T])
        else:
            a = ahead([fore[t] - diag[t] for t in T], is_last)
            b = behind([back[t] - diag[t] for t in T], is_first)
            second.append([a[t] - b[t] for t in T])
        nxt.append(fore)
        prv.append(back)
    result = []
    for r in (0, 1):
        values = []
        for t in T:
            sign = 1.0 if (parity + t) % 2 == 0 else -1.0
            if level == 0:
                along = prv[1][t] - nxt[1][t] if r == 0 else nxt[0][t] - prv[0][t]
                total = along - (SECOND_HOP * sign) * second[r][t]
            else:
                vertical = above[r][t] if sign > 0 else below[r][t]
                near = (nxt[r][t] + prv[r][t]) + vertical
                turn = -sign if r == 0 else sign
                total = near + (
                    (ONSITE_MASS * sign) * centre[r][t] + (SECOND_HOP * turn) * second[1 - r][t]
                )
            total = total * mask[t]
            values.append(total - old[r][t] if level > 1 else total)
        result.append(values)
    return result


SCALES = (1.0, 1.0 / BAND_SCALE, 2.0 / BAND_SCALE, 2.0 / BAND_SCALE)


def scaled(level, mask):
    return mask if level == 0 else [SCALES[level] * m for m in mask]


def turn_row(src, first):
    return src[pl.ds(first, 16)].reshape(LANES, LANES).T


def product(acc, blocks, left_ref, y):
    for t in range(TILES):
        zero = jnp.zeros((SUB, LANES), F32)
        stacked = [blocks(r, m, h, t) for r in (0, 1) for m in range(MOM) for h in (0, 1)]
        rhs = jnp.concatenate([zero if b is None else b for b in stacked], axis=0)
        term = lax.dot_general(
            rhs.astype(jnp.bfloat16),
            left_ref[y, :, t * LANES : (t + 1) * LANES],
            (((1,), (1,)), ((), ())),
            preferred_element_type=F32,
        )
        acc = term if acc is None else acc + term
    return acc


def inner_kernel(recv_ref, pres_ref, left_ref, sum_ref, edge_ref, field, presb):
    rows = left_ref.shape[0]
    wraps = wrap_masks()
    T = range(TILES)

    @pl.loop(0, rows // 4)
    def _(i):
        for k in range(4):
            y = 4 * i + k
            turned = turn_row(recv_ref, y * 16)
            for t in T:
                mask = jnp.broadcast_to(pres_ref[y, pl.ds(t, 1), :], (SUB, LANES))
                presb[y, t] = mask
                for q in range(4):
                    at = (4 * t + q) * SUB
                    field[0, y, q // 2, q % 2, t] = turned[at : at + SUB] * mask

    def load(level, y, half):
        return [[field[level, y, r, half, t] for t in T] for r in (0, 1)]

    for level in range(MOM):
        first = level + 1

        @pl.loop(0, (rows - 2 * first) // 2)
        def _(i, level=level, first=first):
            y = first + 2 * i
            masks = [scaled(level, [presb[y + k, t] for t in T]) for k in (0, 1)]
            for half in (0, 1):
                window = [load(level, y + k, half) for k in (-1, 0, 1, 2)]
                for k in (0, 1):
                    old = load(level - 1, y + k, half) if level > 1 else None
                    values = stencil_row(
                        level, (first + k) % 2, *window[k : k + 3], old, masks[k], wraps
                    )
                    for r in (0, 1):
                        for t in T:
                            field[(level + 1) % MOM, y + k, r, half, t] = values[r][t]

    for level in range(MOM):
        edge_ref[level, 0] = field[level, level : level + 2]
        edge_ref[level, 1] = field[level, rows - 2 - level : rows - level]
    acc = None
    for y in range(1, rows - 1):

        def blocks(r, m, half, t, y=y):
            return field[(m + 1) % MOM, y, r, half, t] if m < y < rows - 1 - m else None

        acc = product(acc, blocks, left_ref, y)
    sum_ref[...] = acc


def outer_kernel(lo_ref, hi_ref, pres_ref, left_ref, sum_ref, edge_ref, out_ref, field, presb):
    rows = left_ref.shape[0]
    wraps = wrap_masks()
    T = range(TILES)
    tail = HALO * 16
    base = (-HALO, rows - 2 * HALO)

    for i in range(HALO):
        for side, src, j in ((0, lo_ref, i), (1, hi_ref, 2 * HALO + i)):
            turned = turn_row(src, i * 16)
            for t in T:
                at = i * TILES + t
                row = src[tail + at // SUB, pl.ds(at % SUB, 1), :]
                mask = jnp.broadcast_to(row, (SUB, LANES))
                presb[side, j, t] = mask
                for q in range(4):
                    at = (4 * t + q) * SUB
                    field[0, side, j, q // 2, q % 2, t] = turned[at : at + SUB] * mask
    for side in (0, 1):
        for i in range(HALO):
            j = HALO + i
            for t in T:
                row = pres_ref[base[side] + j, pl.ds(t, 1), :]
                presb[side, j, t] = jnp.broadcast_to(row, (SUB, LANES))

    def given(level, side):
        first = HALO + level if side == 0 else 2 * HALO - 2 - level
        return first, first + 1

    def tile(level, side, j, r, half, t):
        spots = given(level, side)
        if j in spots:
            return edge_ref[level, side, spots.index(j), r, half, t]
        return field[level, side, j, r, half, t]

    def load(level, side, j, half):
        return [[tile(level, side, j, r, half, t) for t in T] for r in (0, 1)]

    for level in range(MOM):
        for side in (0, 1):
            first = 1 + level if side == 0 else 2 * HALO - 1 - level
            for half in (0, 1):
                window = [load(level, side, first + k, half) for k in range(-1, 5)]
                for k in range(4):
                    j = first + k
                    mask = scaled(level, [presb[side, j, t] for t in T])
                    old = load(level - 1, side, j, half) if level > 1 else None
                    values = stencil_row(level, j % 2, *window[k : k + 3], old, mask, wraps)
                    for r in (0, 1):
                        for t in T:
                            field[(level + 1) % MOM, side, j, r, half, t] = values[r][t]

    acc = sum_ref[...]
    for y in [*range(HALO), *range(rows - HALO, rows)]:
        side = 0 if y < HALO else 1

        def blocks(r, m, half, t, y=y, side=side):
            if m < y < rows - 1 - m:
                return None
            return field[(m + 1) % MOM, side, y - base[side], r, half, t]

        acc = product(acc, blocks, left_ref, y)
    half_rows = MOM * 2 * SUB
    top, bottom = acc[:half_rows], acc[half_rows:]
    lane_out = lax.broadcasted_iota(jnp.int32, top.shape, 1)
    out_ref[...] = pltpu.roll(bottom, LANES // 2, 1) + jnp.where(lane_out < LANES // 2, top, -top)


ROW = (2, 2, TILES, SUB, LANES)


def inner_moments(recv, pres, left):
    rows, n2, _ = left.shape
    vm = pl.BlockSpec(memory_space=pltpu.VMEM)
    return pl.pallas_call(
        inner_kernel,
        in_specs=[vm] * 3,
        out_specs=[vm] * 2,
        out_shape=[
            jax.ShapeDtypeStruct((2 * MOM * 2 * SUB, n2), F32),
            jax.ShapeDtypeStruct((MOM, 2, 2, *ROW), F32),
        ],
        scratch_shapes=[
            pltpu.VMEM((MOM, rows, *ROW), F32),
            pltpu.VMEM((rows, TILES, SUB, LANES), F32),
        ],
        compiler_params=pltpu.CompilerParams(vmem_limit_bytes=40 * 2**20),
        cost_estimate=pl.CostEstimate(flops=10**9, bytes_accessed=10**7, transcendentals=0),
        name="inner_moments",
    )(recv, pres, left)


def outer_moments(lo, hi, pres, left, inner_sum, edges):
    n2 = left.shape[1]
    vm = pl.BlockSpec(memory_space=pltpu.VMEM)
    return pl.pallas_call(
        outer_kernel,
        in_specs=[vm] * 6,
        out_specs=vm,
        out_shape=jax.ShapeDtypeStruct((MOM * 2 * SUB, n2), F32),
        scratch_shapes=[
            pltpu.VMEM((MOM, 2, 3 * HALO, *ROW), F32),
            pltpu.VMEM((2, 3 * HALO, TILES, SUB, LANES), F32),
        ],
        compiler_params=pltpu.CompilerParams(vmem_limit_bytes=40 * 2**20),
        name="outer_moments",
    )(lo, hi, pres, left, inner_sum, edges)


def per_device(right_vectors, left_vectors, vacancy):
    parts, width_group, groups, slabs, _, piece = right_vectors.shape
    count = lax.axis_size("sites")
    up = [(i, (i + 1) % count) for i in range(count)]
    down = [((i + 1) % count, i) for i in range(count)]
    n_left, rows, width = left_vectors.shape[1:]

    packed = pack(right_vectors.reshape(parts * width_group, groups, slabs, piece))
    packed, left_vectors = lax.optimization_barrier((packed, left_vectors))
    recv = lax.all_to_all(packed, ("cols", "sites"), 0, 0, tiled=True)

    site = lax.broadcasted_iota(jnp.int32, (width, width), 0)
    place = lax.broadcasted_iota(jnp.int32, (width, width), 1)
    to_place = (site % TILES * LANES + site // TILES == place).astype(jnp.bfloat16)
    left = left_vectors.reshape(2 * n_left * rows, width)
    left = jnp.dot(left, to_place, preferred_element_type=jnp.bfloat16)
    left = jnp.swapaxes(left.reshape(2 * n_left, rows, width), 0, 1)
    present = jnp.dot(vacancy.astype(jnp.bfloat16), to_place, preferred_element_type=F32)
    present = present.reshape(rows, TILES, LANES)
    recv, left, present = lax.optimization_barrier((recv, left, present))

    edge = HALO * width // piece
    low_mask = present[:HALO].reshape(-1, SUB, LANES)
    high_mask = present[rows - HALO :].reshape(-1, SUB, LANES)
    lo = lax.ppermute(jnp.concatenate([recv[recv.shape[0] - edge :], high_mask]), "sites", up)
    hi = lax.ppermute(jnp.concatenate([recv[:edge], low_mask]), "sites", down)
    inner_sum, edges = inner_moments(recv, present, left)
    total = outer_moments(lo, hi, present, left, inner_sum, edges)
    step = 1
    while step < count:
        total = total + lax.ppermute(total, "sites", [(i, i ^ step) for i in range(count)])
        step *= 2
    out = total.reshape(MOM, width_group, 2, n_left)
    return jnp.transpose(out, (2, 0, 3, 1))[..., None]


def solution(mesh):
    return jax.shard_map(
        per_device,
        mesh=mesh,
        in_specs=(
            P(None, None, None, None, ("cols", "sites"), None),
            P(None, None, "sites", None),
            P("sites", None),
        ),
        out_specs=P(None, None, None, None, "cols"),
        check_vma=False,
    )
```

time: 91.1 us -> 85.7 us (0.941)
  waiting for transfers between devices: 51 us -> 46.6 us
  local copies, waits for them, and re-layouts: 2.98 us -> 0.79 us
  Pallas kernels: 11 us -> 12.2 us
    ppermute x1, waiting for transfers between devices: 6.74 us -> 2.26 us  [per_device(): lax.ppermute(jnp.concatenate([recv[recv.shape[0] - edge:], high_mask]), '...]
    unnamed x4 -> x2, local copies, waits for them, and re-layouts: 2.19 us -> 0.01 us
    pallas_call x1, Pallas kernels: 4.34 us -> 5.85 us  [pack(): pl.pallas_call(pack_kernel, grid=(groups // step,), in_specs=[pl.BlockSpe...]
    pallas_call x1 -> x2, Pallas kernels: 6.69 us -> 6.39 us  [the longest x1 4.47 us: inner_moments(): pl.pallas_call(inner_kernel, in_specs=[vm] * 3, out_specs=[vm] * 2, out_s...]
  transfers between devices with their start and end apart: 8 -> 8, of which waited for: 7 -> 7; matrix products, arithmetic and copies ran while one was open for 6% -> 6% of each run, Pallas kernels for 0% -> 5%
where the time goes in v3:
time: 85.7 us; the launch traced here: 85.4 us
  waiting for transfers between devices  46.6 us (54%)
  starting transfers between devices  20.6 us (24%)
  Pallas kernels  12.2 us (14%)
  matrix products  5.05 us (6%)
    all_to_all x1, waiting for transfers between devices, per_device(): recv = lax.all_to_all(packed, ('cols', 'sites'), 0, 0, tiled=True)  25.1 us
    ppermute x5, waiting for transfers between devices, per_device(): lax.ppermute(total, 'sites', [(i, i ^ step) for i in range(count)])  19.2 us
    all_to_all x1, starting transfers between devices, per_device(): recv = lax.all_to_all(packed, ('cols', 'sites'), 0, 0, tiled=True)  14.7 us
    pallas_call x1, Pallas kernels, pack(): pl.pallas_call(pack_kernel, grid=(groups // step,), in_specs=[pl.BlockSpe...  5.85 us
    pallas_call x1, Pallas kernels, inner_moments(): pl.pallas_call(inner_kernel, in_specs=[vm] * 3, out_specs=[vm] * 2, out_s...  4.47 us
    dot_general x1, matrix products, per_device(): left = jnp.dot(left, to_place, preferred_element_type=jnp.bfloat16)  4.46 us
    ppermute x1, starting transfers between devices, per_device(): hi = lax.ppermute(jnp.concatenate([recv[:edge], low_mask]), 'sites', down)  4.32 us
    ppermute x1, waiting for transfers between devices, per_device(): lax.ppermute(jnp.concatenate([recv[recv.shape[0] - edge:], high_mask]), '...  2.26 us
  transfers between devices with their start and end apart: 8, of which 7 were waited for; matrix products, arithmetic and copies ran while one was open for 6% of the time, Pallas kernels for 5%

profile of v3, /device:TPU:2, one launch (start us, length us, event | category | flops | bytes accessed | tf_op | source)
XLA Modules:
  0.0 85.4 jit_solution(15955253158608743256)
XLA Ops:
  0.0 5.8 %pack.1 = f32[8,32,8,128]{3,2,1,0:T(8,128)} custom-call(f32[32,8,32,32]{3,2,1,0:T(8,128)} %bitcast.15), custom_call_target="tpu_custom_call" | custom-call | tf_op jit(solution)/shard_map/pack/pallas_call | solution.py:48
  5.8 14.7 %all-to-all-start = ((f32[256,8,128]{2,1,0:T(8,128)}), f32[256,8,128]{2,1,0:T(8,128)S(1)}, u32[]{:S(2)}, u32[]{:S(2)}) async-start(f32[256,8,128]{2,1,0:T(8,128)} %bitcast.16), calls=%async_computation | async-start | bytes 2097152 | tf_op jit(solution)/shard_map/all_to_all | solution.py:309
  20.6 0.0 copy-done
  20.6 0.6 convolution_bitcast_fusion
  21.2 4.5 %fusion.2.left_ref = bf16[16,128,512]{2,1,0:T(8,128)(2,1)S(1)} fusion(bf16[128,16,512]{2,1,0:T(8,128)(2,1)} %bitcast.19, s32[512]{0:T(512)S(1)} %get-tuple-element.23, s32[512]{0:T(512)S(1)} %get-tuple-element.26, s32[512]{0:T(512)S(1)} %get-tuple-element.24, s32[512]{0:T(512)S(1)} %get-tuple-element.25, pred[512]{0:T(512)(128)(4,1)S(1)} %get-tuple-element.27, ...), kind=kOutput, calls=%fused_computation.2 | convolution fusion | flops 1075052544 | bytes 4203520 | tf_op jit(solution)/shard_map/dot_general | solution.py:315
  25.7 25.1 %all-to-all-done.recv_ref = f32[256,8,128]{2,1,0:T(8,128)S(1)} async-done(((f32[256,8,128]{2,1,0:T(8,128)}), f32[256,8,128]{2,1,0:T(8,128)S(1)}, u32[]{:S(2)}, u32[]{:S(2)}) %all-to-all-start) | async-done | bytes 1048608 | tf_op jit(solution)/shard_map/all_to_all | solution.py:309
  50.8 1.5 %collective-permute-start = (f32[66,8,128]{2,1,0:T(8,128)S(1)}, f32[66,8,128]{2,1,0:T(8,128)S(1)}, u32[]{:S(2)}, u32[]{:S(2)}) collective-permute-start(f32[66,8,128]{2,1,0:T(8,128)S(1)} %pad_maximum_fusion), channel_id=1, source_target_pairs={{0,1},{1,2},{2,3},{3,4},{4,5},{5,6},{6,7},{7,8},{8,9},{9,10},{10,1... | collective-permute-start | bytes 811016 | tf_op jit(solution)/shard_map/ppermute | solution.py:324
  52.3 4.3 %collective-permute-start.1 = (f32[66,8,128]{2,1,0:T(8,128)S(1)}, f32[66,8,128]{2,1,0:T(8,128)S(1)}, u32[]{:S(2)}, u32[]{:S(2)}) collective-permute-start(f32[66,8,128]{2,1,0:T(8,128)S(1)} %pad_maximum_fusion.1), channel_id=1, source_target_pairs={{1,0},{2,1},{3,2},{4,3},{5,4},{6,5},{7,6},{8,7},{9,8},{10,9},{11,1... | collective-permute-start | bytes 811016 | tf_op jit(solution)/shard_map/ppermute | solution.py:325
  56.6 4.5 %inner_moments.1 = (f32[128,128]{1,0:T(8,128)S(1)}, f32[4,2,2,2,2,4,8,128]{7,6,5,4,3,2,1,0:T(8,128)S(1)}) custom-call(f32[256,8,128]{2,1,0:T(8,128)S(1)} %all-to-all-done.recv_ref, f32[16,4,128]{2,1,0:T(4,128)S(1)} %reshape.24.pres_ref, bf16[16,128,512]{2,1,0:T(8,128)(2,1)S(1)} %fusion.2.left_ref), custom_call_target="tpu_custom_call" | custom-call | flops 1000000000 | bytes 10000000 | tf_op jit(solution)/shard_map/inner_moments/pallas_call | solution.py:265
  61.1 2.3 %collective-permute-done.lo_ref = f32[66,8,128]{2,1,0:T(8,128)S(1)} collective-permute-done((f32[66,8,128]{2,1,0:T(8,128)S(1)}, f32[66,8,128]{2,1,0:T(8,128)S(1)}, u32[]{:S(2)}, u32[]{:S(2)}) %collective-permute-start) | collective-permute-done | bytes 270368 | tf_op jit(solution)/shard_map/ppermute | solution.py:324
  63.4 0.0 collective-permute-done.1.hi_ref
  63.4 1.9 %outer_moments.1 = f32[64,128]{1,0:T(8,128)S(1)} custom-call(f32[66,8,128]{2,1,0:T(8,128)S(1)} %collective-permute-done.lo_ref, f32[66,8,128]{2,1,0:T(8,128)S(1)} %collective-permute-done.1.hi_ref, f32[16,4,128]{2,1,0:T(4,128)S(1)} %reshape.24.pres_ref, bf16[16,128,512]{2,1,0:T(8,128)(2,1)S(1)} %fusion.2.left_ref, f32[128,128]{1,0:T(8,128)S(1)} %get-tuple-element.17.sum_ref, ...), custom_call_target="tpu_custom_call" | custom-call | tf_op jit(solution)/shard_map/outer_moments/pallas_call | solution.py:286
  65.3 0.1 collective-permute-start.2
  65.4 1.2 %collective-permute-done.2 = f32[64,128]{1,0:T(8,128)S(1)} collective-permute-done((f32[64,128]{1,0:T(8,128)S(1)}, f32[64,128]{1,0:T(8,128)S(1)}, u32[]{:S(2)}, u32[]{:S(2)}) %collective-permute-start.2) | collective-permute-done | bytes 32800 | tf_op jit(solution)/shard_map/ppermute | solution.py:330
  66.6 0.0 collective-permute-start.3
  66.6 3.9 %collective-permute-done.3 = f32[64,128]{1,0:T(8,128)S(1)} collective-permute-done((f32[64,128]{1,0:T(8,128)S(1)}, f32[64,128]{1,0:T(8,128)S(1)}, u32[]{:S(2)}, u32[]{:S(2)}) %collective-permute-start.3) | collective-permute-done | bytes 32800 | tf_op jit(solution)/shard_map/ppermute | solution.py:330
  70.5 0.0 collective-permute-start.4
  70.5 4.8 %collective-permute-done.4 = f32[64,128]{1,0:T(8,128)S(1)} collective-permute-done((f32[64,128]{1,0:T(8,128)S(1)}, f32[64,128]{1,0:T(8,128)S(1)}, u32[]{:S(2)}, u32[]{:S(2)}) %collective-permute-start.4) | collective-permute-done | bytes 32800 | tf_op jit(solution)/shard_map/ppermute | solution.py:330
  75.3 0.0 collective-permute-start.5
  75.3 3.9 %collective-permute-done.5 = f32[64,128]{1,0:T(8,128)S(1)} collective-permute-done((f32[64,128]{1,0:T(8,128)S(1)}, f32[64,128]{1,0:T(8,128)S(1)}, u32[]{:S(2)}, u32[]{:S(2)}) %collective-permute-start.5) | collective-permute-done | bytes 32800 | tf_op jit(solution)/shard_map/ppermute | solution.py:330
  79.3 0.0 collective-permute-start.6
  79.3 5.4 %collective-permute-done.6 = f32[64,128]{1,0:T(8,128)S(1)} collective-permute-done((f32[64,128]{1,0:T(8,128)S(1)}, f32[64,128]{1,0:T(8,128)S(1)}, u32[]{:S(2)}, u32[]{:S(2)}) %collective-permute-start.6) | collective-permute-done | bytes 32800 | tf_op jit(solution)/shard_map/ppermute | solution.py:330
  84.7 0.1 reshape.27
  84.8 0.6 copy.5
  (14 shorter events, 0.1 us)
Async XLA Ops:
  5.8 14.7 %copy-start = (s32[16,512]{1,0:T(8,128)S(1)}, s32[16,512]{1,0:T(8,128)}, u32[]{:S(2)}) copy-start(s32[16,512]{1,0:T(8,128)} %param.5) | copy-start | bytes 98308
  5.8 44.9 %all-to-all-start = ((f32[256,8,128]{2,1,0:T(8,128)}), f32[256,8,128]{2,1,0:T(8,128)S(1)}, u32[]{:S(2)}, u32[]{:S(2)}) async-start(f32[256,8,128]{2,1,0:T(8,128)} %bitcast.16), calls=%async_computation | async-start | bytes 2097152 | tf_op jit(solution)/shard_map/all_to_all | solution.py:309
  50.8 12.6 %collective-permute-start = (f32[66,8,128]{2,1,0:T(8,128)S(1)}, f32[66,8,128]{2,1,0:T(8,128)S(1)}, u32[]{:S(2)}, u32[]{:S(2)}) collective-permute-start(f32[66,8,128]{2,1,0:T(8,128)S(1)} %pad_maximum_fusion), channel_id=1, source_target_pairs={{0,1},{1,2},{2,3},{3,4},{4,5},{5,6},{6,7},{7,8},{8,9},{9,10},{10,1... | collective-permute-start | bytes 811016 | tf_op jit(solution)/shard_map/ppermute | solution.py:324
  52.3 11.1 %collective-permute-start.1 = (f32[66,8,128]{2,1,0:T(8,128)S(1)}, f32[66,8,128]{2,1,0:T(8,128)S(1)}, u32[]{:S(2)}, u32[]{:S(2)}) collective-permute-start(f32[66,8,128]{2,1,0:T(8,128)S(1)} %pad_maximum_fusion.1), channel_id=1, source_target_pairs={{1,0},{2,1},{3,2},{4,3},{5,4},{6,5},{7,6},{8,7},{9,8},{10,9},{11,1... | collective-permute-start | bytes 811016 | tf_op jit(solution)/shard_map/ppermute | solution.py:325
  65.3 1.3 %collective-permute-start.2 = (f32[64,128]{1,0:T(8,128)S(1)}, f32[64,128]{1,0:T(8,128)S(1)}, u32[]{:S(2)}, u32[]{:S(2)}) collective-permute-start(f32[64,128]{1,0:T(8,128)S(1)} %outer_moments.1), channel_id=1, source_target_pairs={{0,1},{1,0},{2,3},{3,2},{4,5},{5,4},{6,7},{7,6},{8,9},{9,8},{10,11... | collective-permute-start | bytes 98312 | tf_op jit(solution)/shard_map/ppermute | solution.py:330
  66.6 3.9 %collective-permute-start.3 = (f32[64,128]{1,0:T(8,128)S(1)}, f32[64,128]{1,0:T(8,128)S(1)}, u32[]{:S(2)}, u32[]{:S(2)}) collective-permute-start(f32[64,128]{1,0:T(8,128)S(1)} %add.33), channel_id=1, source_target_pairs={{0,2},{1,3},{2,0},{3,1},{4,6},{5,7},{6,4},{7,5},{8,10},{9,11},{10,... | collective-permute-start | bytes 98312 | tf_op jit(solution)/shard_map/ppermute | solution.py:330
  70.5 4.8 %collective-permute-start.4 = (f32[64,128]{1,0:T(8,128)S(1)}, f32[64,128]{1,0:T(8,128)S(1)}, u32[]{:S(2)}, u32[]{:S(2)}) collective-permute-start(f32[64,128]{1,0:T(8,128)S(1)} %add.34), channel_id=1, source_target_pairs={{0,4},{1,5},{2,6},{3,7},{4,0},{5,1},{6,2},{7,3},{8,12},{9,13},{10,... | collective-permute-start | bytes 98312 | tf_op jit(solution)/shard_map/ppermute | solution.py:330
  75.3 3.9 %collective-permute-start.5 = (f32[64,128]{1,0:T(8,128)S(1)}, f32[64,128]{1,0:T(8,128)S(1)}, u32[]{:S(2)}, u32[]{:S(2)}) collective-permute-start(f32[64,128]{1,0:T(8,128)S(1)} %add.35), channel_id=1, source_target_pairs={{0,8},{1,9},{2,10},{3,11},{4,12},{5,13},{6,14},{7,15},{8,0},{9,1},... | collective-permute-start | bytes 98312 | tf_op jit(solution)/shard_map/ppermute | solution.py:330
  79.3 5.4 %collective-permute-start.6 = (f32[64,128]{1,0:T(8,128)S(1)}, f32[64,128]{1,0:T(8,128)S(1)}, u32[]{:S(2)}, u32[]{:S(2)}) collective-permute-start(f32[64,128]{1,0:T(8,128)S(1)} %add.36), channel_id=1, source_target_pairs={{0,16},{1,17},{2,18},{3,19},{4,20},{5,21},{6,22},{7,23},{8,24},{9,... | collective-permute-start | bytes 98312 | tf_op jit(solution)/shard_map/ppermute | solution.py:330

commit v4 on v3

--- a/solution.py
+++ b/solution.py
@@ -16,35 +16,45 @@
 F32 = jnp.float32
 
 
+PACK_GROUPS = 4
+MERGES = 16
+
+
 def pack_kernel(in_ref, out_ref, turned):
     columns, groups, slabs, width = in_ref.shape
-    block = lax.broadcasted_iota(jnp.int32, (SUB, LANES), 1) // width
-    odd, high = block % 2 == 1, block >= 2
     lane = lax.broadcasted_iota(jnp.int32, (SUB, LANES), 1)
+    odd, high = lane // width % 2 == 1, lane // width >= 2
     swapped = jnp.where(odd, lane - width, lane + width)
-    spots = [(k, base) for k in range(groups) for base in range(0, slabs, 4)]
-    for slot, (k, base) in enumerate(spots):
-        if base % 8 == 0:
-            octets = [jnp.swapaxes(in_ref[c : c + SUB, k, base : base + SUB, :], 0, 1) for c in range(0, columns, SUB)]
-        rows = [octets[c][base % 8 + s] for s in range(4) for c in range(columns // SUB)]
-        turned[slot] = jnp.concatenate(rows, axis=0).T
-    for slot, (k, base) in enumerate(spots):
-        v = [turned[slot, pl.ds(t, SUB, stride=TILES), :] for t in range(TILES)]
-        for p in (0, 2):
-            low, upper = v[p], v[p + 1]
-            moved = jnp.take_along_axis(jnp.where(odd, low, upper), swapped, axis=1)
-            v[p], v[p + 1] = jnp.where(odd, moved, low), jnp.where(odd, upper, moved)
-        for p in (0, 1):
-            low, upper = v[p], v[p + 2]
-            moved = pltpu.roll(jnp.where(high, low, upper), LANES // 2, 1)
-            v[p], v[p + 2] = jnp.where(high, moved, low), jnp.where(high, upper, moved)
-        for s in range(4):
-            out_ref[k, base + s] = v[s]
+    for k in range(groups):
+        for base in range(0, slabs, SUB):
+            octets = [
+                jnp.swapaxes(in_ref[c : c + SUB, k, base : base + SUB, :], 0, 1)
+                for c in range(0, columns, SUB)
+            ]
+            for half in (0, 4):
+                rows = [octet[half + s] for s in range(4) for octet in octets]
+                turned[(k * slabs + base + half) // 4] = jnp.concatenate(rows, axis=0).T
+
+    @pl.loop(0, groups * slabs // 4 // MERGES)
+    def _(i):
+        for j in range(MERGES):
+            slot = i * MERGES + j
+            v = [turned[slot, pl.ds(t, SUB, stride=TILES), :] for t in range(TILES)]
+            for p in (0, 2):
+                low, upper = v[p], v[p + 1]
+                moved = jnp.take_along_axis(jnp.where(odd, low, upper), swapped, axis=1)
+                v[p], v[p + 1] = jnp.where(odd, moved, low), jnp.where(odd, upper, moved)
+            for p in (0, 1):
+                low, upper = v[p], v[p + 2]
+                moved = pltpu.roll(jnp.where(high, low, upper), LANES // 2, 1)
+                v[p], v[p + 2] = jnp.where(high, moved, low), jnp.where(high, upper, moved)
+            for s in range(4):
+                out_ref[slot * 4 // slabs, slot * 4 % slabs + s] = v[s]
 
 
 def pack(pieces):
     columns, groups, slabs, width = pieces.shape
-    step = 2
+    step = PACK_GROUPS
     out = pl.pallas_call(
         pack_kernel,
         grid=(groups // step,),
@@ -325,12 +335,10 @@
     hi = lax.ppermute(jnp.concatenate([recv[:edge], low_mask]), "sites", down)
     inner_sum, edges = inner_moments(recv, present, left)
     total = outer_moments(lo, hi, present, left, inner_sum, edges)
-    step = 1
-    while step < count:
-        total = total + lax.ppermute(total, "sites", [(i, i ^ step) for i in range(count)])
-        step *= 2
-    out = total.reshape(MOM, width_group, 2, n_left)
-    return jnp.transpose(out, (2, 0, 3, 1))[..., None]
+    for flip in (1, 2, 4, 8, 24):
+        total = total + lax.ppermute(total, "sites", [(i, i ^ flip) for i in range(count)])
+    out = jnp.stack([total[:, :n_left], total[:, n_left:]]).reshape(2, MOM, width_group, n_left)
+    return jnp.swapaxes(out, 2, 3)[..., None]
 
 
 def solution(mesh):

time: 85.7 us -> 83.8 us (0.978)
  Pallas kernels: 12.2 us -> 10.7 us
    pallas_call x1, Pallas kernels: 5.85 us -> 4.32 us  [pack(): pl.pallas_call(pack_kernel, grid=(groups // step,), in_specs=[pl.BlockSpe...]
where the time goes in v4:
time: 83.8 us; the launch traced here: 83.6 us
  waiting for transfers between devices  46.3 us (55%)
  starting transfers between devices  20.6 us (25%)
  Pallas kernels  10.7 us (13%)
  matrix products  5.05 us (6%)
    all_to_all x1, waiting for transfers between devices, per_device(): recv = lax.all_to_all(packed, ('cols', 'sites'), 0, 0, tiled=True)  25.1 us
    ppermute x5, waiting for transfers between devices, per_device(): lax.ppermute(total, 'sites', [(i, i ^ flip) for i in range(count)])  18.9 us
    all_to_all x1, starting transfers between devices, per_device(): recv = lax.all_to_all(packed, ('cols', 'sites'), 0, 0, tiled=True)  14.7 us
    pallas_call x1, Pallas kernels, inner_moments(): pl.pallas_call(inner_kernel, in_specs=[vm] * 3, out_specs=[vm] * 2, out_s...  4.47 us
    dot_general x1, matrix products, per_device(): left = jnp.dot(left, to_place, preferred_element_type=jnp.bfloat16)  4.46 us
    ppermute x1, starting transfers between devices, per_device(): hi = lax.ppermute(jnp.concatenate([recv[:edge], low_mask]), 'sites', down)  4.32 us
    pallas_call x1, Pallas kernels, pack(): pl.pallas_call(pack_kernel, grid=(groups // step,), in_specs=[pl.BlockSpe...  4.32 us
    ppermute x1, waiting for transfers between devices, per_device(): lax.ppermute(jnp.concatenate([recv[recv.shape[0] - edge:], high_mask]), '...  2.27 us
  transfers between devices with their start and end apart: 8, of which 7 were waited for; matrix products, arithmetic and copies ran while one was open for 6% of the time, Pallas kernels for 5%

profile of v4, /device:TPU:2, one launch (start us, length us, event | category | flops | bytes accessed | tf_op | source)
XLA Modules:
  0.0 83.6 jit_solution(12322420772457937378)
XLA Ops:
  0.0 4.3 %pack.1 = f32[8,32,8,128]{3,2,1,0:T(8,128)} custom-call(f32[32,8,32,32]{3,2,1,0:T(8,128)} %bitcast.17), custom_call_target="tpu_custom_call" | custom-call | tf_op jit(solution)/shard_map/pack/pallas_call | solution.py:58
  4.3 14.7 %all-to-all-start = ((f32[256,8,128]{2,1,0:T(8,128)}), f32[256,8,128]{2,1,0:T(8,128)S(1)}, u32[]{:S(2)}, u32[]{:S(2)}) async-start(f32[256,8,128]{2,1,0:T(8,128)} %bitcast.18), calls=%async_computation | async-start | bytes 2097152 | tf_op jit(solution)/shard_map/all_to_all | solution.py:319
  19.1 0.0 copy-done
  19.1 0.6 convolution_bitcast_fusion
  19.7 4.5 %fusion.2.left_ref = bf16[16,128,512]{2,1,0:T(8,128)(2,1)S(1)} fusion(bf16[128,16,512]{2,1,0:T(8,128)(2,1)} %bitcast.23, s32[512]{0:T(512)S(1)} %get-tuple-element.25, s32[512]{0:T(512)S(1)} %get-tuple-element.28, s32[512]{0:T(512)S(1)} %get-tuple-element.26, s32[512]{0:T(512)S(1)} %get-tuple-element.27, pred[512]{0:T(512)(128)(4,1)S(1)} %get-tuple-element.29, ...), kind=kOutput, calls=%fused_computation.2 | convolution fusion | flops 1075052544 | bytes 4203520 | tf_op jit(solution)/shard_map/dot_general | solution.py:325
  24.2 25.1 %all-to-all-done.recv_ref = f32[256,8,128]{2,1,0:T(8,128)S(1)} async-done(((f32[256,8,128]{2,1,0:T(8,128)}), f32[256,8,128]{2,1,0:T(8,128)S(1)}, u32[]{:S(2)}, u32[]{:S(2)}) %all-to-all-start) | async-done | bytes 1048608 | tf_op jit(solution)/shard_map/all_to_all | solution.py:319
  49.3 1.5 %collective-permute-start = (f32[66,8,128]{2,1,0:T(8,128)S(1)}, f32[66,8,128]{2,1,0:T(8,128)S(1)}, u32[]{:S(2)}, u32[]{:S(2)}) collective-permute-start(f32[66,8,128]{2,1,0:T(8,128)S(1)} %pad_maximum_fusion), channel_id=1, source_target_pairs={{0,1},{1,2},{2,3},{3,4},{4,5},{5,6},{6,7},{7,8},{8,9},{9,10},{10,1... | collective-permute-start | bytes 811016 | tf_op jit(solution)/shard_map/ppermute | solution.py:334
  50.8 4.3 %collective-permute-start.1 = (f32[66,8,128]{2,1,0:T(8,128)S(1)}, f32[66,8,128]{2,1,0:T(8,128)S(1)}, u32[]{:S(2)}, u32[]{:S(2)}) collective-permute-start(f32[66,8,128]{2,1,0:T(8,128)S(1)} %pad_maximum_fusion.1), channel_id=1, source_target_pairs={{1,0},{2,1},{3,2},{4,3},{5,4},{6,5},{7,6},{8,7},{9,8},{10,9},{11,1... | collective-permute-start | bytes 811016 | tf_op jit(solution)/shard_map/ppermute | solution.py:335
  55.1 4.5 %inner_moments.1 = (f32[128,128]{1,0:T(8,128)S(1)}, f32[4,2,2,2,2,4,8,128]{7,6,5,4,3,2,1,0:T(8,128)S(1)}) custom-call(f32[256,8,128]{2,1,0:T(8,128)S(1)} %all-to-all-done.recv_ref, f32[16,4,128]{2,1,0:T(4,128)S(1)} %reshape.26.pres_ref, bf16[16,128,512]{2,1,0:T(8,128)(2,1)S(1)} %fusion.2.left_ref), custom_call_target="tpu_custom_call" | custom-call | flops 1000000000 | bytes 10000000 | tf_op jit(solution)/shard_map/inner_moments/pallas_call | solution.py:275
  59.6 2.3 %collective-permute-done.lo_ref = f32[66,8,128]{2,1,0:T(8,128)S(1)} collective-permute-done((f32[66,8,128]{2,1,0:T(8,128)S(1)}, f32[66,8,128]{2,1,0:T(8,128)S(1)}, u32[]{:S(2)}, u32[]{:S(2)}) %collective-permute-start) | collective-permute-done | bytes 270368 | tf_op jit(solution)/shard_map/ppermute | solution.py:334
  61.9 0.0 collective-permute-done.1.hi_ref
  61.9 1.9 %outer_moments.1 = f32[64,128]{1,0:T(8,128)S(1)} custom-call(f32[66,8,128]{2,1,0:T(8,128)S(1)} %collective-permute-done.lo_ref, f32[66,8,128]{2,1,0:T(8,128)S(1)} %collective-permute-done.1.hi_ref, f32[16,4,128]{2,1,0:T(4,128)S(1)} %reshape.26.pres_ref, bf16[16,128,512]{2,1,0:T(8,128)(2,1)S(1)} %fusion.2.left_ref, f32[128,128]{1,0:T(8,128)S(1)} %get-tuple-element.17.sum_ref, ...), custom_call_target="tpu_custom_call" | custom-call | tf_op jit(solution)/shard_map/outer_moments/pallas_call | solution.py:296
  63.8 0.1 collective-permute-start.2
  63.9 1.2 %collective-permute-done.2 = f32[64,128]{1,0:T(8,128)S(1)} collective-permute-done((f32[64,128]{1,0:T(8,128)S(1)}, f32[64,128]{1,0:T(8,128)S(1)}, u32[]{:S(2)}, u32[]{:S(2)}) %collective-permute-start.2) | collective-permute-done | bytes 32800 | tf_op jit(solution)/shard_map/ppermute | solution.py:339
  65.1 0.0 collective-permute-start.3
  65.1 3.9 %collective-permute-done.3 = f32[64,128]{1,0:T(8,128)S(1)} collective-permute-done((f32[64,128]{1,0:T(8,128)S(1)}, f32[64,128]{1,0:T(8,128)S(1)}, u32[]{:S(2)}, u32[]{:S(2)}) %collective-permute-start.3) | collective-permute-done | bytes 32800 | tf_op jit(solution)/shard_map/ppermute | solution.py:339
  69.0 0.0 collective-permute-start.4
  69.0 4.8 %collective-permute-done.4 = f32[64,128]{1,0:T(8,128)S(1)} collective-permute-done((f32[64,128]{1,0:T(8,128)S(1)}, f32[64,128]{1,0:T(8,128)S(1)}, u32[]{:S(2)}, u32[]{:S(2)}) %collective-permute-start.4) | collective-permute-done | bytes 32800 | tf_op jit(solution)/shard_map/ppermute | solution.py:339
  73.8 0.0 collective-permute-start.5
  73.8 3.9 %collective-permute-done.5 = f32[64,128]{1,0:T(8,128)S(1)} collective-permute-done((f32[64,128]{1,0:T(8,128)S(1)}, f32[64,128]{1,0:T(8,128)S(1)}, u32[]{:S(2)}, u32[]{:S(2)}) %collective-permute-start.5) | collective-permute-done | bytes 32800 | tf_op jit(solution)/shard_map/ppermute | solution.py:339
  77.7 0.0 collective-permute-start.6
  77.7 5.1 %collective-permute-done.6 = f32[64,128]{1,0:T(8,128)S(1)} collective-permute-done((f32[64,128]{1,0:T(8,128)S(1)}, f32[64,128]{1,0:T(8,128)S(1)}, u32[]{:S(2)}, u32[]{:S(2)}) %collective-permute-start.6) | collective-permute-done | bytes 32800 | tf_op jit(solution)/shard_map/ppermute | solution.py:339
  82.9 0.1 fusion.14
  82.9 0.6 pad_maximum_fusion.2
  (14 shorter events, 0.1 us)
Async XLA Ops:
  4.3 14.7 %copy-start = (s32[16,512]{1,0:T(8,128)S(1)}, s32[16,512]{1,0:T(8,128)}, u32[]{:S(2)}) copy-start(s32[16,512]{1,0:T(8,128)} %param.5) | copy-start | bytes 98308
  4.3 44.9 %all-to-all-start = ((f32[256,8,128]{2,1,0:T(8,128)}), f32[256,8,128]{2,1,0:T(8,128)S(1)}, u32[]{:S(2)}, u32[]{:S(2)}) async-start(f32[256,8,128]{2,1,0:T(8,128)} %bitcast.18), calls=%async_computation | async-start | bytes 2097152 | tf_op jit(solution)/shard_map/all_to_all | solution.py:319
  49.3 12.6 %collective-permute-start = (f32[66,8,128]{2,1,0:T(8,128)S(1)}, f32[66,8,128]{2,1,0:T(8,128)S(1)}, u32[]{:S(2)}, u32[]{:S(2)}) collective-permute-start(f32[66,8,128]{2,1,0:T(8,128)S(1)} %pad_maximum_fusion), channel_id=1, source_target_pairs={{0,1},{1,2},{2,3},{3,4},{4,5},{5,6},{6,7},{7,8},{8,9},{9,10},{10,1... | collective-permute-start | bytes 811016 | tf_op jit(solution)/shard_map/ppermute | solution.py:334
  50.8 11.1 %collective-permute-start.1 = (f32[66,8,128]{2,1,0:T(8,128)S(1)}, f32[66,8,128]{2,1,0:T(8,128)S(1)}, u32[]{:S(2)}, u32[]{:S(2)}) collective-permute-start(f32[66,8,128]{2,1,0:T(8,128)S(1)} %pad_maximum_fusion.1), channel_id=1, source_target_pairs={{1,0},{2,1},{3,2},{4,3},{5,4},{6,5},{7,6},{8,7},{9,8},{10,9},{11,1... | collective-permute-start | bytes 811016 | tf_op jit(solution)/shard_map/ppermute | solution.py:335
  63.8 1.3 %collective-permute-start.2 = (f32[64,128]{1,0:T(8,128)S(1)}, f32[64,128]{1,0:T(8,128)S(1)}, u32[]{:S(2)}, u32[]{:S(2)}) collective-permute-start(f32[64,128]{1,0:T(8,128)S(1)} %outer_moments.1), channel_id=1, source_target_pairs={{0,1},{1,0},{2,3},{3,2},{4,5},{5,4},{6,7},{7,6},{8,9},{9,8},{10,11... | collective-permute-start | bytes 98312 | tf_op jit(solution)/shard_map/ppermute | solution.py:339
  65.1 3.9 %collective-permute-start.3 = (f32[64,128]{1,0:T(8,128)S(1)}, f32[64,128]{1,0:T(8,128)S(1)}, u32[]{:S(2)}, u32[]{:S(2)}) collective-permute-start(f32[64,128]{1,0:T(8,128)S(1)} %add.33), channel_id=1, source_target_pairs={{0,2},{1,3},{2,0},{3,1},{4,6},{5,7},{6,4},{7,5},{8,10},{9,11},{10,... | collective-permute-start | bytes 98312 | tf_op jit(solution)/shard_map/ppermute | solution.py:339
  69.0 4.8 %collective-permute-start.4 = (f32[64,128]{1,0:T(8,128)S(1)}, f32[64,128]{1,0:T(8,128)S(1)}, u32[]{:S(2)}, u32[]{:S(2)}) collective-permute-start(f32[64,128]{1,0:T(8,128)S(1)} %add.34), channel_id=1, source_target_pairs={{0,4},{1,5},{2,6},{3,7},{4,0},{5,1},{6,2},{7,3},{8,12},{9,13},{10,... | collective-permute-start | bytes 98312 | tf_op jit(solution)/shard_map/ppermute | solution.py:339
  73.8 3.9 %collective-permute-start.5 = (f32[64,128]{1,0:T(8,128)S(1)}, f32[64,128]{1,0:T(8,128)S(1)}, u32[]{:S(2)}, u32[]{:S(2)}) collective-permute-start(f32[64,128]{1,0:T(8,128)S(1)} %add.35), channel_id=1, source_target_pairs={{0,8},{1,9},{2,10},{3,11},{4,12},{5,13},{6,14},{7,15},{8,0},{9,1},... | collective-permute-start | bytes 98312 | tf_op jit(solution)/shard_map/ppermute | solution.py:339
  77.7 5.1 %collective-permute-start.6 = (f32[64,128]{1,0:T(8,128)S(1)}, f32[64,128]{1,0:T(8,128)S(1)}, u32[]{:S(2)}, u32[]{:S(2)}) collective-permute-start(f32[64,128]{1,0:T(8,128)S(1)} %add.36), channel_id=1, source_target_pairs={{0,24},{1,25},{2,26},{3,27},{4,28},{5,29},{6,30},{7,31},{8,16},{9,... | collective-permute-start | bytes 98312 | tf_op jit(solution)/shard_map/ppermute | solution.py:339

commit v5 on v4

--- a/solution.py
+++ b/solution.py
@@ -335,8 +335,13 @@
     hi = lax.ppermute(jnp.concatenate([recv[:edge], low_mask]), "sites", down)
     inner_sum, edges = inner_moments(recv, present, left)
     total = outer_moments(lo, hi, present, left, inner_sum, edges)
-    for flip in (1, 2, 4, 8, 24):
-        total = total + lax.ppermute(total, "sites", [(i, i ^ flip) for i in range(count)])
+    def moved(values, target):
+        return lax.ppermute(values, "sites", [(i, target(i)) for i in range(count)])
+
+    for flip in (1, 2, 4):
+        total = total + moved(total, lambda i: i ^ flip)
+    far, one, other = [moved(total, lambda i: (i + 8 * k) % count) for k in (2, 1, 3)]
+    total = (total + far) + (one + other)
     out = jnp.stack([total[:, :n_left], total[:, n_left:]]).reshape(2, MOM, width_group, n_left)
     return jnp.swapaxes(out, 2, 3)[..., None]
 

time: 83.8 us -> 82.2 us (0.981)
  waiting for transfers between devices: 46.3 us -> 42.6 us
  starting transfers between devices: 20.6 us -> 22.6 us
    ppermute x5 -> x6, waiting for transfers between devices: 18.9 us -> 15.3 us  [moved(): return lax.ppermute(values, 'sites', [(i, target(i)) for i in range(count)])]
    ppermute x5 -> x6, starting transfers between devices: 0.09 us -> 2.15 us  [moved(): return lax.ppermute(values, 'sites', [(i, target(i)) for i in range(count)])]
  transfers between devices with their start and end apart: 8 -> 9, of which waited for: 7 -> 8; matrix products, arithmetic and copies ran while one was open for 6% -> 6% of each run, Pallas kernels for 5% -> 5%
where the time goes in v5:
time: 82.2 us; the launch traced here: 82 us
  waiting for transfers between devices  42.6 us (52%)
  starting transfers between devices  22.6 us (27%)
  Pallas kernels  10.7 us (13%)
  matrix products  5.05 us (6%)
    all_to_all x1, waiting for transfers between devices, per_device(): recv = lax.all_to_all(packed, ('cols', 'sites'), 0, 0, tiled=True)  25.1 us
    ppermute x6, waiting for transfers between devices, moved(): return lax.ppermute(values, 'sites', [(i, target(i)) for i in range(count)])  15.3 us
    all_to_all x1, starting transfers between devices, per_device(): recv = lax.all_to_all(packed, ('cols', 'sites'), 0, 0, tiled=True)  14.7 us
    pallas_call x1, Pallas kernels, inner_moments(): pl.pallas_call(inner_kernel, in_specs=[vm] * 3, out_specs=[vm] * 2, out_s...  4.47 us
    dot_general x1, matrix products, per_device(): left = jnp.dot(left, to_place, preferred_element_type=jnp.bfloat16)  4.46 us
    pallas_call x1, Pallas kernels, pack(): pl.pallas_call(pack_kernel, grid=(groups // step,), in_specs=[pl.BlockSpe...  4.33 us
    ppermute x1, starting transfers between devices, per_device(): hi = lax.ppermute(jnp.concatenate([recv[:edge], low_mask]), 'sites', down)  4.32 us
    ppermute x1, waiting for transfers between devices, per_device(): lax.ppermute(jnp.concatenate([recv[recv.shape[0] - edge:], high_mask]), '...  2.26 us
  transfers between devices with their start and end apart: 9, of which 8 were waited for; matrix products, arithmetic and copies ran while one was open for 6% of the time, Pallas kernels for 5%

profile of v5, /device:TPU:2, one launch (start us, length us, event | category | flops | bytes accessed | tf_op | source)
XLA Modules:
  0.0 82.0 jit_solution(12369120563896153720)
XLA Ops:
  0.0 4.3 %pack.1 = f32[8,32,8,128]{3,2,1,0:T(8,128)} custom-call(f32[32,8,32,32]{3,2,1,0:T(8,128)} %bitcast.17), custom_call_target="tpu_custom_call" | custom-call | tf_op jit(solution)/shard_map/pack/pallas_call | solution.py:58
  4.3 14.7 %all-to-all-start = ((f32[256,8,128]{2,1,0:T(8,128)}), f32[256,8,128]{2,1,0:T(8,128)S(1)}, u32[]{:S(2)}, u32[]{:S(2)}) async-start(f32[256,8,128]{2,1,0:T(8,128)} %bitcast.18), calls=%async_computation | async-start | bytes 2097152 | tf_op jit(solution)/shard_map/all_to_all | solution.py:319
  19.1 0.6 convolution_bitcast_fusion
  19.7 4.5 %fusion.2.left_ref = bf16[16,128,512]{2,1,0:T(8,128)(2,1)S(1)} fusion(bf16[128,16,512]{2,1,0:T(8,128)(2,1)} %bitcast.23, s32[512]{0:T(512)S(1)} %get-tuple-element.25, s32[512]{0:T(512)S(1)} %get-tuple-element.28, s32[512]{0:T(512)S(1)} %get-tuple-element.26, s32[512]{0:T(512)S(1)} %get-tuple-element.27, pred[512]{0:T(512)(128)(4,1)S(1)} %get-tuple-element.29, ...), kind=kOutput, calls=%fused_computation.2 | convolution fusion | flops 1075052544 | bytes 4203520 | tf_op jit(solution)/shard_map/dot_general | solution.py:325
  24.2 25.1 %all-to-all-done.recv_ref = f32[256,8,128]{2,1,0:T(8,128)S(1)} async-done(((f32[256,8,128]{2,1,0:T(8,128)}), f32[256,8,128]{2,1,0:T(8,128)S(1)}, u32[]{:S(2)}, u32[]{:S(2)}) %all-to-all-start) | async-done | bytes 1048608 | tf_op jit(solution)/shard_map/all_to_all | solution.py:319
  49.3 1.5 %collective-permute-start = (f32[66,8,128]{2,1,0:T(8,128)S(1)}, f32[66,8,128]{2,1,0:T(8,128)S(1)}, u32[]{:S(2)}, u32[]{:S(2)}) collective-permute-start(f32[66,8,128]{2,1,0:T(8,128)S(1)} %pad_maximum_fusion), channel_id=1, source_target_pairs={{0,1},{1,2},{2,3},{3,4},{4,5},{5,6},{6,7},{7,8},{8,9},{9,10},{10,1... | collective-permute-start | bytes 811016 | tf_op jit(solution)/shard_map/ppermute | solution.py:334
  50.8 4.3 %collective-permute-start.1 = (f32[66,8,128]{2,1,0:T(8,128)S(1)}, f32[66,8,128]{2,1,0:T(8,128)S(1)}, u32[]{:S(2)}, u32[]{:S(2)}) collective-permute-start(f32[66,8,128]{2,1,0:T(8,128)S(1)} %pad_maximum_fusion.1), channel_id=1, source_target_pairs={{1,0},{2,1},{3,2},{4,3},{5,4},{6,5},{7,6},{8,7},{9,8},{10,9},{11,1... | collective-permute-start | bytes 811016 | tf_op jit(solution)/shard_map/ppermute | solution.py:335
  55.1 4.5 %inner_moments.1 = (f32[128,128]{1,0:T(8,128)S(1)}, f32[4,2,2,2,2,4,8,128]{7,6,5,4,3,2,1,0:T(8,128)S(1)}) custom-call(f32[256,8,128]{2,1,0:T(8,128)S(1)} %all-to-all-done.recv_ref, f32[16,4,128]{2,1,0:T(4,128)S(1)} %reshape.26.pres_ref, bf16[16,128,512]{2,1,0:T(8,128)(2,1)S(1)} %fusion.2.left_ref), custom_call_target="tpu_custom_call" | custom-call | flops 1000000000 | bytes 10000000 | tf_op jit(solution)/shard_map/inner_moments/pallas_call | solution.py:275
  59.6 2.3 %collective-permute-done.lo_ref = f32[66,8,128]{2,1,0:T(8,128)S(1)} collective-permute-done((f32[66,8,128]{2,1,0:T(8,128)S(1)}, f32[66,8,128]{2,1,0:T(8,128)S(1)}, u32[]{:S(2)}, u32[]{:S(2)}) %collective-permute-start) | collective-permute-done | bytes 270368 | tf_op jit(solution)/shard_map/ppermute | solution.py:334
  61.9 1.9 %outer_moments.1 = f32[64,128]{1,0:T(8,128)S(1)} custom-call(f32[66,8,128]{2,1,0:T(8,128)S(1)} %collective-permute-done.lo_ref, f32[66,8,128]{2,1,0:T(8,128)S(1)} %collective-permute-done.1.hi_ref, f32[16,4,128]{2,1,0:T(4,128)S(1)} %reshape.26.pres_ref, bf16[16,128,512]{2,1,0:T(8,128)(2,1)S(1)} %fusion.2.left_ref, f32[128,128]{1,0:T(8,128)S(1)} %get-tuple-element.17.sum_ref, ...), custom_call_target="tpu_custom_call" | custom-call | tf_op jit(solution)/shard_map/outer_moments/pallas_call | solution.py:296
  63.8 0.1 collective-permute-start.2
  63.9 1.2 %collective-permute-done.2 = f32[64,128]{1,0:T(8,128)S(1)} collective-permute-done((f32[64,128]{1,0:T(8,128)S(1)}, f32[64,128]{1,0:T(8,128)S(1)}, u32[]{:S(2)}, u32[]{:S(2)}) %collective-permute-start.2) | collective-permute-done | bytes 32800 | tf_op jit(solution)/shard_map/ppermute | solution.py:339
  65.1 0.0 collective-permute-start.3
  65.1 3.9 %collective-permute-done.3 = f32[64,128]{1,0:T(8,128)S(1)} collective-permute-done((f32[64,128]{1,0:T(8,128)S(1)}, f32[64,128]{1,0:T(8,128)S(1)}, u32[]{:S(2)}, u32[]{:S(2)}) %collective-permute-start.3) | collective-permute-done | bytes 32800 | tf_op jit(solution)/shard_map/ppermute | solution.py:339
  69.0 0.0 collective-permute-start.4
  69.0 4.8 %collective-permute-done.4 = f32[64,128]{1,0:T(8,128)S(1)} collective-permute-done((f32[64,128]{1,0:T(8,128)S(1)}, f32[64,128]{1,0:T(8,128)S(1)}, u32[]{:S(2)}, u32[]{:S(2)}) %collective-permute-start.4) | collective-permute-done | bytes 32800 | tf_op jit(solution)/shard_map/ppermute | solution.py:339
  73.8 0.0 collective-permute-start.7
  73.8 2.0 %collective-permute-start.6 = (f32[64,128]{1,0:T(8,128)S(1)}, f32[64,128]{1,0:T(8,128)S(1)}, u32[]{:S(2)}, u32[]{:S(2)}) collective-permute-start(f32[64,128]{1,0:T(8,128)S(1)} %add.38), channel_id=1, source_target_pairs={{0,8},{1,9},{2,10},{3,11},{4,12},{5,13},{6,14},{7,15},{8,16},{9,17... | collective-permute-start | bytes 98312 | tf_op jit(solution)/shard_map/ppermute | solution.py:339
  75.8 0.0 collective-permute-start.5
  75.9 1.8 %collective-permute-done.7 = f32[64,128]{1,0:T(8,128)S(1)} collective-permute-done((f32[64,128]{1,0:T(8,128)S(1)}, f32[64,128]{1,0:T(8,128)S(1)}, u32[]{:S(2)}, u32[]{:S(2)}) %collective-permute-start.7) | collective-permute-done | bytes 32800 | tf_op jit(solution)/shard_map/ppermute | solution.py:339
  77.7 1.3 %collective-permute-done.6 = f32[64,128]{1,0:T(8,128)S(1)} collective-permute-done((f32[64,128]{1,0:T(8,128)S(1)}, f32[64,128]{1,0:T(8,128)S(1)}, u32[]{:S(2)}, u32[]{:S(2)}) %collective-permute-start.6) | collective-permute-done | bytes 32800 | tf_op jit(solution)/shard_map/ppermute | solution.py:339
  79.0 2.2 %collective-permute-done.5 = f32[64,128]{1,0:T(8,128)S(1)} collective-permute-done((f32[64,128]{1,0:T(8,128)S(1)}, f32[64,128]{1,0:T(8,128)S(1)}, u32[]{:S(2)}, u32[]{:S(2)}) %collective-permute-start.5) | collective-permute-done | bytes 32800 | tf_op jit(solution)/shard_map/ppermute | solution.py:339
  81.3 0.1 fusion.14
  81.3 0.6 pad_maximum_fusion.2
  (15 shorter events, 0.1 us)
Async XLA Ops:
  4.3 14.7 %copy-start = (s32[16,512]{1,0:T(8,128)S(1)}, s32[16,512]{1,0:T(8,128)}, u32[]{:S(2)}) copy-start(s32[16,512]{1,0:T(8,128)} %param.5) | copy-start | bytes 98308
  4.3 44.9 %all-to-all-start = ((f32[256,8,128]{2,1,0:T(8,128)}), f32[256,8,128]{2,1,0:T(8,128)S(1)}, u32[]{:S(2)}, u32[]{:S(2)}) async-start(f32[256,8,128]{2,1,0:T(8,128)} %bitcast.18), calls=%async_computation | async-start | bytes 2097152 | tf_op jit(solution)/shard_map/all_to_all | solution.py:319
  49.3 12.6 %collective-permute-start = (f32[66,8,128]{2,1,0:T(8,128)S(1)}, f32[66,8,128]{2,1,0:T(8,128)S(1)}, u32[]{:S(2)}, u32[]{:S(2)}) collective-permute-start(f32[66,8,128]{2,1,0:T(8,128)S(1)} %pad_maximum_fusion), channel_id=1, source_target_pairs={{0,1},{1,2},{2,3},{3,4},{4,5},{5,6},{6,7},{7,8},{8,9},{9,10},{10,1... | collective-permute-start | bytes 811016 | tf_op jit(solution)/shard_map/ppermute | solution.py:334
  50.8 11.1 %collective-permute-start.1 = (f32[66,8,128]{2,1,0:T(8,128)S(1)}, f32[66,8,128]{2,1,0:T(8,128)S(1)}, u32[]{:S(2)}, u32[]{:S(2)}) collective-permute-start(f32[66,8,128]{2,1,0:T(8,128)S(1)} %pad_maximum_fusion.1), channel_id=1, source_target_pairs={{1,0},{2,1},{3,2},{4,3},{5,4},{6,5},{7,6},{8,7},{9,8},{10,9},{11,1... | collective-permute-start | bytes 811016 | tf_op jit(solution)/shard_map/ppermute | solution.py:335
  63.8 1.3 %collective-permute-start.2 = (f32[64,128]{1,0:T(8,128)S(1)}, f32[64,128]{1,0:T(8,128)S(1)}, u32[]{:S(2)}, u32[]{:S(2)}) collective-permute-start(f32[64,128]{1,0:T(8,128)S(1)} %outer_moments.1), channel_id=1, source_target_pairs={{0,1},{1,0},{2,3},{3,2},{4,5},{5,4},{6,7},{7,6},{8,9},{9,8},{10,11... | collective-permute-start | bytes 98312 | tf_op jit(solution)/shard_map/ppermute | solution.py:339
  65.1 3.9 %collective-permute-start.3 = (f32[64,128]{1,0:T(8,128)S(1)}, f32[64,128]{1,0:T(8,128)S(1)}, u32[]{:S(2)}, u32[]{:S(2)}) collective-permute-start(f32[64,128]{1,0:T(8,128)S(1)} %add.36), channel_id=1, source_target_pairs={{0,2},{1,3},{2,0},{3,1},{4,6},{5,7},{6,4},{7,5},{8,10},{9,11},{10,... | collective-permute-start | bytes 98312 | tf_op jit(solution)/shard_map/ppermute | solution.py:339
  69.0 4.8 %collective-permute-start.4 = (f32[64,128]{1,0:T(8,128)S(1)}, f32[64,128]{1,0:T(8,128)S(1)}, u32[]{:S(2)}, u32[]{:S(2)}) collective-permute-start(f32[64,128]{1,0:T(8,128)S(1)} %add.37), channel_id=1, source_target_pairs={{0,4},{1,5},{2,6},{3,7},{4,0},{5,1},{6,2},{7,3},{8,12},{9,13},{10,... | collective-permute-start | bytes 98312 | tf_op jit(solution)/shard_map/ppermute | solution.py:339
  73.8 3.9 %collective-permute-start.7 = (f32[64,128]{1,0:T(8,128)S(1)}, f32[64,128]{1,0:T(8,128)S(1)}, u32[]{:S(2)}, u32[]{:S(2)}) collective-permute-start(f32[64,128]{1,0:T(8,128)S(1)} %add.38), channel_id=1, source_target_pairs={{0,24},{1,25},{2,26},{3,27},{4,28},{5,29},{6,30},{7,31},{8,0},{9,1... | collective-permute-start | bytes 98312 | tf_op jit(solution)/shard_map/ppermute | solution.py:339
  73.8 5.2 %collective-permute-start.6 = (f32[64,128]{1,0:T(8,128)S(1)}, f32[64,128]{1,0:T(8,128)S(1)}, u32[]{:S(2)}, u32[]{:S(2)}) collective-permute-start(f32[64,128]{1,0:T(8,128)S(1)} %add.38), channel_id=1, source_target_pairs={{0,8},{1,9},{2,10},{3,11},{4,12},{5,13},{6,14},{7,15},{8,16},{9,17... | collective-permute-start | bytes 98312 | tf_op jit(solution)/shard_map/ppermute | solution.py:339
  75.8 5.4 %collective-permute-start.5 = (f32[64,128]{1,0:T(8,128)S(1)}, f32[64,128]{1,0:T(8,128)S(1)}, u32[]{:S(2)}, u32[]{:S(2)}) collective-permute-start(f32[64,128]{1,0:T(8,128)S(1)} %add.38), channel_id=1, source_target_pairs={{0,16},{1,17},{2,18},{3,19},{4,20},{5,21},{6,22},{7,23},{8,24},{9,... | collective-permute-start | bytes 98312 | tf_op jit(solution)/shard_map/ppermute | solution.py:339

commit v6 on v5

--- a/solution.py
+++ b/solution.py
@@ -1,3 +1,5 @@
+import functools
+
 import jax
 import jax.numpy as jnp
 from jax import lax
@@ -198,72 +200,72 @@
     sum_ref[...] = acc
 
 
-def outer_kernel(lo_ref, hi_ref, pres_ref, left_ref, sum_ref, edge_ref, out_ref, field, presb):
+def edge_kernel(across, core_ref, src_ref, pres_ref, left_ref, sum_ref, edge_ref, out_ref, field, presb):
     rows = left_ref.shape[0]
     wraps = wrap_masks()
     T = range(TILES)
     tail = HALO * 16
-    base = (-HALO, rows - 2 * HALO)
-
-    for i in range(HALO):
-        for side, src, j in ((0, lo_ref, i), (1, hi_ref, 2 * HALO + i)):
-            turned = turn_row(src, i * 16)
+
+    def side_sum(side):
+        base = (-HALO, rows - 2 * HALO)[side]
+        for i in range(HALO):
+            j = i if side == 0 else 2 * HALO + i
+            turned = turn_row(src_ref, i * 16)
             for t in T:
                 at = i * TILES + t
-                row = src[tail + at // SUB, pl.ds(at % SUB, 1), :]
+                row = src_ref[tail + at // SUB, pl.ds(at % SUB, 1), :]
                 mask = jnp.broadcast_to(row, (SUB, LANES))
-                presb[side, j, t] = mask
+                presb[j, t] = mask
                 for q in range(4):
                     at = (4 * t + q) * SUB
-                    field[0, side, j, q // 2, q % 2, t] = turned[at : at + SUB] * mask
-    for side in (0, 1):
-        for i in range(HALO):
-            j = HALO + i
+                    field[0, j, q // 2, q % 2, t] = turned[at : at + SUB] * mask
+        for j in range(HALO, 2 * HALO):
             for t in T:
-                row = pres_ref[base[side] + j, pl.ds(t, 1), :]
-                presb[side, j, t] = jnp.broadcast_to(row, (SUB, LANES))
-
-    def given(level, side):
-        first = HALO + level if side == 0 else 2 * HALO - 2 - level
-        return first, first + 1
-
-    def tile(level, side, j, r, half, t):
-        spots = given(level, side)
-        if j in spots:
-            return edge_ref[level, side, spots.index(j), r, half, t]
-        return field[level, side, j, r, half, t]
-
-    def load(level, side, j, half):
-        return [[tile(level, side, j, r, half, t) for t in T] for r in (0, 1)]
-
-    for level in range(MOM):
-        for side in (0, 1):
+                presb[j, t] = jnp.broadcast_to(pres_ref[base + j, pl.ds(t, 1), :], (SUB, LANES))
+
+        def tile(level, j, r, half, t):
+            first = HALO + level if side == 0 else 2 * HALO - 2 - level
+            if first <= j < first + 2:
+                return edge_ref[level, side, j - first, r, half, t]
+            return field[level, j, r, half, t]
+
+        def load(level, j, half):
+            return [[tile(level, j, r, half, t) for t in T] for r in (0, 1)]
+
+        for level in range(MOM):
             first = 1 + level if side == 0 else 2 * HALO - 1 - level
             for half in (0, 1):
-                window = [load(level, side, first + k, half) for k in range(-1, 5)]
+                window = [load(level, first + k, half) for k in range(-1, 5)]
                 for k in range(4):
                     j = first + k
-                    mask = scaled(level, [presb[side, j, t] for t in T])
-                    old = load(level - 1, side, j, half) if level > 1 else None
+                    mask = scaled(level, [presb[j, t] for t in T])
+                    old = load(level - 1, j, half) if level > 1 else None
                     values = stencil_row(level, j % 2, *window[k : k + 3], old, mask, wraps)
                     for r in (0, 1):
                         for t in T:
-                            field[(level + 1) % MOM, side, j, r, half, t] = values[r][t]
-
-    acc = sum_ref[...]
-    for y in [*range(HALO), *range(rows - HALO, rows)]:
-        side = 0 if y < HALO else 1
-
-        def blocks(r, m, half, t, y=y, side=side):
-            if m < y < rows - 1 - m:
-                return None
-            return field[(m + 1) % MOM, side, y - base[side], r, half, t]
-
-        acc = product(acc, blocks, left_ref, y)
-    half_rows = MOM * 2 * SUB
-    top, bottom = acc[:half_rows], acc[half_rows:]
-    lane_out = lax.broadcasted_iota(jnp.int32, top.shape, 1)
-    out_ref[...] = pltpu.roll(bottom, LANES // 2, 1) + jnp.where(lane_out < LANES // 2, top, -top)
+                            field[(level + 1) % MOM, j, r, half, t] = values[r][t]
+
+        acc = sum_ref[...]
+        for y in range(HALO) if side == 0 else range(rows - HALO, rows):
+
+            def blocks(r, m, half, t, y=y):
+                if m < y < rows - 1 - m:
+                    return None
+                return field[(m + 1) % MOM, y - base, r, half, t]
+
+            acc = product(acc, blocks, left_ref, y)
+        if across:
+            half_rows = MOM * 2 * SUB
+            top, bottom = acc[:half_rows], acc[half_rows:]
+            lane_out = lax.broadcasted_iota(jnp.int32, top.shape, 1)
+            acc = pltpu.roll(bottom, LANES // 2, 1) + jnp.where(lane_out < LANES // 2, top, -top)
+        out_ref[...] = acc
+
+    for core in (0, 1):
+
+        @pl.when(core_ref[0] == core)
+        def _(side=core if across else 1 - core):
+            side_sum(side)
 
 
 ROW = (2, 2, TILES, SUB, LANES)
@@ -290,28 +292,27 @@
     )(recv, pres, left)
 
 
-def outer_moments(lo, hi, pres, left, inner_sum, edges):
+def edge_moments(across, core, src, pres, left, total, edges):
     n2 = left.shape[1]
     vm = pl.BlockSpec(memory_space=pltpu.VMEM)
     return pl.pallas_call(
-        outer_kernel,
-        in_specs=[vm] * 6,
+        functools.partial(edge_kernel, across),
+        in_specs=[pl.BlockSpec(memory_space=pltpu.SMEM)] + [vm] * 5,
         out_specs=vm,
-        out_shape=jax.ShapeDtypeStruct((MOM * 2 * SUB, n2), F32),
+        out_shape=jax.ShapeDtypeStruct(((1 if across else 2) * MOM * 2 * SUB, n2), F32),
         scratch_shapes=[
-            pltpu.VMEM((MOM, 2, 3 * HALO, *ROW), F32),
-            pltpu.VMEM((2, 3 * HALO, TILES, SUB, LANES), F32),
+            pltpu.VMEM((MOM, 3 * HALO, *ROW), F32),
+            pltpu.VMEM((3 * HALO, TILES, SUB, LANES), F32),
         ],
         compiler_params=pltpu.CompilerParams(vmem_limit_bytes=40 * 2**20),
-        name="outer_moments",
-    )(lo, hi, pres, left, inner_sum, edges)
+        cost_estimate=pl.CostEstimate(flops=10**8, bytes_accessed=10**6, transcendentals=0),
+        name="edge_across" if across else "edge_sibling",
+    )(core, src, pres, left, total, edges)
 
 
 def per_device(right_vectors, left_vectors, vacancy):
     parts, width_group, groups, slabs, _, piece = right_vectors.shape
     count = lax.axis_size("sites")
-    up = [(i, (i + 1) % count) for i in range(count)]
-    down = [((i + 1) % count, i) for i in range(count)]
     n_left, rows, width = left_vectors.shape[1:]
 
     packed = pack(right_vectors.reshape(parts * width_group, groups, slabs, piece))
@@ -331,10 +332,18 @@
     edge = HALO * width // piece
     low_mask = present[:HALO].reshape(-1, SUB, LANES)
     high_mask = present[rows - HALO :].reshape(-1, SUB, LANES)
-    lo = lax.ppermute(jnp.concatenate([recv[recv.shape[0] - edge :], high_mask]), "sites", up)
-    hi = lax.ppermute(jnp.concatenate([recv[:edge], low_mask]), "sites", down)
-    inner_sum, edges = inner_moments(recv, present, left)
-    total = outer_moments(lo, hi, present, left, inner_sum, edges)
+    low = jnp.concatenate([recv[:edge], low_mask])
+    high = jnp.concatenate([recv[recv.shape[0] - edge :], high_mask])
+    core = lax.axis_index("sites") % 2
+    lower_slab = core == 0
+    to_chip = [(i, (i + 1 if i % 2 else i - 1) % count) for i in range(count)]
+    to_core = [(i, i ^ 1) for i in range(count)]
+    across = lax.ppermute(jnp.where(lower_slab, low, high), "sites", to_chip)
+    sibling = lax.ppermute(jnp.where(lower_slab, high, low), "sites", to_core)
+    core = core.astype(jnp.int32).reshape(1)
+    total, edges = inner_moments(recv, present, left)
+    total = edge_moments(False, core, sibling, present, left, total, edges)
+    total = edge_moments(True, core, across, present, left, total, edges)
     def moved(values, target):
         return lax.ppermute(values, "sites", [(i, target(i)) for i in range(count)])
 

time: 82.2 us -> 81 us (0.985)
  waiting for transfers between devices: 42.6 us -> 41.4 us
  starting transfers between devices: 22.6 us -> 21.7 us
    ppermute x2, starting transfers between devices: 5.81 us -> 3.52 us  [the longest x1 2.02 us: per_device(): across = lax.ppermute(jnp.where(lower_slab, low, high), 'sites', to_chip)]
    ppermute x6, starting transfers between devices: 2.15 us -> 3.54 us  [moved(): return lax.ppermute(values, 'sites', [(i, target(i)) for i in range(count)])]
    ppermute x6, waiting for transfers between devices: 15.3 us -> 13.9 us  [moved(): return lax.ppermute(values, 'sites', [(i, target(i)) for i in range(count)])]
    pallas_call x1 -> x2, Pallas kernels: 1.91 us -> 2.1 us  [edge_moments(): pl.pallas_call(functools.partial(edge_kernel, across), in_specs=[pl.Block...]
  transfers between devices with their start and end apart: 9 -> 9, of which waited for: 8 -> 8; matrix products, arithmetic and copies ran while one was open for 6% -> 6% of each run, Pallas kernels for 5% -> 7%
where the time goes in v6:
time: 81 us; the launch traced here: 80.1 us
  waiting for transfers between devices  41.4 us (51%)
  starting transfers between devices  21.7 us (27%)
  Pallas kernels  10.9 us (13%)
  matrix products  5.05 us (6%)
    all_to_all x1, waiting for transfers between devices, per_device(): recv = lax.all_to_all(packed, ('cols', 'sites'), 0, 0, tiled=True)  25.1 us
    all_to_all x1, starting transfers between devices, per_device(): recv = lax.all_to_all(packed, ('cols', 'sites'), 0, 0, tiled=True)  14.7 us
    ppermute x6, waiting for transfers between devices, moved(): return lax.ppermute(values, 'sites', [(i, target(i)) for i in range(count)])  13.9 us
    pallas_call x1, Pallas kernels, inner_moments(): pl.pallas_call(inner_kernel, in_specs=[vm] * 3, out_specs=[vm] * 2, out_s...  4.47 us
    dot_general x1, matrix products, per_device(): left = jnp.dot(left, to_place, preferred_element_type=jnp.bfloat16)  4.46 us
    pallas_call x1, Pallas kernels, pack(): pl.pallas_call(pack_kernel, grid=(groups // step,), in_specs=[pl.BlockSpe...  4.32 us
    ppermute x6, starting transfers between devices, moved(): return lax.ppermute(values, 'sites', [(i, target(i)) for i in range(count)])  3.54 us
    ppermute x1, waiting for transfers between devices, per_device(): across = lax.ppermute(jnp.where(lower_slab, low, high), 'sites', to_chip)  2.46 us
  transfers between devices with their start and end apart: 9, of which 8 were waited for; matrix products, arithmetic and copies ran while one was open for 6% of the time, Pallas kernels for 7%

profile of v6, /device:TPU:2, one launch (start us, length us, event | category | flops | bytes accessed | tf_op | source)
XLA Modules:
  0.0 80.1 jit_solution(5424927434550543891)
XLA Ops:
  0.0 4.3 %pack.1 = f32[8,32,8,128]{3,2,1,0:T(8,128)} custom-call(f32[32,8,32,32]{3,2,1,0:T(8,128)} %bitcast.18), custom_call_target="tpu_custom_call" | custom-call | tf_op jit(solution)/shard_map/pack/pallas_call | solution.py:60
  4.3 14.7 %all-to-all-start = ((f32[256,8,128]{2,1,0:T(8,128)}), f32[256,8,128]{2,1,0:T(8,128)S(1)}, u32[]{:S(2)}, u32[]{:S(2)}) async-start(f32[256,8,128]{2,1,0:T(8,128)} %bitcast.19), calls=%async_computation | async-start | bytes 2097152 | tf_op jit(solution)/shard_map/all_to_all | solution.py:320
  19.1 0.6 convolution_bitcast_fusion
  19.7 4.5 %fusion.2.left_ref = bf16[16,128,512]{2,1,0:T(8,128)(2,1)S(1)} fusion(bf16[128,16,512]{2,1,0:T(8,128)(2,1)} %bitcast.24, s32[512]{0:T(512)S(1)} %get-tuple-element.27, s32[512]{0:T(512)S(1)} %get-tuple-element.30, s32[512]{0:T(512)S(1)} %get-tuple-element.28, s32[512]{0:T(512)S(1)} %get-tuple-element.29, pred[512]{0:T(512)(128)(4,1)S(1)} %get-tuple-element.31, ...), kind=kOutput, calls=%fused_computation.2 | convolution fusion | flops 1075052544 | bytes 4203520 | tf_op jit(solution)/shard_map/dot_general | solution.py:326
  24.2 25.1 %all-to-all-done.recv_ref = f32[256,8,128]{2,1,0:T(8,128)S(1)} async-done(((f32[256,8,128]{2,1,0:T(8,128)}), f32[256,8,128]{2,1,0:T(8,128)S(1)}, u32[]{:S(2)}, u32[]{:S(2)}) %all-to-all-start) | async-done | bytes 1048608 | tf_op jit(solution)/shard_map/all_to_all | solution.py:320
  49.3 1.5 %collective-permute-start.1 = (f32[66,8,128]{2,1,0:T(8,128)S(1)}, f32[66,8,128]{2,1,0:T(8,128)S(1)}, u32[]{:S(2)}, u32[]{:S(2)}) collective-permute-start(f32[66,8,128]{2,1,0:T(8,128)S(1)} %get-tuple-element.21), channel_id=1, source_target_pairs={{0,1},{1,0},{2,3},{3,2},{4,5},{5,4},{6,7},{7,6},{8,9},{9,8},{10,11... | collective-permute-start | bytes 811016 | tf_op jit(solution)/shard_map/ppermute | solution.py:342
  50.8 2.0 %collective-permute-start = (f32[66,8,128]{2,1,0:T(8,128)S(1)}, f32[66,8,128]{2,1,0:T(8,128)S(1)}, u32[]{:S(2)}, u32[]{:S(2)}) collective-permute-start(f32[66,8,128]{2,1,0:T(8,128)S(1)} %get-tuple-element.22), channel_id=1, source_target_pairs={{0,31},{1,2},{2,1},{3,4},{4,3},{5,6},{6,5},{7,8},{8,7},{9,10},{10,... | collective-permute-start | bytes 811016 | tf_op jit(solution)/shard_map/ppermute | solution.py:341
  52.8 4.5 %inner_moments.1 = (f32[128,128]{1,0:T(8,128)S(1)}, f32[4,2,2,2,2,4,8,128]{7,6,5,4,3,2,1,0:T(8,128)S(1)}) custom-call(f32[256,8,128]{2,1,0:T(8,128)S(1)} %all-to-all-done.recv_ref, f32[16,4,128]{2,1,0:T(4,128)S(1)} %reshape.30.pres_ref, bf16[16,128,512]{2,1,0:T(8,128)(2,1)S(1)} %fusion.2.left_ref), custom_call_target="tpu_custom_call" | custom-call | flops 1000000000 | bytes 10000000 | tf_op jit(solution)/shard_map/inner_moments/pallas_call | solution.py:277
  57.3 1.1 %edge_sibling.1.sum_ref = f32[128,128]{1,0:T(8,128)S(1)} custom-call(s32[1]{0:T(128)} %bitcast.core_ref, f32[66,8,128]{2,1,0:T(8,128)S(1)} %collective-permute-done.1.src_ref, f32[16,4,128]{2,1,0:T(4,128)S(1)} %reshape.30.pres_ref, bf16[16,128,512]{2,1,0:T(8,128)(2,1)S(1)} %fusion.2.left_ref, f32[128,128]{1,0:T(8,128)S(1)} %get-tuple-element.17.sum_ref, ...), custom_call_target="tpu_custom_call" | custom-call | flops 100000000 | bytes 1000000 | tf_op jit(solution)/shard_map/edge_sibling/pallas_call | solution.py:298
  58.4 2.5 %collective-permute-done.src_ref = f32[66,8,128]{2,1,0:T(8,128)S(1)} collective-permute-done((f32[66,8,128]{2,1,0:T(8,128)S(1)}, f32[66,8,128]{2,1,0:T(8,128)S(1)}, u32[]{:S(2)}, u32[]{:S(2)}) %collective-permute-start) | collective-permute-done | bytes 270368 | tf_op jit(solution)/shard_map/ppermute | solution.py:341
  60.9 1.0 %edge_across.1 = f32[64,128]{1,0:T(8,128)S(1)} custom-call(s32[1]{0:T(128)} %bitcast.core_ref, f32[66,8,128]{2,1,0:T(8,128)S(1)} %collective-permute-done.src_ref, f32[16,4,128]{2,1,0:T(4,128)S(1)} %reshape.30.pres_ref, bf16[16,128,512]{2,1,0:T(8,128)(2,1)S(1)} %fusion.2.left_ref, f32[128,128]{1,0:T(8,128)S(1)} %edge_sibling.1.sum_ref, ...), custom_call_target="tpu_custom_call" | custom-call | flops 100000000 | bytes 1000000 | tf_op jit(solution)/shard_map/edge_across/pallas_call | solution.py:298
  61.9 0.1 collective-permute-start.2
  62.0 1.2 %collective-permute-done.2 = f32[64,128]{1,0:T(8,128)S(1)} collective-permute-done((f32[64,128]{1,0:T(8,128)S(1)}, f32[64,128]{1,0:T(8,128)S(1)}, u32[]{:S(2)}, u32[]{:S(2)}) %collective-permute-start.2) | collective-permute-done | bytes 32800 | tf_op jit(solution)/shard_map/ppermute | solution.py:348
  63.2 0.0 collective-permute-start.3
  63.2 3.9 %collective-permute-done.3 = f32[64,128]{1,0:T(8,128)S(1)} collective-permute-done((f32[64,128]{1,0:T(8,128)S(1)}, f32[64,128]{1,0:T(8,128)S(1)}, u32[]{:S(2)}, u32[]{:S(2)}) %collective-permute-start.3) | collective-permute-done | bytes 32800 | tf_op jit(solution)/shard_map/ppermute | solution.py:348
  67.1 4.8 %collective-permute-done.4 = f32[64,128]{1,0:T(8,128)S(1)} collective-permute-done((f32[64,128]{1,0:T(8,128)S(1)}, f32[64,128]{1,0:T(8,128)S(1)}, u32[]{:S(2)}, u32[]{:S(2)}) %collective-permute-start.4) | collective-permute-done | bytes 32800 | tf_op jit(solution)/shard_map/ppermute | solution.py:348
  71.9 0.1 collective-permute-start.7
  72.0 1.9 %collective-permute-start.6 = (f32[64,128]{1,0:T(8,128)S(1)}, f32[64,128]{1,0:T(8,128)S(1)}, u32[]{:S(2)}, u32[]{:S(2)}) collective-permute-start(f32[64,128]{1,0:T(8,128)S(1)} %add.43), channel_id=1, source_target_pairs={{0,8},{1,9},{2,10},{3,11},{4,12},{5,13},{6,14},{7,15},{8,16},{9,17... | collective-permute-start | bytes 98312 | tf_op jit(solution)/shard_map/ppermute | solution.py:348
  73.9 1.4 %collective-permute-start.5 = (f32[64,128]{1,0:T(8,128)S(1)}, f32[64,128]{1,0:T(8,128)S(1)}, u32[]{:S(2)}, u32[]{:S(2)}) collective-permute-start(f32[64,128]{1,0:T(8,128)S(1)} %add.43), channel_id=1, source_target_pairs={{0,16},{1,17},{2,18},{3,19},{4,20},{5,21},{6,22},{7,23},{8,24},{9,... | collective-permute-start | bytes 98312 | tf_op jit(solution)/shard_map/ppermute | solution.py:348
  75.4 0.5 collective-permute-done.7
  75.8 1.3 %collective-permute-done.6 = f32[64,128]{1,0:T(8,128)S(1)} collective-permute-done((f32[64,128]{1,0:T(8,128)S(1)}, f32[64,128]{1,0:T(8,128)S(1)}, u32[]{:S(2)}, u32[]{:S(2)}) %collective-permute-start.6) | collective-permute-done | bytes 32800 | tf_op jit(solution)/shard_map/ppermute | solution.py:348
  77.2 2.2 %collective-permute-done.5 = f32[64,128]{1,0:T(8,128)S(1)} collective-permute-done((f32[64,128]{1,0:T(8,128)S(1)}, f32[64,128]{1,0:T(8,128)S(1)}, u32[]{:S(2)}, u32[]{:S(2)}) %collective-permute-start.5) | collective-permute-done | bytes 32800 | tf_op jit(solution)/shard_map/ppermute | solution.py:348
  79.4 0.1 fusion.16
  79.4 0.6 pad_maximum_fusion.2
  (15 shorter events, 0.1 us)
Async XLA Ops:
  4.3 14.8 %copy-start = (s32[16,512]{1,0:T(8,128)S(1)}, s32[16,512]{1,0:T(8,128)}, u32[]{:S(2)}) copy-start(s32[16,512]{1,0:T(8,128)} %param.5) | copy-start | bytes 98308
  4.3 44.9 %all-to-all-start = ((f32[256,8,128]{2,1,0:T(8,128)}), f32[256,8,128]{2,1,0:T(8,128)S(1)}, u32[]{:S(2)}, u32[]{:S(2)}) async-start(f32[256,8,128]{2,1,0:T(8,128)} %bitcast.19), calls=%async_computation | async-start | bytes 2097152 | tf_op jit(solution)/shard_map/all_to_all | solution.py:320
  49.3 8.0 %collective-permute-start.1 = (f32[66,8,128]{2,1,0:T(8,128)S(1)}, f32[66,8,128]{2,1,0:T(8,128)S(1)}, u32[]{:S(2)}, u32[]{:S(2)}) collective-permute-start(f32[66,8,128]{2,1,0:T(8,128)S(1)} %get-tuple-element.21), channel_id=1, source_target_pairs={{0,1},{1,0},{2,3},{3,2},{4,5},{5,4},{6,7},{7,6},{8,9},{9,8},{10,11... | collective-permute-start | bytes 811016 | tf_op jit(solution)/shard_map/ppermute | solution.py:342
  50.8 10.0 %collective-permute-start = (f32[66,8,128]{2,1,0:T(8,128)S(1)}, f32[66,8,128]{2,1,0:T(8,128)S(1)}, u32[]{:S(2)}, u32[]{:S(2)}) collective-permute-start(f32[66,8,128]{2,1,0:T(8,128)S(1)} %get-tuple-element.22), channel_id=1, source_target_pairs={{0,31},{1,2},{2,1},{3,4},{4,3},{5,6},{6,5},{7,8},{8,7},{9,10},{10,... | collective-permute-start | bytes 811016 | tf_op jit(solution)/shard_map/ppermute | solution.py:341
  61.9 1.3 %collective-permute-start.2 = (f32[64,128]{1,0:T(8,128)S(1)}, f32[64,128]{1,0:T(8,128)S(1)}, u32[]{:S(2)}, u32[]{:S(2)}) collective-permute-start(f32[64,128]{1,0:T(8,128)S(1)} %edge_across.1), channel_id=1, source_target_pairs={{0,1},{1,0},{2,3},{3,2},{4,5},{5,4},{6,7},{7,6},{8,9},{9,8},{10,11... | collective-permute-start | bytes 98312 | tf_op jit(solution)/shard_map/ppermute | solution.py:348
  63.2 3.9 %collective-permute-start.3 = (f32[64,128]{1,0:T(8,128)S(1)}, f32[64,128]{1,0:T(8,128)S(1)}, u32[]{:S(2)}, u32[]{:S(2)}) collective-permute-start(f32[64,128]{1,0:T(8,128)S(1)} %add.41), channel_id=1, source_target_pairs={{0,2},{1,3},{2,0},{3,1},{4,6},{5,7},{6,4},{7,5},{8,10},{9,11},{10,... | collective-permute-start | bytes 98312 | tf_op jit(solution)/shard_map/ppermute | solution.py:348
  67.1 4.8 %collective-permute-start.4 = (f32[64,128]{1,0:T(8,128)S(1)}, f32[64,128]{1,0:T(8,128)S(1)}, u32[]{:S(2)}, u32[]{:S(2)}) collective-permute-start(f32[64,128]{1,0:T(8,128)S(1)} %add.42), channel_id=1, source_target_pairs={{0,4},{1,5},{2,6},{3,7},{4,0},{5,1},{6,2},{7,3},{8,12},{9,13},{10,... | collective-permute-start | bytes 98312 | tf_op jit(solution)/shard_map/ppermute | solution.py:348
  71.9 3.9 %collective-permute-start.7 = (f32[64,128]{1,0:T(8,128)S(1)}, f32[64,128]{1,0:T(8,128)S(1)}, u32[]{:S(2)}, u32[]{:S(2)}) collective-permute-start(f32[64,128]{1,0:T(8,128)S(1)} %add.43), channel_id=1, source_target_pairs={{0,24},{1,25},{2,26},{3,27},{4,28},{5,29},{6,30},{7,31},{8,0},{9,1... | collective-permute-start | bytes 98312 | tf_op jit(solution)/shard_map/ppermute | solution.py:348
  72.0 5.1 %collective-permute-start.6 = (f32[64,128]{1,0:T(8,128)S(1)}, f32[64,128]{1,0:T(8,128)S(1)}, u32[]{:S(2)}, u32[]{:S(2)}) collective-permute-start(f32[64,128]{1,0:T(8,128)S(1)} %add.43), channel_id=1, source_target_pairs={{0,8},{1,9},{2,10},{3,11},{4,12},{5,13},{6,14},{7,15},{8,16},{9,17... | collective-permute-start | bytes 98312 | tf_op jit(solution)/shard_map/ppermute | solution.py:348
  73.9 5.4 %collective-permute-start.5 = (f32[64,128]{1,0:T(8,128)S(1)}, f32[64,128]{1,0:T(8,128)S(1)}, u32[]{:S(2)}, u32[]{:S(2)}) collective-permute-start(f32[64,128]{1,0:T(8,128)S(1)} %add.43), channel_id=1, source_target_pairs={{0,16},{1,17},{2,18},{3,19},{4,20},{5,21},{6,22},{7,23},{8,24},{9,... | collective-permute-start | bytes 98312 | tf_op jit(solution)/shard_map/ppermute | solution.py:348

commit v7 on v6

--- a/solution.py
+++ b/solution.py
@@ -310,6 +310,26 @@
     )(core, src, pres, left, total, edges)
 
 
+def last_sum_kernel(mine_ref, far_ref, one_ref, other_ref, out_ref):
+    total = (mine_ref[...] + far_ref[...]) + (one_ref[...] + other_ref[...])
+    half = out_ref.shape[2]
+    out_ref[0] = total[:, :half]
+    out_ref[1] = total[:, half:]
+
+
+def last_sum(mine, far, one, other):
+    rows, width = mine.shape
+    vm = pl.BlockSpec(memory_space=pltpu.VMEM)
+    return pl.pallas_call(
+        last_sum_kernel,
+        in_specs=[vm] * 4,
+        out_specs=vm,
+        out_shape=jax.ShapeDtypeStruct((2, rows, width // 2), F32),
+        compiler_params=pltpu.CompilerParams(vmem_limit_bytes=8 * 2**20),
+        name="last_sum",
+    )(mine, far, one, other)
+
+
 def per_device(right_vectors, left_vectors, vacancy):
     parts, width_group, groups, slabs, _, piece = right_vectors.shape
     count = lax.axis_size("sites")
@@ -350,8 +370,7 @@
     for flip in (1, 2, 4):
         total = total + moved(total, lambda i: i ^ flip)
     far, one, other = [moved(total, lambda i: (i + 8 * k) % count) for k in (2, 1, 3)]
-    total = (total + far) + (one + other)
-    out = jnp.stack([total[:, :n_left], total[:, n_left:]]).reshape(2, MOM, width_group, n_left)
+    out = last_sum(total, far, one, other).reshape(2, MOM, width_group, n_left)
     return jnp.swapaxes(out, 2, 3)[..., None]
 
 

time: 81 us -> 81 us (level)
  no operation moved by 1% of the time
where the time goes in v7:
time: 81 us; the launch traced here: 80.1 us
  waiting for transfers between devices  41.4 us (51%)
  starting transfers between devices  21.8 us (27%)
  Pallas kernels  11.6 us (14%)
  matrix products  5.05 us (6%)
    all_to_all x1, waiting for transfers between devices, per_device(): recv = lax.all_to_all(packed, ('cols', 'sites'), 0, 0, tiled=True)  25.1 us
    all_to_all x1, starting transfers between devices, per_device(): recv = lax.all_to_all(packed, ('cols', 'sites'), 0, 0, tiled=True)  14.7 us
    ppermute x6, waiting for transfers between devices, moved(): return lax.ppermute(values, 'sites', [(i, target(i)) for i in range(count)])  13.9 us
    pallas_call x1, Pallas kernels, inner_moments(): pl.pallas_call(inner_kernel, in_specs=[vm] * 3, out_specs=[vm] * 2, out_s...  4.47 us
    dot_general x1, matrix products, per_device(): left = jnp.dot(left, to_place, preferred_element_type=jnp.bfloat16)  4.46 us
    pallas_call x1, Pallas kernels, pack(): pl.pallas_call(pack_kernel, grid=(groups // step,), in_specs=[pl.BlockSpe...  4.33 us
    ppermute x6, starting transfers between devices, moved(): return lax.ppermute(values, 'sites', [(i, target(i)) for i in range(count)])  3.55 us
    ppermute x1, waiting for transfers between devices, per_device(): across = lax.ppermute(jnp.where(lower_slab, low, high), 'sites', to_chip)  2.46 us
  transfers between devices with their start and end apart: 9, of which 8 were waited for; matrix products, arithmetic and copies ran while one was open for 6% of the time, Pallas kernels for 7%

profile of v7, /device:TPU:2, one launch (start us, length us, event | category | flops | bytes accessed | tf_op | source)
XLA Modules:
  0.0 80.1 jit_solution(15481665670789758475)
XLA Ops:
  0.0 4.3 %pack.1 = f32[8,32,8,128]{3,2,1,0:T(8,128)} custom-call(f32[32,8,32,32]{3,2,1,0:T(8,128)} %bitcast.18), custom_call_target="tpu_custom_call" | custom-call | tf_op jit(solution)/shard_map/pack/pallas_call | solution.py:60
  4.3 14.7 %all-to-all-start = ((f32[256,8,128]{2,1,0:T(8,128)}), f32[256,8,128]{2,1,0:T(8,128)S(1)}, u32[]{:S(2)}, u32[]{:S(2)}) async-start(f32[256,8,128]{2,1,0:T(8,128)} %bitcast.19), calls=%async_computation | async-start | bytes 2097152 | tf_op jit(solution)/shard_map/all_to_all | solution.py:340
  19.1 0.6 convolution_bitcast_fusion
  19.7 4.5 %fusion.2.left_ref = bf16[16,128,512]{2,1,0:T(8,128)(2,1)S(1)} fusion(bf16[128,16,512]{2,1,0:T(8,128)(2,1)} %bitcast.22, s32[512]{0:T(512)S(1)} %get-tuple-element.25, s32[512]{0:T(512)S(1)} %get-tuple-element.28, s32[512]{0:T(512)S(1)} %get-tuple-element.26, s32[512]{0:T(512)S(1)} %get-tuple-element.27, pred[512]{0:T(512)(128)(4,1)S(1)} %get-tuple-element.29, ...), kind=kOutput, calls=%fused_computation.2 | convolution fusion | flops 1075052544 | bytes 4203520 | tf_op jit(solution)/shard_map/dot_general | solution.py:346
  24.2 25.1 %all-to-all-done.recv_ref = f32[256,8,128]{2,1,0:T(8,128)S(1)} async-done(((f32[256,8,128]{2,1,0:T(8,128)}), f32[256,8,128]{2,1,0:T(8,128)S(1)}, u32[]{:S(2)}, u32[]{:S(2)}) %all-to-all-start) | async-done | bytes 1048608 | tf_op jit(solution)/shard_map/all_to_all | solution.py:340
  49.3 1.5 %collective-permute-start.1 = (f32[66,8,128]{2,1,0:T(8,128)S(1)}, f32[66,8,128]{2,1,0:T(8,128)S(1)}, u32[]{:S(2)}, u32[]{:S(2)}) collective-permute-start(f32[66,8,128]{2,1,0:T(8,128)S(1)} %get-tuple-element.21), channel_id=1, source_target_pairs={{0,1},{1,0},{2,3},{3,2},{4,5},{5,4},{6,7},{7,6},{8,9},{9,8},{10,11... | collective-permute-start | bytes 811016 | tf_op jit(solution)/shard_map/ppermute | solution.py:362
  50.8 2.0 %collective-permute-start = (f32[66,8,128]{2,1,0:T(8,128)S(1)}, f32[66,8,128]{2,1,0:T(8,128)S(1)}, u32[]{:S(2)}, u32[]{:S(2)}) collective-permute-start(f32[66,8,128]{2,1,0:T(8,128)S(1)} %get-tuple-element.22), channel_id=1, source_target_pairs={{0,31},{1,2},{2,1},{3,4},{4,3},{5,6},{6,5},{7,8},{8,7},{9,10},{10,... | collective-permute-start | bytes 811016 | tf_op jit(solution)/shard_map/ppermute | solution.py:361
  52.8 4.5 %inner_moments.1 = (f32[128,128]{1,0:T(8,128)S(1)}, f32[4,2,2,2,2,4,8,128]{7,6,5,4,3,2,1,0:T(8,128)S(1)}) custom-call(f32[256,8,128]{2,1,0:T(8,128)S(1)} %all-to-all-done.recv_ref, f32[16,4,128]{2,1,0:T(4,128)S(1)} %reshape.28.pres_ref, bf16[16,128,512]{2,1,0:T(8,128)(2,1)S(1)} %fusion.2.left_ref), custom_call_target="tpu_custom_call" | custom-call | flops 1000000000 | bytes 10000000 | tf_op jit(solution)/shard_map/inner_moments/pallas_call | solution.py:277
  57.3 0.0 collective-permute-done.1.src_ref
  57.3 1.1 %edge_sibling.1.sum_ref = f32[128,128]{1,0:T(8,128)S(1)} custom-call(s32[1]{0:T(128)} %bitcast.core_ref, f32[66,8,128]{2,1,0:T(8,128)S(1)} %collective-permute-done.1.src_ref, f32[16,4,128]{2,1,0:T(4,128)S(1)} %reshape.28.pres_ref, bf16[16,128,512]{2,1,0:T(8,128)(2,1)S(1)} %fusion.2.left_ref, f32[128,128]{1,0:T(8,128)S(1)} %get-tuple-element.17.sum_ref, ...), custom_call_target="tpu_custom_call" | custom-call | flops 100000000 | bytes 1000000 | tf_op jit(solution)/shard_map/edge_sibling/pallas_call | solution.py:298
  58.4 2.5 %collective-permute-done.src_ref = f32[66,8,128]{2,1,0:T(8,128)S(1)} collective-permute-done((f32[66,8,128]{2,1,0:T(8,128)S(1)}, f32[66,8,128]{2,1,0:T(8,128)S(1)}, u32[]{:S(2)}, u32[]{:S(2)}) %collective-permute-start) | collective-permute-done | bytes 270368 | tf_op jit(solution)/shard_map/ppermute | solution.py:361
  60.9 1.0 %edge_across.1 = f32[64,128]{1,0:T(8,128)S(1)} custom-call(s32[1]{0:T(128)} %bitcast.core_ref, f32[66,8,128]{2,1,0:T(8,128)S(1)} %collective-permute-done.src_ref, f32[16,4,128]{2,1,0:T(4,128)S(1)} %reshape.28.pres_ref, bf16[16,128,512]{2,1,0:T(8,128)(2,1)S(1)} %fusion.2.left_ref, f32[128,128]{1,0:T(8,128)S(1)} %edge_sibling.1.sum_ref, ...), custom_call_target="tpu_custom_call" | custom-call | flops 100000000 | bytes 1000000 | tf_op jit(solution)/shard_map/edge_across/pallas_call | solution.py:298
  61.9 0.1 collective-permute-start.2
  62.0 1.2 %collective-permute-done.2 = f32[64,128]{1,0:T(8,128)S(1)} collective-permute-done((f32[64,128]{1,0:T(8,128)S(1)}, f32[64,128]{1,0:T(8,128)S(1)}, u32[]{:S(2)}, u32[]{:S(2)}) %collective-permute-start.2) | collective-permute-done | bytes 32800 | tf_op jit(solution)/shard_map/ppermute | solution.py:368
  63.2 3.9 %collective-permute-done.3 = f32[64,128]{1,0:T(8,128)S(1)} collective-permute-done((f32[64,128]{1,0:T(8,128)S(1)}, f32[64,128]{1,0:T(8,128)S(1)}, u32[]{:S(2)}, u32[]{:S(2)}) %collective-permute-start.3) | collective-permute-done | bytes 32800 | tf_op jit(solution)/shard_map/ppermute | solution.py:368
  67.1 0.0 collective-permute-start.4
  67.1 4.8 %collective-permute-done.4 = f32[64,128]{1,0:T(8,128)S(1)} collective-permute-done((f32[64,128]{1,0:T(8,128)S(1)}, f32[64,128]{1,0:T(8,128)S(1)}, u32[]{:S(2)}, u32[]{:S(2)}) %collective-permute-start.4) | collective-permute-done | bytes 32800 | tf_op jit(solution)/shard_map/ppermute | solution.py:368
  71.9 0.1 collective-permute-start.7
  72.1 1.9 %collective-permute-start.6 = (f32[64,128]{1,0:T(8,128)S(1)}, f32[64,128]{1,0:T(8,128)S(1)}, u32[]{:S(2)}, u32[]{:S(2)}) collective-permute-start(f32[64,128]{1,0:T(8,128)S(1)} %add.34.mine_ref), channel_id=1, source_target_pairs={{0,8},{1,9},{2,10},{3,11},{4,12},{5,13},{6,14},{7,15},{8,16},{9,17... | collective-permute-start | bytes 98312 | tf_op jit(solution)/shard_map/ppermute | solution.py:368
  73.9 1.4 %collective-permute-start.5 = (f32[64,128]{1,0:T(8,128)S(1)}, f32[64,128]{1,0:T(8,128)S(1)}, u32[]{:S(2)}, u32[]{:S(2)}) collective-permute-start(f32[64,128]{1,0:T(8,128)S(1)} %add.34.mine_ref), channel_id=1, source_target_pairs={{0,16},{1,17},{2,18},{3,19},{4,20},{5,21},{6,22},{7,23},{8,24},{9,... | collective-permute-start | bytes 98312 | tf_op jit(solution)/shard_map/ppermute | solution.py:368
  75.4 0.4 collective-permute-done.7.other_ref
  75.8 1.3 %collective-permute-done.6.one_ref = f32[64,128]{1,0:T(8,128)S(1)} collective-permute-done((f32[64,128]{1,0:T(8,128)S(1)}, f32[64,128]{1,0:T(8,128)S(1)}, u32[]{:S(2)}, u32[]{:S(2)}) %collective-permute-start.6) | collective-permute-done | bytes 32800 | tf_op jit(solution)/shard_map/ppermute | solution.py:368
  77.2 2.2 %collective-permute-done.5.far_ref = f32[64,128]{1,0:T(8,128)S(1)} collective-permute-done((f32[64,128]{1,0:T(8,128)S(1)}, f32[64,128]{1,0:T(8,128)S(1)}, u32[]{:S(2)}, u32[]{:S(2)}) %collective-permute-start.5) | collective-permute-done | bytes 32800 | tf_op jit(solution)/shard_map/ppermute | solution.py:368
  79.4 0.7 last_sum.1
  (13 shorter events, 0.1 us)
Async XLA Ops:
  4.3 14.8 %copy-start = (s32[16,512]{1,0:T(8,128)S(1)}, s32[16,512]{1,0:T(8,128)}, u32[]{:S(2)}) copy-start(s32[16,512]{1,0:T(8,128)} %param.5) | copy-start | bytes 98308
  4.3 44.9 %all-to-all-start = ((f32[256,8,128]{2,1,0:T(8,128)}), f32[256,8,128]{2,1,0:T(8,128)S(1)}, u32[]{:S(2)}, u32[]{:S(2)}) async-start(f32[256,8,128]{2,1,0:T(8,128)} %bitcast.19), calls=%async_computation | async-start | bytes 2097152 | tf_op jit(solution)/shard_map/all_to_all | solution.py:340
  49.3 8.0 %collective-permute-start.1 = (f32[66,8,128]{2,1,0:T(8,128)S(1)}, f32[66,8,128]{2,1,0:T(8,128)S(1)}, u32[]{:S(2)}, u32[]{:S(2)}) collective-permute-start(f32[66,8,128]{2,1,0:T(8,128)S(1)} %get-tuple-element.21), channel_id=1, source_target_pairs={{0,1},{1,0},{2,3},{3,2},{4,5},{5,4},{6,7},{7,6},{8,9},{9,8},{10,11... | collective-permute-start | bytes 811016 | tf_op jit(solution)/shard_map/ppermute | solution.py:362
  50.8 10.0 %collective-permute-start = (f32[66,8,128]{2,1,0:T(8,128)S(1)}, f32[66,8,128]{2,1,0:T(8,128)S(1)}, u32[]{:S(2)}, u32[]{:S(2)}) collective-permute-start(f32[66,8,128]{2,1,0:T(8,128)S(1)} %get-tuple-element.22), channel_id=1, source_target_pairs={{0,31},{1,2},{2,1},{3,4},{4,3},{5,6},{6,5},{7,8},{8,7},{9,10},{10,... | collective-permute-start | bytes 811016 | tf_op jit(solution)/shard_map/ppermute | solution.py:361
  61.9 1.3 %collective-permute-start.2 = (f32[64,128]{1,0:T(8,128)S(1)}, f32[64,128]{1,0:T(8,128)S(1)}, u32[]{:S(2)}, u32[]{:S(2)}) collective-permute-start(f32[64,128]{1,0:T(8,128)S(1)} %edge_across.1), channel_id=1, source_target_pairs={{0,1},{1,0},{2,3},{3,2},{4,5},{5,4},{6,7},{7,6},{8,9},{9,8},{10,11... | collective-permute-start | bytes 98312 | tf_op jit(solution)/shard_map/ppermute | solution.py:368
  63.2 3.9 %collective-permute-start.3 = (f32[64,128]{1,0:T(8,128)S(1)}, f32[64,128]{1,0:T(8,128)S(1)}, u32[]{:S(2)}, u32[]{:S(2)}) collective-permute-start(f32[64,128]{1,0:T(8,128)S(1)} %add.32), channel_id=1, source_target_pairs={{0,2},{1,3},{2,0},{3,1},{4,6},{5,7},{6,4},{7,5},{8,10},{9,11},{10,... | collective-permute-start | bytes 98312 | tf_op jit(solution)/shard_map/ppermute | solution.py:368
  67.1 4.8 %collective-permute-start.4 = (f32[64,128]{1,0:T(8,128)S(1)}, f32[64,128]{1,0:T(8,128)S(1)}, u32[]{:S(2)}, u32[]{:S(2)}) collective-permute-start(f32[64,128]{1,0:T(8,128)S(1)} %add.33), channel_id=1, source_target_pairs={{0,4},{1,5},{2,6},{3,7},{4,0},{5,1},{6,2},{7,3},{8,12},{9,13},{10,... | collective-permute-start | bytes 98312 | tf_op jit(solution)/shard_map/ppermute | solution.py:368
  71.9 3.9 %collective-permute-start.7 = (f32[64,128]{1,0:T(8,128)S(1)}, f32[64,128]{1,0:T(8,128)S(1)}, u32[]{:S(2)}, u32[]{:S(2)}) collective-permute-start(f32[64,128]{1,0:T(8,128)S(1)} %add.34.mine_ref), channel_id=1, source_target_pairs={{0,24},{1,25},{2,26},{3,27},{4,28},{5,29},{6,30},{7,31},{8,0},{9,1... | collective-permute-start | bytes 98312 | tf_op jit(solution)/shard_map/ppermute | solution.py:368
  72.1 5.1 %collective-permute-start.6 = (f32[64,128]{1,0:T(8,128)S(1)}, f32[64,128]{1,0:T(8,128)S(1)}, u32[]{:S(2)}, u32[]{:S(2)}) collective-permute-start(f32[64,128]{1,0:T(8,128)S(1)} %add.34.mine_ref), channel_id=1, source_target_pairs={{0,8},{1,9},{2,10},{3,11},{4,12},{5,13},{6,14},{7,15},{8,16},{9,17... | collective-permute-start | bytes 98312 | tf_op jit(solution)/shard_map/ppermute | solution.py:368
  73.9 5.4 %collective-permute-start.5 = (f32[64,128]{1,0:T(8,128)S(1)}, f32[64,128]{1,0:T(8,128)S(1)}, u32[]{:S(2)}, u32[]{:S(2)}) collective-permute-start(f32[64,128]{1,0:T(8,128)S(1)} %add.34.mine_ref), channel_id=1, source_target_pairs={{0,16},{1,17},{2,18},{3,19},{4,20},{5,21},{6,22},{7,23},{8,24},{9,... | collective-permute-start | bytes 98312 | tf_op jit(solution)/shard_map/ppermute | solution.py:368

commit v8 on v7

--- a/solution.py
+++ b/solution.py
@@ -364,13 +364,14 @@
     total, edges = inner_moments(recv, present, left)
     total = edge_moments(False, core, sibling, present, left, total, edges)
     total = edge_moments(True, core, across, present, left, total, edges)
-    def moved(values, target):
-        return lax.ppermute(values, "sites", [(i, target(i)) for i in range(count)])
-
-    for flip in (1, 2, 4):
-        total = total + moved(total, lambda i: i ^ flip)
-    far, one, other = [moved(total, lambda i: (i + 8 * k) % count) for k in (2, 1, 3)]
-    out = last_sum(total, far, one, other).reshape(2, MOM, width_group, n_left)
+    def moved(values, flip):
+        return lax.ppermute(values, "sites", [(i, i ^ flip) for i in range(count)])
+
+    total = total + moved(total, 1)
+    z_near, y_near, both = moved(total, 2), moved(total, 8), moved(total, 10)
+    total = (total + z_near) + (y_near + both)
+    z_far, y_far, both = moved(total, 4), moved(total, 24), moved(total, 28)
+    out = last_sum(total, z_far, y_far, both).reshape(2, MOM, width_group, n_left)
     return jnp.swapaxes(out, 2, 3)[..., None]
 
 

time: 81 us -> 79.3 us (0.979)
  waiting for transfers between devices: 41.4 us -> 33.9 us
  starting transfers between devices: 21.8 us -> 27.4 us
    ppermute x6 -> x7, waiting for transfers between devices: 13.9 us -> 6.39 us  [moved(): return lax.ppermute(values, 'sites', [(i, i ^ flip) for i in range(count)])]
    ppermute x6 -> x7, starting transfers between devices: 3.55 us -> 9.24 us  [moved(): return lax.ppermute(values, 'sites', [(i, i ^ flip) for i in range(count)])]
  transfers between devices with their start and end apart: 9 -> 10, of which waited for: 8 -> 7; matrix products, arithmetic and copies ran while one was open for 6% -> 6% of each run, Pallas kernels for 7% -> 7%
where the time goes in v8:
time: 79.3 us; the launch traced here: 78.3 us
  waiting for transfers between devices  33.9 us (43%)
  starting transfers between devices  27.4 us (35%)
  Pallas kernels  11.6 us (15%)
  matrix products  5.05 us (6%)
    all_to_all x1, waiting for transfers between devices, per_device(): recv = lax.all_to_all(packed, ('cols', 'sites'), 0, 0, tiled=True)  25.1 us
    all_to_all x1, starting transfers between devices, per_device(): recv = lax.all_to_all(packed, ('cols', 'sites'), 0, 0, tiled=True)  14.7 us
    ppermute x7, starting transfers between devices, moved(): return lax.ppermute(values, 'sites', [(i, i ^ flip) for i in range(count)])  9.24 us
    ppermute x7, waiting for transfers between devices, moved(): return lax.ppermute(values, 'sites', [(i, i ^ flip) for i in range(count)])  6.39 us
    pallas_call x1, Pallas kernels, inner_moments(): pl.pallas_call(inner_kernel, in_specs=[vm] * 3, out_specs=[vm] * 2, out_s...  4.47 us
    dot_general x1, matrix products, per_device(): left = jnp.dot(left, to_place, preferred_element_type=jnp.bfloat16)  4.46 us
    pallas_call x1, Pallas kernels, pack(): pl.pallas_call(pack_kernel, grid=(groups // step,), in_specs=[pl.BlockSpe...  4.32 us
    ppermute x1, waiting for transfers between devices, per_device(): across = lax.ppermute(jnp.where(lower_slab, low, high), 'sites', to_chip)  2.46 us
  transfers between devices with their start and end apart: 10, of which 7 were waited for; matrix products, arithmetic and copies ran while one was open for 6% of the time, Pallas kernels for 7%

profile of v8, /device:TPU:2, one launch (start us, length us, event | category | flops | bytes accessed | tf_op | source)
XLA Modules:
  0.0 78.3 jit_solution(5661553723429547999)
XLA Ops:
  0.0 4.3 %pack.1 = f32[8,32,8,128]{3,2,1,0:T(8,128)} custom-call(f32[32,8,32,32]{3,2,1,0:T(8,128)} %bitcast.18), custom_call_target="tpu_custom_call" | custom-call | tf_op jit(solution)/shard_map/pack/pallas_call | solution.py:60
  4.3 14.7 %all-to-all-start = ((f32[256,8,128]{2,1,0:T(8,128)}), f32[256,8,128]{2,1,0:T(8,128)S(1)}, u32[]{:S(2)}, u32[]{:S(2)}) async-start(f32[256,8,128]{2,1,0:T(8,128)} %bitcast.19), calls=%async_computation | async-start | bytes 2097152 | tf_op jit(solution)/shard_map/all_to_all | solution.py:340
  19.1 0.6 convolution_bitcast_fusion
  19.7 4.5 %fusion.2.left_ref = bf16[16,128,512]{2,1,0:T(8,128)(2,1)S(1)} fusion(bf16[128,16,512]{2,1,0:T(8,128)(2,1)} %bitcast.22, s32[512]{0:T(512)S(1)} %get-tuple-element.25, s32[512]{0:T(512)S(1)} %get-tuple-element.28, s32[512]{0:T(512)S(1)} %get-tuple-element.26, s32[512]{0:T(512)S(1)} %get-tuple-element.27, pred[512]{0:T(512)(128)(4,1)S(1)} %get-tuple-element.29, ...), kind=kOutput, calls=%fused_computation.2 | convolution fusion | flops 1075052544 | bytes 4203520 | tf_op jit(solution)/shard_map/dot_general | solution.py:346
  24.2 25.1 %all-to-all-done.recv_ref = f32[256,8,128]{2,1,0:T(8,128)S(1)} async-done(((f32[256,8,128]{2,1,0:T(8,128)}), f32[256,8,128]{2,1,0:T(8,128)S(1)}, u32[]{:S(2)}, u32[]{:S(2)}) %all-to-all-start) | async-done | bytes 1048608 | tf_op jit(solution)/shard_map/all_to_all | solution.py:340
  49.3 1.5 %collective-permute-start.1 = (f32[66,8,128]{2,1,0:T(8,128)S(1)}, f32[66,8,128]{2,1,0:T(8,128)S(1)}, u32[]{:S(2)}, u32[]{:S(2)}) collective-permute-start(f32[66,8,128]{2,1,0:T(8,128)S(1)} %get-tuple-element.21), channel_id=1, source_target_pairs={{0,1},{1,0},{2,3},{3,2},{4,5},{5,4},{6,7},{7,6},{8,9},{9,8},{10,11... | collective-permute-start | bytes 811016 | tf_op jit(solution)/shard_map/ppermute | solution.py:362
  50.8 2.0 %collective-permute-start = (f32[66,8,128]{2,1,0:T(8,128)S(1)}, f32[66,8,128]{2,1,0:T(8,128)S(1)}, u32[]{:S(2)}, u32[]{:S(2)}) collective-permute-start(f32[66,8,128]{2,1,0:T(8,128)S(1)} %get-tuple-element.22), channel_id=1, source_target_pairs={{0,31},{1,2},{2,1},{3,4},{4,3},{5,6},{6,5},{7,8},{8,7},{9,10},{10,... | collective-permute-start | bytes 811016 | tf_op jit(solution)/shard_map/ppermute | solution.py:361
  52.8 4.5 %inner_moments.1 = (f32[128,128]{1,0:T(8,128)S(1)}, f32[4,2,2,2,2,4,8,128]{7,6,5,4,3,2,1,0:T(8,128)S(1)}) custom-call(f32[256,8,128]{2,1,0:T(8,128)S(1)} %all-to-all-done.recv_ref, f32[16,4,128]{2,1,0:T(4,128)S(1)} %reshape.28.pres_ref, bf16[16,128,512]{2,1,0:T(8,128)(2,1)S(1)} %fusion.2.left_ref), custom_call_target="tpu_custom_call" | custom-call | flops 1000000000 | bytes 10000000 | tf_op jit(solution)/shard_map/inner_moments/pallas_call | solution.py:277
  57.3 1.1 %edge_sibling.1.sum_ref = f32[128,128]{1,0:T(8,128)S(1)} custom-call(s32[1]{0:T(128)} %bitcast.core_ref, f32[66,8,128]{2,1,0:T(8,128)S(1)} %collective-permute-done.1.src_ref, f32[16,4,128]{2,1,0:T(4,128)S(1)} %reshape.28.pres_ref, bf16[16,128,512]{2,1,0:T(8,128)(2,1)S(1)} %fusion.2.left_ref, f32[128,128]{1,0:T(8,128)S(1)} %get-tuple-element.17.sum_ref, ...), custom_call_target="tpu_custom_call" | custom-call | flops 100000000 | bytes 1000000 | tf_op jit(solution)/shard_map/edge_sibling/pallas_call | solution.py:298
  58.4 2.5 %collective-permute-done.src_ref = f32[66,8,128]{2,1,0:T(8,128)S(1)} collective-permute-done((f32[66,8,128]{2,1,0:T(8,128)S(1)}, f32[66,8,128]{2,1,0:T(8,128)S(1)}, u32[]{:S(2)}, u32[]{:S(2)}) %collective-permute-start) | collective-permute-done | bytes 270368 | tf_op jit(solution)/shard_map/ppermute | solution.py:361
  60.9 1.0 %edge_across.1 = f32[64,128]{1,0:T(8,128)S(1)} custom-call(s32[1]{0:T(128)} %bitcast.core_ref, f32[66,8,128]{2,1,0:T(8,128)S(1)} %collective-permute-done.src_ref, f32[16,4,128]{2,1,0:T(4,128)S(1)} %reshape.28.pres_ref, bf16[16,128,512]{2,1,0:T(8,128)(2,1)S(1)} %fusion.2.left_ref, f32[128,128]{1,0:T(8,128)S(1)} %edge_sibling.1.sum_ref, ...), custom_call_target="tpu_custom_call" | custom-call | flops 100000000 | bytes 1000000 | tf_op jit(solution)/shard_map/edge_across/pallas_call | solution.py:298
  61.9 0.1 collective-permute-start.2
  62.0 1.2 %collective-permute-done.2 = f32[64,128]{1,0:T(8,128)S(1)} collective-permute-done((f32[64,128]{1,0:T(8,128)S(1)}, f32[64,128]{1,0:T(8,128)S(1)}, u32[]{:S(2)}, u32[]{:S(2)}) %collective-permute-start.2) | collective-permute-done | bytes 32800 | tf_op jit(solution)/shard_map/ppermute | solution.py:368
  63.2 0.0 collective-permute-start.5
  63.2 1.7 %collective-permute-start.4 = (f32[64,128]{1,0:T(8,128)S(1)}, f32[64,128]{1,0:T(8,128)S(1)}, u32[]{:S(2)}, u32[]{:S(2)}) collective-permute-start(f32[64,128]{1,0:T(8,128)S(1)} %add.35), channel_id=1, source_target_pairs={{0,8},{1,9},{2,10},{3,11},{4,12},{5,13},{6,14},{7,15},{8,0},{9,1},... | collective-permute-start | bytes 98312 | tf_op jit(solution)/shard_map/ppermute | solution.py:368
  64.8 1.8 %collective-permute-start.3 = (f32[64,128]{1,0:T(8,128)S(1)}, f32[64,128]{1,0:T(8,128)S(1)}, u32[]{:S(2)}, u32[]{:S(2)}) collective-permute-start(f32[64,128]{1,0:T(8,128)S(1)} %add.35), channel_id=1, source_target_pairs={{0,2},{1,3},{2,0},{3,1},{4,6},{5,7},{6,4},{7,5},{8,10},{9,11},{10,... | collective-permute-start | bytes 98312 | tf_op jit(solution)/shard_map/ppermute | solution.py:368
  66.7 1.4 %collective-permute-done.5 = f32[64,128]{1,0:T(8,128)S(1)} collective-permute-done((f32[64,128]{1,0:T(8,128)S(1)}, f32[64,128]{1,0:T(8,128)S(1)}, u32[]{:S(2)}, u32[]{:S(2)}) %collective-permute-start.5) | collective-permute-done | bytes 32800 | tf_op jit(solution)/shard_map/ppermute | solution.py:368
  68.0 0.0 collective-permute-done.4
  68.0 0.7 collective-permute-done.3
  68.8 3.7 %collective-permute-start.8 = (f32[64,128]{1,0:T(8,128)S(1)}, f32[64,128]{1,0:T(8,128)S(1)}, u32[]{:S(2)}, u32[]{:S(2)}) collective-permute-start(f32[64,128]{1,0:T(8,128)S(1)} %add_add_fusion.mine_ref), channel_id=1, source_target_pairs={{0,28},{1,29},{2,30},{3,31},{4,24},{5,25},{6,26},{7,27},{8,20},{9,... | collective-permute-start | bytes 98312 | tf_op jit(solution)/shard_map/ppermute | solution.py:368
  72.4 2.0 %collective-permute-start.6 = (f32[64,128]{1,0:T(8,128)S(1)}, f32[64,128]{1,0:T(8,128)S(1)}, u32[]{:S(2)}, u32[]{:S(2)}) collective-permute-start(f32[64,128]{1,0:T(8,128)S(1)} %add_add_fusion.mine_ref), channel_id=1, source_target_pairs={{0,4},{1,5},{2,6},{3,7},{4,0},{5,1},{6,2},{7,3},{8,12},{9,13},{10,... | collective-permute-start | bytes 98312 | tf_op jit(solution)/shard_map/ppermute | solution.py:368
  74.5 1.3 %collective-permute-done.8.other_ref = f32[64,128]{1,0:T(8,128)S(1)} collective-permute-done((f32[64,128]{1,0:T(8,128)S(1)}, f32[64,128]{1,0:T(8,128)S(1)}, u32[]{:S(2)}, u32[]{:S(2)}) %collective-permute-start.8) | collective-permute-done | bytes 32800 | tf_op jit(solution)/shard_map/ppermute | solution.py:368
  75.8 1.8 %collective-permute-done.7.one_ref = f32[64,128]{1,0:T(8,128)S(1)} collective-permute-done((f32[64,128]{1,0:T(8,128)S(1)}, f32[64,128]{1,0:T(8,128)S(1)}, u32[]{:S(2)}, u32[]{:S(2)}) %collective-permute-start.7) | collective-permute-done | bytes 32800 | tf_op jit(solution)/shard_map/ppermute | solution.py:368
  77.6 0.7 last_sum.1
  (14 shorter events, 0.1 us)
Async XLA Ops:
  4.3 14.8 %copy-start = (s32[16,512]{1,0:T(8,128)S(1)}, s32[16,512]{1,0:T(8,128)}, u32[]{:S(2)}) copy-start(s32[16,512]{1,0:T(8,128)} %param.5) | copy-start | bytes 98308
  4.3 44.9 %all-to-all-start = ((f32[256,8,128]{2,1,0:T(8,128)}), f32[256,8,128]{2,1,0:T(8,128)S(1)}, u32[]{:S(2)}, u32[]{:S(2)}) async-start(f32[256,8,128]{2,1,0:T(8,128)} %bitcast.19), calls=%async_computation | async-start | bytes 2097152 | tf_op jit(solution)/shard_map/all_to_all | solution.py:340
  49.3 8.0 %collective-permute-start.1 = (f32[66,8,128]{2,1,0:T(8,128)S(1)}, f32[66,8,128]{2,1,0:T(8,128)S(1)}, u32[]{:S(2)}, u32[]{:S(2)}) collective-permute-start(f32[66,8,128]{2,1,0:T(8,128)S(1)} %get-tuple-element.21), channel_id=1, source_target_pairs={{0,1},{1,0},{2,3},{3,2},{4,5},{5,4},{6,7},{7,6},{8,9},{9,8},{10,11... | collective-permute-start | bytes 811016 | tf_op jit(solution)/shard_map/ppermute | solution.py:362
  50.8 10.0 %collective-permute-start = (f32[66,8,128]{2,1,0:T(8,128)S(1)}, f32[66,8,128]{2,1,0:T(8,128)S(1)}, u32[]{:S(2)}, u32[]{:S(2)}) collective-permute-start(f32[66,8,128]{2,1,0:T(8,128)S(1)} %get-tuple-element.22), channel_id=1, source_target_pairs={{0,31},{1,2},{2,1},{3,4},{4,3},{5,6},{6,5},{7,8},{8,7},{9,10},{10,... | collective-permute-start | bytes 811016 | tf_op jit(solution)/shard_map/ppermute | solution.py:361
  61.9 1.3 %collective-permute-start.2 = (f32[64,128]{1,0:T(8,128)S(1)}, f32[64,128]{1,0:T(8,128)S(1)}, u32[]{:S(2)}, u32[]{:S(2)}) collective-permute-start(f32[64,128]{1,0:T(8,128)S(1)} %edge_across.1), channel_id=1, source_target_pairs={{0,1},{1,0},{2,3},{3,2},{4,5},{5,4},{6,7},{7,6},{8,9},{9,8},{10,11... | collective-permute-start | bytes 98312 | tf_op jit(solution)/shard_map/ppermute | solution.py:368
  63.2 4.9 %collective-permute-start.5 = (f32[64,128]{1,0:T(8,128)S(1)}, f32[64,128]{1,0:T(8,128)S(1)}, u32[]{:S(2)}, u32[]{:S(2)}) collective-permute-start(f32[64,128]{1,0:T(8,128)S(1)} %add.35), channel_id=1, source_target_pairs={{0,10},{1,11},{2,8},{3,9},{4,14},{5,15},{6,12},{7,13},{8,2},{9,3},... | collective-permute-start | bytes 98312 | tf_op jit(solution)/shard_map/ppermute | solution.py:368
  63.2 4.8 %collective-permute-start.4 = (f32[64,128]{1,0:T(8,128)S(1)}, f32[64,128]{1,0:T(8,128)S(1)}, u32[]{:S(2)}, u32[]{:S(2)}) collective-permute-start(f32[64,128]{1,0:T(8,128)S(1)} %add.35), channel_id=1, source_target_pairs={{0,8},{1,9},{2,10},{3,11},{4,12},{5,13},{6,14},{7,15},{8,0},{9,1},... | collective-permute-start | bytes 98312 | tf_op jit(solution)/shard_map/ppermute | solution.py:368
  64.8 3.9 %collective-permute-start.3 = (f32[64,128]{1,0:T(8,128)S(1)}, f32[64,128]{1,0:T(8,128)S(1)}, u32[]{:S(2)}, u32[]{:S(2)}) collective-permute-start(f32[64,128]{1,0:T(8,128)S(1)} %add.35), channel_id=1, source_target_pairs={{0,2},{1,3},{2,0},{3,1},{4,6},{5,7},{6,4},{7,5},{8,10},{9,11},{10,... | collective-permute-start | bytes 98312 | tf_op jit(solution)/shard_map/ppermute | solution.py:368
  68.8 7.0 %collective-permute-start.8 = (f32[64,128]{1,0:T(8,128)S(1)}, f32[64,128]{1,0:T(8,128)S(1)}, u32[]{:S(2)}, u32[]{:S(2)}) collective-permute-start(f32[64,128]{1,0:T(8,128)S(1)} %add_add_fusion.mine_ref), channel_id=1, source_target_pairs={{0,28},{1,29},{2,30},{3,31},{4,24},{5,25},{6,26},{7,27},{8,20},{9,... | collective-permute-start | bytes 98312 | tf_op jit(solution)/shard_map/ppermute | solution.py:368
  72.4 5.1 %collective-permute-start.7 = (f32[64,128]{1,0:T(8,128)S(1)}, f32[64,128]{1,0:T(8,128)S(1)}, u32[]{:S(2)}, u32[]{:S(2)}) collective-permute-start(f32[64,128]{1,0:T(8,128)S(1)} %add_add_fusion.mine_ref), channel_id=1, source_target_pairs={{0,24},{1,25},{2,26},{3,27},{4,28},{5,29},{6,30},{7,31},{8,16},{9,... | collective-permute-start | bytes 98312 | tf_op jit(solution)/shard_map/ppermute | solution.py:368
  72.4 5.1 %collective-permute-start.6 = (f32[64,128]{1,0:T(8,128)S(1)}, f32[64,128]{1,0:T(8,128)S(1)}, u32[]{:S(2)}, u32[]{:S(2)}) collective-permute-start(f32[64,128]{1,0:T(8,128)S(1)} %add_add_fusion.mine_ref), channel_id=1, source_target_pairs={{0,4},{1,5},{2,6},{3,7},{4,0},{5,1},{6,2},{7,3},{8,12},{9,13},{10,... | collective-permute-start | bytes 98312 | tf_op jit(solution)/shard_map/ppermute | solution.py:368

commit v9 on v8

--- a/solution.py
+++ b/solution.py
@@ -368,10 +368,10 @@
         return lax.ppermute(values, "sites", [(i, i ^ flip) for i in range(count)])
 
     total = total + moved(total, 1)
-    z_near, y_near, both = moved(total, 2), moved(total, 8), moved(total, 10)
-    total = (total + z_near) + (y_near + both)
-    z_far, y_far, both = moved(total, 4), moved(total, 24), moved(total, 28)
-    out = last_sum(total, z_far, y_far, both).reshape(2, MOM, width_group, n_left)
+    y_near, z_near, both = moved(total, 8), moved(total, 2), moved(total, 10)
+    total = (total + y_near) + (z_near + both)
+    y_far, z_far, both = moved(total, 24), moved(total, 4), moved(total, 28)
+    out = last_sum(total, y_far, z_far, both).reshape(2, MOM, width_group, n_left)
     return jnp.swapaxes(out, 2, 3)[..., None]
 
 

time: 79.3 us -> 79.6 us (level)
  transfers between devices with their start and end apart: 10 -> 10, of which waited for: 7 -> 8; matrix products, arithmetic and copies ran while one was open for 6% -> 6% of each run, Pallas kernels for 7% -> 7%
where the time goes in v9:
time: 79.6 us; the launch traced here: 78.5 us
  waiting for transfers between devices  34.1 us (43%)
  starting transfers between devices  27.4 us (34%)
  Pallas kernels  11.6 us (15%)
  matrix products  5.05 us (6%)
    all_to_all x1, waiting for transfers between devices, per_device(): recv = lax.all_to_all(packed, ('cols', 'sites'), 0, 0, tiled=True)  25.1 us
    all_to_all x1, starting transfers between devices, per_device(): recv = lax.all_to_all(packed, ('cols', 'sites'), 0, 0, tiled=True)  14.7 us
    ppermute x7, starting transfers between devices, moved(): return lax.ppermute(values, 'sites', [(i, i ^ flip) for i in range(count)])  9.24 us
    ppermute x7, waiting for transfers between devices, moved(): return lax.ppermute(values, 'sites', [(i, i ^ flip) for i in range(count)])  6.58 us
    pallas_call x1, Pallas kernels, inner_moments(): pl.pallas_call(inner_kernel, in_specs=[vm] * 3, out_specs=[vm] * 2, out_s...  4.47 us
    dot_general x1, matrix products, per_device(): left = jnp.dot(left, to_place, preferred_element_type=jnp.bfloat16)  4.46 us
    pallas_call x1, Pallas kernels, pack(): pl.pallas_call(pack_kernel, grid=(groups // step,), in_specs=[pl.BlockSpe...  4.32 us
    ppermute x1, waiting for transfers between devices, per_device(): across = lax.ppermute(jnp.where(lower_slab, low, high), 'sites', to_chip)  2.46 us
  transfers between devices with their start and end apart: 10, of which 8 were waited for; matrix products, arithmetic and copies ran while one was open for 6% of the time, Pallas kernels for 7%

profile of v9, /device:TPU:2, one launch (start us, length us, event | category | flops | bytes accessed | tf_op | source)
XLA Modules:
  0.0 78.5 jit_solution(14005024512600881285)
XLA Ops:
  0.0 4.3 %pack.1 = f32[8,32,8,128]{3,2,1,0:T(8,128)} custom-call(f32[32,8,32,32]{3,2,1,0:T(8,128)} %bitcast.18), custom_call_target="tpu_custom_call" | custom-call | tf_op jit(solution)/shard_map/pack/pallas_call | solution.py:60
  4.3 14.7 %all-to-all-start = ((f32[256,8,128]{2,1,0:T(8,128)}), f32[256,8,128]{2,1,0:T(8,128)S(1)}, u32[]{:S(2)}, u32[]{:S(2)}) async-start(f32[256,8,128]{2,1,0:T(8,128)} %bitcast.19), calls=%async_computation | async-start | bytes 2097152 | tf_op jit(solution)/shard_map/all_to_all | solution.py:340
  19.1 0.6 convolution_bitcast_fusion
  19.7 4.5 %fusion.2.left_ref = bf16[16,128,512]{2,1,0:T(8,128)(2,1)S(1)} fusion(bf16[128,16,512]{2,1,0:T(8,128)(2,1)} %bitcast.22, s32[512]{0:T(512)S(1)} %get-tuple-element.25, s32[512]{0:T(512)S(1)} %get-tuple-element.28, s32[512]{0:T(512)S(1)} %get-tuple-element.26, s32[512]{0:T(512)S(1)} %get-tuple-element.27, pred[512]{0:T(512)(128)(4,1)S(1)} %get-tuple-element.29, ...), kind=kOutput, calls=%fused_computation.2 | convolution fusion | flops 1075052544 | bytes 4203520 | tf_op jit(solution)/shard_map/dot_general | solution.py:346
  24.2 25.1 %all-to-all-done.recv_ref = f32[256,8,128]{2,1,0:T(8,128)S(1)} async-done(((f32[256,8,128]{2,1,0:T(8,128)}), f32[256,8,128]{2,1,0:T(8,128)S(1)}, u32[]{:S(2)}, u32[]{:S(2)}) %all-to-all-start) | async-done | bytes 1048608 | tf_op jit(solution)/shard_map/all_to_all | solution.py:340
  49.3 1.5 %collective-permute-start.1 = (f32[66,8,128]{2,1,0:T(8,128)S(1)}, f32[66,8,128]{2,1,0:T(8,128)S(1)}, u32[]{:S(2)}, u32[]{:S(2)}) collective-permute-start(f32[66,8,128]{2,1,0:T(8,128)S(1)} %get-tuple-element.21), channel_id=1, source_target_pairs={{0,1},{1,0},{2,3},{3,2},{4,5},{5,4},{6,7},{7,6},{8,9},{9,8},{10,11... | collective-permute-start | bytes 811016 | tf_op jit(solution)/shard_map/ppermute | solution.py:362
  50.8 2.0 %collective-permute-start = (f32[66,8,128]{2,1,0:T(8,128)S(1)}, f32[66,8,128]{2,1,0:T(8,128)S(1)}, u32[]{:S(2)}, u32[]{:S(2)}) collective-permute-start(f32[66,8,128]{2,1,0:T(8,128)S(1)} %get-tuple-element.22), channel_id=1, source_target_pairs={{0,31},{1,2},{2,1},{3,4},{4,3},{5,6},{6,5},{7,8},{8,7},{9,10},{10,... | collective-permute-start | bytes 811016 | tf_op jit(solution)/shard_map/ppermute | solution.py:361
  52.8 4.5 %inner_moments.1 = (f32[128,128]{1,0:T(8,128)S(1)}, f32[4,2,2,2,2,4,8,128]{7,6,5,4,3,2,1,0:T(8,128)S(1)}) custom-call(f32[256,8,128]{2,1,0:T(8,128)S(1)} %all-to-all-done.recv_ref, f32[16,4,128]{2,1,0:T(4,128)S(1)} %reshape.28.pres_ref, bf16[16,128,512]{2,1,0:T(8,128)(2,1)S(1)} %fusion.2.left_ref), custom_call_target="tpu_custom_call" | custom-call | flops 1000000000 | bytes 10000000 | tf_op jit(solution)/shard_map/inner_moments/pallas_call | solution.py:277
  57.3 1.1 %edge_sibling.1.sum_ref = f32[128,128]{1,0:T(8,128)S(1)} custom-call(s32[1]{0:T(128)} %bitcast.core_ref, f32[66,8,128]{2,1,0:T(8,128)S(1)} %collective-permute-done.1.src_ref, f32[16,4,128]{2,1,0:T(4,128)S(1)} %reshape.28.pres_ref, bf16[16,128,512]{2,1,0:T(8,128)(2,1)S(1)} %fusion.2.left_ref, f32[128,128]{1,0:T(8,128)S(1)} %get-tuple-element.17.sum_ref, ...), custom_call_target="tpu_custom_call" | custom-call | flops 100000000 | bytes 1000000 | tf_op jit(solution)/shard_map/edge_sibling/pallas_call | solution.py:298
  58.4 2.5 %collective-permute-done.src_ref = f32[66,8,128]{2,1,0:T(8,128)S(1)} collective-permute-done((f32[66,8,128]{2,1,0:T(8,128)S(1)}, f32[66,8,128]{2,1,0:T(8,128)S(1)}, u32[]{:S(2)}, u32[]{:S(2)}) %collective-permute-start) | collective-permute-done | bytes 270368 | tf_op jit(solution)/shard_map/ppermute | solution.py:361
  60.9 1.0 %edge_across.1 = f32[64,128]{1,0:T(8,128)S(1)} custom-call(s32[1]{0:T(128)} %bitcast.core_ref, f32[66,8,128]{2,1,0:T(8,128)S(1)} %collective-permute-done.src_ref, f32[16,4,128]{2,1,0:T(4,128)S(1)} %reshape.28.pres_ref, bf16[16,128,512]{2,1,0:T(8,128)(2,1)S(1)} %fusion.2.left_ref, f32[128,128]{1,0:T(8,128)S(1)} %edge_sibling.1.sum_ref, ...), custom_call_target="tpu_custom_call" | custom-call | flops 100000000 | bytes 1000000 | tf_op jit(solution)/shard_map/edge_across/pallas_call | solution.py:298
  61.9 0.1 collective-permute-start.2
  62.0 1.2 %collective-permute-done.2 = f32[64,128]{1,0:T(8,128)S(1)} collective-permute-done((f32[64,128]{1,0:T(8,128)S(1)}, f32[64,128]{1,0:T(8,128)S(1)}, u32[]{:S(2)}, u32[]{:S(2)}) %collective-permute-start.2) | collective-permute-done | bytes 32800 | tf_op jit(solution)/shard_map/ppermute | solution.py:368
  63.2 2.8 %collective-permute-start.4 = (f32[64,128]{1,0:T(8,128)S(1)}, f32[64,128]{1,0:T(8,128)S(1)}, u32[]{:S(2)}, u32[]{:S(2)}) collective-permute-start(f32[64,128]{1,0:T(8,128)S(1)} %add.35), channel_id=1, source_target_pairs={{0,2},{1,3},{2,0},{3,1},{4,6},{5,7},{6,4},{7,5},{8,10},{9,11},{10,... | collective-permute-start | bytes 98312 | tf_op jit(solution)/shard_map/ppermute | solution.py:368
  66.0 0.6 collective-permute-start.3
  66.7 1.3 %collective-permute-done.5 = f32[64,128]{1,0:T(8,128)S(1)} collective-permute-done((f32[64,128]{1,0:T(8,128)S(1)}, f32[64,128]{1,0:T(8,128)S(1)}, u32[]{:S(2)}, u32[]{:S(2)}) %collective-permute-start.5) | collective-permute-done | bytes 32800 | tf_op jit(solution)/shard_map/ppermute | solution.py:368
  68.0 0.3 collective-permute-done.4
  68.3 1.7 %collective-permute-done.3 = f32[64,128]{1,0:T(8,128)S(1)} collective-permute-done((f32[64,128]{1,0:T(8,128)S(1)}, f32[64,128]{1,0:T(8,128)S(1)}, u32[]{:S(2)}, u32[]{:S(2)}) %collective-permute-start.3) | collective-permute-done | bytes 32800 | tf_op jit(solution)/shard_map/ppermute | solution.py:368
  70.0 1.3 %collective-permute-start.8 = (f32[64,128]{1,0:T(8,128)S(1)}, f32[64,128]{1,0:T(8,128)S(1)}, u32[]{:S(2)}, u32[]{:S(2)}) collective-permute-start(f32[64,128]{1,0:T(8,128)S(1)} %add_add_fusion.mine_ref), channel_id=1, source_target_pairs={{0,28},{1,29},{2,30},{3,31},{4,24},{5,25},{6,26},{7,27},{8,20},{9,... | collective-permute-start | bytes 98312 | tf_op jit(solution)/shard_map/ppermute | solution.py:368
  71.2 1.4 %collective-permute-start.7 = (f32[64,128]{1,0:T(8,128)S(1)}, f32[64,128]{1,0:T(8,128)S(1)}, u32[]{:S(2)}, u32[]{:S(2)}) collective-permute-start(f32[64,128]{1,0:T(8,128)S(1)} %add_add_fusion.mine_ref), channel_id=1, source_target_pairs={{0,4},{1,5},{2,6},{3,7},{4,0},{5,1},{6,2},{7,3},{8,12},{9,13},{10,... | collective-permute-start | bytes 98312 | tf_op jit(solution)/shard_map/ppermute | solution.py:368
  72.6 3.0 %collective-permute-start.6 = (f32[64,128]{1,0:T(8,128)S(1)}, f32[64,128]{1,0:T(8,128)S(1)}, u32[]{:S(2)}, u32[]{:S(2)}) collective-permute-start(f32[64,128]{1,0:T(8,128)S(1)} %add_add_fusion.mine_ref), channel_id=1, source_target_pairs={{0,24},{1,25},{2,26},{3,27},{4,28},{5,29},{6,30},{7,31},{8,16},{9,... | collective-permute-start | bytes 98312 | tf_op jit(solution)/shard_map/ppermute | solution.py:368
  75.6 1.5 %collective-permute-done.8.other_ref = f32[64,128]{1,0:T(8,128)S(1)} collective-permute-done((f32[64,128]{1,0:T(8,128)S(1)}, f32[64,128]{1,0:T(8,128)S(1)}, u32[]{:S(2)}, u32[]{:S(2)}) %collective-permute-start.8) | collective-permute-done | bytes 32800 | tf_op jit(solution)/shard_map/ppermute | solution.py:368
  77.1 0.6 collective-permute-done.6.far_ref
  77.8 0.7 last_sum.1
  (14 shorter events, 0.1 us)
Async XLA Ops:
  4.3 14.8 %copy-start = (s32[16,512]{1,0:T(8,128)S(1)}, s32[16,512]{1,0:T(8,128)}, u32[]{:S(2)}) copy-start(s32[16,512]{1,0:T(8,128)} %param.5) | copy-start | bytes 98308
  4.3 44.9 %all-to-all-start = ((f32[256,8,128]{2,1,0:T(8,128)}), f32[256,8,128]{2,1,0:T(8,128)S(1)}, u32[]{:S(2)}, u32[]{:S(2)}) async-start(f32[256,8,128]{2,1,0:T(8,128)} %bitcast.19), calls=%async_computation | async-start | bytes 2097152 | tf_op jit(solution)/shard_map/all_to_all | solution.py:340
  49.3 8.0 %collective-permute-start.1 = (f32[66,8,128]{2,1,0:T(8,128)S(1)}, f32[66,8,128]{2,1,0:T(8,128)S(1)}, u32[]{:S(2)}, u32[]{:S(2)}) collective-permute-start(f32[66,8,128]{2,1,0:T(8,128)S(1)} %get-tuple-element.21), channel_id=1, source_target_pairs={{0,1},{1,0},{2,3},{3,2},{4,5},{5,4},{6,7},{7,6},{8,9},{9,8},{10,11... | collective-permute-start | bytes 811016 | tf_op jit(solution)/shard_map/ppermute | solution.py:362
  50.8 10.0 %collective-permute-start = (f32[66,8,128]{2,1,0:T(8,128)S(1)}, f32[66,8,128]{2,1,0:T(8,128)S(1)}, u32[]{:S(2)}, u32[]{:S(2)}) collective-permute-start(f32[66,8,128]{2,1,0:T(8,128)S(1)} %get-tuple-element.22), channel_id=1, source_target_pairs={{0,31},{1,2},{2,1},{3,4},{4,3},{5,6},{6,5},{7,8},{8,7},{9,10},{10,... | collective-permute-start | bytes 811016 | tf_op jit(solution)/shard_map/ppermute | solution.py:361
  61.9 1.3 %collective-permute-start.2 = (f32[64,128]{1,0:T(8,128)S(1)}, f32[64,128]{1,0:T(8,128)S(1)}, u32[]{:S(2)}, u32[]{:S(2)}) collective-permute-start(f32[64,128]{1,0:T(8,128)S(1)} %edge_across.1), channel_id=1, source_target_pairs={{0,1},{1,0},{2,3},{3,2},{4,5},{5,4},{6,7},{7,6},{8,9},{9,8},{10,11... | collective-permute-start | bytes 98312 | tf_op jit(solution)/shard_map/ppermute | solution.py:368
  63.2 4.8 %collective-permute-start.5 = (f32[64,128]{1,0:T(8,128)S(1)}, f32[64,128]{1,0:T(8,128)S(1)}, u32[]{:S(2)}, u32[]{:S(2)}) collective-permute-start(f32[64,128]{1,0:T(8,128)S(1)} %add.35), channel_id=1, source_target_pairs={{0,10},{1,11},{2,8},{3,9},{4,14},{5,15},{6,12},{7,13},{8,2},{9,3},... | collective-permute-start | bytes 98312 | tf_op jit(solution)/shard_map/ppermute | solution.py:368
  63.2 5.1 %collective-permute-start.4 = (f32[64,128]{1,0:T(8,128)S(1)}, f32[64,128]{1,0:T(8,128)S(1)}, u32[]{:S(2)}, u32[]{:S(2)}) collective-permute-start(f32[64,128]{1,0:T(8,128)S(1)} %add.35), channel_id=1, source_target_pairs={{0,2},{1,3},{2,0},{3,1},{4,6},{5,7},{6,4},{7,5},{8,10},{9,11},{10,... | collective-permute-start | bytes 98312 | tf_op jit(solution)/shard_map/ppermute | solution.py:368
  66.0 3.9 %collective-permute-start.3 = (f32[64,128]{1,0:T(8,128)S(1)}, f32[64,128]{1,0:T(8,128)S(1)}, u32[]{:S(2)}, u32[]{:S(2)}) collective-permute-start(f32[64,128]{1,0:T(8,128)S(1)} %add.35), channel_id=1, source_target_pairs={{0,8},{1,9},{2,10},{3,11},{4,12},{5,13},{6,14},{7,15},{8,0},{9,1},... | collective-permute-start | bytes 98312 | tf_op jit(solution)/shard_map/ppermute | solution.py:368
  70.0 7.2 %collective-permute-start.8 = (f32[64,128]{1,0:T(8,128)S(1)}, f32[64,128]{1,0:T(8,128)S(1)}, u32[]{:S(2)}, u32[]{:S(2)}) collective-permute-start(f32[64,128]{1,0:T(8,128)S(1)} %add_add_fusion.mine_ref), channel_id=1, source_target_pairs={{0,28},{1,29},{2,30},{3,31},{4,24},{5,25},{6,26},{7,27},{8,20},{9,... | collective-permute-start | bytes 98312 | tf_op jit(solution)/shard_map/ppermute | solution.py:368
  71.2 5.9 %collective-permute-start.7 = (f32[64,128]{1,0:T(8,128)S(1)}, f32[64,128]{1,0:T(8,128)S(1)}, u32[]{:S(2)}, u32[]{:S(2)}) collective-permute-start(f32[64,128]{1,0:T(8,128)S(1)} %add_add_fusion.mine_ref), channel_id=1, source_target_pairs={{0,4},{1,5},{2,6},{3,7},{4,0},{5,1},{6,2},{7,3},{8,12},{9,13},{10,... | collective-permute-start | bytes 98312 | tf_op jit(solution)/shard_map/ppermute | solution.py:368
  72.6 5.1 %collective-permute-start.6 = (f32[64,128]{1,0:T(8,128)S(1)}, f32[64,128]{1,0:T(8,128)S(1)}, u32[]{:S(2)}, u32[]{:S(2)}) collective-permute-start(f32[64,128]{1,0:T(8,128)S(1)} %add_add_fusion.mine_ref), channel_id=1, source_target_pairs={{0,24},{1,25},{2,26},{3,27},{4,28},{5,29},{6,30},{7,31},{8,16},{9,... | collective-permute-start | bytes 98312 | tf_op jit(solution)/shard_map/ppermute | solution.py:368

commit v10 on v8

--- a/solution.py
+++ b/solution.py
@@ -352,14 +352,18 @@
     edge = HALO * width // piece
     low_mask = present[:HALO].reshape(-1, SUB, LANES)
     high_mask = present[rows - HALO :].reshape(-1, SUB, LANES)
-    low = jnp.concatenate([recv[:edge], low_mask])
-    high = jnp.concatenate([recv[recv.shape[0] - edge :], high_mask])
     core = lax.axis_index("sites") % 2
-    lower_slab = core == 0
     to_chip = [(i, (i + 1 if i % 2 else i - 1) % count) for i in range(count)]
     to_core = [(i, i ^ 1) for i in range(count)]
-    across = lax.ppermute(jnp.where(lower_slab, low, high), "sites", to_chip)
-    sibling = lax.ppermute(jnp.where(lower_slab, high, low), "sites", to_core)
+    masks = jnp.concatenate([low_mask, high_mask])
+
+    def edge_rows(side):
+        tiles = lax.dynamic_slice_in_dim(recv, side * (recv.shape[0] - edge), edge)
+        mask = lax.dynamic_slice_in_dim(masks, side * low_mask.shape[0], low_mask.shape[0])
+        return jnp.concatenate([tiles, mask])
+
+    across = lax.ppermute(edge_rows(core), "sites", to_chip)
+    sibling = lax.ppermute(edge_rows(1 - core), "sites", to_core)
     core = core.astype(jnp.int32).reshape(1)
     total, edges = inner_moments(recv, present, left)
     total = edge_moments(False, core, sibling, present, left, total, edges)

time: 79.3 us -> 79.4 us (level)
  transfers between devices with their start and end apart: 10 -> 10, of which waited for: 7 -> 7; matrix products, arithmetic and copies ran while one was open for 6% -> 7% of each run, Pallas kernels for 7% -> 7%
where the time goes in v10:
time: 79.4 us; the launch traced here: 78.4 us
  waiting for transfers between devices  33.9 us (43%)
  starting transfers between devices  27.5 us (35%)
  Pallas kernels  11.6 us (15%)
  matrix products  5.05 us (6%)
    all_to_all x1, waiting for transfers between devices, per_device(): recv = lax.all_to_all(packed, ('cols', 'sites'), 0, 0, tiled=True)  25 us
    all_to_all x1, starting transfers between devices, per_device(): recv = lax.all_to_all(packed, ('cols', 'sites'), 0, 0, tiled=True)  14.7 us
    ppermute x7, starting transfers between devices, moved(): return lax.ppermute(values, 'sites', [(i, i ^ flip) for i in range(count)])  9.24 us
    ppermute x7, waiting for transfers between devices, moved(): return lax.ppermute(values, 'sites', [(i, i ^ flip) for i in range(count)])  6.39 us
    pallas_call x1, Pallas kernels, inner_moments(): pl.pallas_call(inner_kernel, in_specs=[vm] * 3, out_specs=[vm] * 2, out_s...  4.47 us
    dot_general x1, matrix products, per_device(): left = jnp.dot(left, to_place, preferred_element_type=jnp.bfloat16)  4.46 us
    pallas_call x1, Pallas kernels, pack(): pl.pallas_call(pack_kernel, grid=(groups // step,), in_specs=[pl.BlockSpe...  4.32 us
    ppermute x1, waiting for transfers between devices, per_device(): across = lax.ppermute(edge_rows(core), 'sites', to_chip)  2.46 us
  transfers between devices with their start and end apart: 10, of which 7 were waited for; matrix products, arithmetic and copies ran while one was open for 7% of the time, Pallas kernels for 7%

profile of v10, /device:TPU:2, one launch (start us, length us, event | category | flops | bytes accessed | tf_op | source)
XLA Modules:
  0.0 78.4 jit_solution(9047169467840071687)
XLA Ops:
  0.0 4.3 %pack.1 = f32[8,32,8,128]{3,2,1,0:T(8,128)} custom-call(f32[32,8,32,32]{3,2,1,0:T(8,128)} %bitcast.18), custom_call_target="tpu_custom_call" | custom-call | tf_op jit(solution)/shard_map/pack/pallas_call | solution.py:60
  4.3 14.7 %all-to-all-start = ((f32[256,8,128]{2,1,0:T(8,128)}), f32[256,8,128]{2,1,0:T(8,128)S(1)}, u32[]{:S(2)}, u32[]{:S(2)}) async-start(f32[256,8,128]{2,1,0:T(8,128)} %bitcast.19), calls=%async_computation | async-start | bytes 2097152 | tf_op jit(solution)/shard_map/all_to_all | solution.py:340
  19.1 0.6 convolution_bitcast_fusion
  19.7 4.5 %fusion.2.left_ref = bf16[16,128,512]{2,1,0:T(8,128)(2,1)S(1)} fusion(bf16[128,16,512]{2,1,0:T(8,128)(2,1)} %bitcast.22, s32[512]{0:T(512)S(1)} %get-tuple-element.27, s32[512]{0:T(512)S(1)} %get-tuple-element.30, s32[512]{0:T(512)S(1)} %get-tuple-element.28, s32[512]{0:T(512)S(1)} %get-tuple-element.29, pred[512]{0:T(512)(128)(4,1)S(1)} %get-tuple-element.25, ...), kind=kOutput, calls=%fused_computation.2 | convolution fusion | flops 1075052544 | bytes 4203520 | tf_op jit(solution)/shard_map/dot_general | solution.py:346
  24.2 25.0 %all-to-all-done.recv_ref = f32[256,8,128]{2,1,0:T(8,128)S(1)} async-done(((f32[256,8,128]{2,1,0:T(8,128)}), f32[256,8,128]{2,1,0:T(8,128)S(1)}, u32[]{:S(2)}, u32[]{:S(2)}) %all-to-all-start) | async-done | bytes 1048608 | tf_op jit(solution)/shard_map/all_to_all | solution.py:340
  49.3 1.5 %collective-permute-start.1 = (f32[66,8,128]{2,1,0:T(8,128)S(1)}, f32[66,8,128]{2,1,0:T(8,128)S(1)}, u32[]{:S(2)}, u32[]{:S(2)}) collective-permute-start(f32[66,8,128]{2,1,0:T(8,128)S(1)} %pad_maximum_fusion.1), channel_id=1, source_target_pairs={{0,1},{1,0},{2,3},{3,2},{4,5},{5,4},{6,7},{7,6},{8,9},{9,8},{10,11... | collective-permute-start | bytes 811016 | tf_op jit(solution)/shard_map/ppermute | solution.py:366
  50.8 2.1 %collective-permute-start = (f32[66,8,128]{2,1,0:T(8,128)S(1)}, f32[66,8,128]{2,1,0:T(8,128)S(1)}, u32[]{:S(2)}, u32[]{:S(2)}) collective-permute-start(f32[66,8,128]{2,1,0:T(8,128)S(1)} %pad_maximum_fusion), channel_id=1, source_target_pairs={{0,31},{1,2},{2,1},{3,4},{4,3},{5,6},{6,5},{7,8},{8,7},{9,10},{10,... | collective-permute-start | bytes 811016 | tf_op jit(solution)/shard_map/ppermute | solution.py:365
  53.0 4.5 %inner_moments.1 = (f32[128,128]{1,0:T(8,128)S(1)}, f32[4,2,2,2,2,4,8,128]{7,6,5,4,3,2,1,0:T(8,128)S(1)}) custom-call(f32[256,8,128]{2,1,0:T(8,128)S(1)} %all-to-all-done.recv_ref, f32[16,4,128]{2,1,0:T(4,128)S(1)} %reshape.28.pres_ref, bf16[16,128,512]{2,1,0:T(8,128)(2,1)S(1)} %fusion.2.left_ref), custom_call_target="tpu_custom_call" | custom-call | flops 1000000000 | bytes 10000000 | tf_op jit(solution)/shard_map/inner_moments/pallas_call | solution.py:277
  57.4 1.1 %edge_sibling.1.sum_ref = f32[128,128]{1,0:T(8,128)S(1)} custom-call(s32[1]{0:T(128)} %bitcast.core_ref, f32[66,8,128]{2,1,0:T(8,128)S(1)} %collective-permute-done.1.src_ref, f32[16,4,128]{2,1,0:T(4,128)S(1)} %reshape.28.pres_ref, bf16[16,128,512]{2,1,0:T(8,128)(2,1)S(1)} %fusion.2.left_ref, f32[128,128]{1,0:T(8,128)S(1)} %get-tuple-element.17.sum_ref, ...), custom_call_target="tpu_custom_call" | custom-call | flops 100000000 | bytes 1000000 | tf_op jit(solution)/shard_map/edge_sibling/pallas_call | solution.py:298
  58.5 2.5 %collective-permute-done.src_ref = f32[66,8,128]{2,1,0:T(8,128)S(1)} collective-permute-done((f32[66,8,128]{2,1,0:T(8,128)S(1)}, f32[66,8,128]{2,1,0:T(8,128)S(1)}, u32[]{:S(2)}, u32[]{:S(2)}) %collective-permute-start) | collective-permute-done | bytes 270368 | tf_op jit(solution)/shard_map/ppermute | solution.py:365
  61.0 1.0 %edge_across.1 = f32[64,128]{1,0:T(8,128)S(1)} custom-call(s32[1]{0:T(128)} %bitcast.core_ref, f32[66,8,128]{2,1,0:T(8,128)S(1)} %collective-permute-done.src_ref, f32[16,4,128]{2,1,0:T(4,128)S(1)} %reshape.28.pres_ref, bf16[16,128,512]{2,1,0:T(8,128)(2,1)S(1)} %fusion.2.left_ref, f32[128,128]{1,0:T(8,128)S(1)} %edge_sibling.1.sum_ref, ...), custom_call_target="tpu_custom_call" | custom-call | flops 100000000 | bytes 1000000 | tf_op jit(solution)/shard_map/edge_across/pallas_call | solution.py:298
  62.0 0.1 collective-permute-start.2
  62.1 1.2 %collective-permute-done.2 = f32[64,128]{1,0:T(8,128)S(1)} collective-permute-done((f32[64,128]{1,0:T(8,128)S(1)}, f32[64,128]{1,0:T(8,128)S(1)}, u32[]{:S(2)}, u32[]{:S(2)}) %collective-permute-start.2) | collective-permute-done | bytes 32800 | tf_op jit(solution)/shard_map/ppermute | solution.py:372
  63.3 0.0 collective-permute-start.5
  63.3 1.4 %collective-permute-start.4 = (f32[64,128]{1,0:T(8,128)S(1)}, f32[64,128]{1,0:T(8,128)S(1)}, u32[]{:S(2)}, u32[]{:S(2)}) collective-permute-start(f32[64,128]{1,0:T(8,128)S(1)} %add.51), channel_id=1, source_target_pairs={{0,8},{1,9},{2,10},{3,11},{4,12},{5,13},{6,14},{7,15},{8,0},{9,1},... | collective-permute-start | bytes 98312 | tf_op jit(solution)/shard_map/ppermute | solution.py:372
  64.7 2.0 %collective-permute-start.3 = (f32[64,128]{1,0:T(8,128)S(1)}, f32[64,128]{1,0:T(8,128)S(1)}, u32[]{:S(2)}, u32[]{:S(2)}) collective-permute-start(f32[64,128]{1,0:T(8,128)S(1)} %add.51), channel_id=1, source_target_pairs={{0,2},{1,3},{2,0},{3,1},{4,6},{5,7},{6,4},{7,5},{8,10},{9,11},{10,... | collective-permute-start | bytes 98312 | tf_op jit(solution)/shard_map/ppermute | solution.py:372
  66.8 1.4 %collective-permute-done.5 = f32[64,128]{1,0:T(8,128)S(1)} collective-permute-done((f32[64,128]{1,0:T(8,128)S(1)}, f32[64,128]{1,0:T(8,128)S(1)}, u32[]{:S(2)}, u32[]{:S(2)}) %collective-permute-start.5) | collective-permute-done | bytes 32800 | tf_op jit(solution)/shard_map/ppermute | solution.py:372
  68.2 0.5 collective-permute-done.3
  68.7 3.9 %collective-permute-start.8 = (f32[64,128]{1,0:T(8,128)S(1)}, f32[64,128]{1,0:T(8,128)S(1)}, u32[]{:S(2)}, u32[]{:S(2)}) collective-permute-start(f32[64,128]{1,0:T(8,128)S(1)} %add_add_fusion.mine_ref), channel_id=1, source_target_pairs={{0,28},{1,29},{2,30},{3,31},{4,24},{5,25},{6,26},{7,27},{8,20},{9,... | collective-permute-start | bytes 98312 | tf_op jit(solution)/shard_map/ppermute | solution.py:372
  72.6 0.0 collective-permute-start.7
  72.6 1.8 %collective-permute-start.6 = (f32[64,128]{1,0:T(8,128)S(1)}, f32[64,128]{1,0:T(8,128)S(1)}, u32[]{:S(2)}, u32[]{:S(2)}) collective-permute-start(f32[64,128]{1,0:T(8,128)S(1)} %add_add_fusion.mine_ref), channel_id=1, source_target_pairs={{0,4},{1,5},{2,6},{3,7},{4,0},{5,1},{6,2},{7,3},{8,12},{9,13},{10,... | collective-permute-start | bytes 98312 | tf_op jit(solution)/shard_map/ppermute | solution.py:372
  74.4 1.3 %collective-permute-done.8.other_ref = f32[64,128]{1,0:T(8,128)S(1)} collective-permute-done((f32[64,128]{1,0:T(8,128)S(1)}, f32[64,128]{1,0:T(8,128)S(1)}, u32[]{:S(2)}, u32[]{:S(2)}) %collective-permute-start.8) | collective-permute-done | bytes 32800 | tf_op jit(solution)/shard_map/ppermute | solution.py:372
  75.7 2.0 %collective-permute-done.7.one_ref = f32[64,128]{1,0:T(8,128)S(1)} collective-permute-done((f32[64,128]{1,0:T(8,128)S(1)}, f32[64,128]{1,0:T(8,128)S(1)}, u32[]{:S(2)}, u32[]{:S(2)}) %collective-permute-start.7) | collective-permute-done | bytes 32800 | tf_op jit(solution)/shard_map/ppermute | solution.py:372
  77.7 0.7 last_sum.1
  (16 shorter events, 0.2 us)
Async XLA Ops:
  4.3 14.8 %copy-start = (s32[16,512]{1,0:T(8,128)S(1)}, s32[16,512]{1,0:T(8,128)}, u32[]{:S(2)}) copy-start(s32[16,512]{1,0:T(8,128)} %param.5) | copy-start | bytes 98308
  4.3 44.9 %all-to-all-start = ((f32[256,8,128]{2,1,0:T(8,128)}), f32[256,8,128]{2,1,0:T(8,128)S(1)}, u32[]{:S(2)}, u32[]{:S(2)}) async-start(f32[256,8,128]{2,1,0:T(8,128)} %bitcast.19), calls=%async_computation | async-start | bytes 2097152 | tf_op jit(solution)/shard_map/all_to_all | solution.py:340
  49.3 8.1 %collective-permute-start.1 = (f32[66,8,128]{2,1,0:T(8,128)S(1)}, f32[66,8,128]{2,1,0:T(8,128)S(1)}, u32[]{:S(2)}, u32[]{:S(2)}) collective-permute-start(f32[66,8,128]{2,1,0:T(8,128)S(1)} %pad_maximum_fusion.1), channel_id=1, source_target_pairs={{0,1},{1,0},{2,3},{3,2},{4,5},{5,4},{6,7},{7,6},{8,9},{9,8},{10,11... | collective-permute-start | bytes 811016 | tf_op jit(solution)/shard_map/ppermute | solution.py:366
  50.8 10.1 %collective-permute-start = (f32[66,8,128]{2,1,0:T(8,128)S(1)}, f32[66,8,128]{2,1,0:T(8,128)S(1)}, u32[]{:S(2)}, u32[]{:S(2)}) collective-permute-start(f32[66,8,128]{2,1,0:T(8,128)S(1)} %pad_maximum_fusion), channel_id=1, source_target_pairs={{0,31},{1,2},{2,1},{3,4},{4,3},{5,6},{6,5},{7,8},{8,7},{9,10},{10,... | collective-permute-start | bytes 811016 | tf_op jit(solution)/shard_map/ppermute | solution.py:365
  62.0 1.3 %collective-permute-start.2 = (f32[64,128]{1,0:T(8,128)S(1)}, f32[64,128]{1,0:T(8,128)S(1)}, u32[]{:S(2)}, u32[]{:S(2)}) collective-permute-start(f32[64,128]{1,0:T(8,128)S(1)} %edge_across.1), channel_id=1, source_target_pairs={{0,1},{1,0},{2,3},{3,2},{4,5},{5,4},{6,7},{7,6},{8,9},{9,8},{10,11... | collective-permute-start | bytes 98312 | tf_op jit(solution)/shard_map/ppermute | solution.py:372
  63.3 4.9 %collective-permute-start.5 = (f32[64,128]{1,0:T(8,128)S(1)}, f32[64,128]{1,0:T(8,128)S(1)}, u32[]{:S(2)}, u32[]{:S(2)}) collective-permute-start(f32[64,128]{1,0:T(8,128)S(1)} %add.51), channel_id=1, source_target_pairs={{0,10},{1,11},{2,8},{3,9},{4,14},{5,15},{6,12},{7,13},{8,2},{9,3},... | collective-permute-start | bytes 98312 | tf_op jit(solution)/shard_map/ppermute | solution.py:372
  63.3 4.9 %collective-permute-start.4 = (f32[64,128]{1,0:T(8,128)S(1)}, f32[64,128]{1,0:T(8,128)S(1)}, u32[]{:S(2)}, u32[]{:S(2)}) collective-permute-start(f32[64,128]{1,0:T(8,128)S(1)} %add.51), channel_id=1, source_target_pairs={{0,8},{1,9},{2,10},{3,11},{4,12},{5,13},{6,14},{7,15},{8,0},{9,1},... | collective-permute-start | bytes 98312 | tf_op jit(solution)/shard_map/ppermute | solution.py:372
  64.7 3.9 %collective-permute-start.3 = (f32[64,128]{1,0:T(8,128)S(1)}, f32[64,128]{1,0:T(8,128)S(1)}, u32[]{:S(2)}, u32[]{:S(2)}) collective-permute-start(f32[64,128]{1,0:T(8,128)S(1)} %add.51), channel_id=1, source_target_pairs={{0,2},{1,3},{2,0},{3,1},{4,6},{5,7},{6,4},{7,5},{8,10},{9,11},{10,... | collective-permute-start | bytes 98312 | tf_op jit(solution)/shard_map/ppermute | solution.py:372
  68.7 7.0 %collective-permute-start.8 = (f32[64,128]{1,0:T(8,128)S(1)}, f32[64,128]{1,0:T(8,128)S(1)}, u32[]{:S(2)}, u32[]{:S(2)}) collective-permute-start(f32[64,128]{1,0:T(8,128)S(1)} %add_add_fusion.mine_ref), channel_id=1, source_target_pairs={{0,28},{1,29},{2,30},{3,31},{4,24},{5,25},{6,26},{7,27},{8,20},{9,... | collective-permute-start | bytes 98312 | tf_op jit(solution)/shard_map/ppermute | solution.py:372
  72.6 5.1 %collective-permute-start.7 = (f32[64,128]{1,0:T(8,128)S(1)}, f32[64,128]{1,0:T(8,128)S(1)}, u32[]{:S(2)}, u32[]{:S(2)}) collective-permute-start(f32[64,128]{1,0:T(8,128)S(1)} %add_add_fusion.mine_ref), channel_id=1, source_target_pairs={{0,24},{1,25},{2,26},{3,27},{4,28},{5,29},{6,30},{7,31},{8,16},{9,... | collective-permute-start | bytes 98312 | tf_op jit(solution)/shard_map/ppermute | solution.py:372
  72.6 5.1 %collective-permute-start.6 = (f32[64,128]{1,0:T(8,128)S(1)}, f32[64,128]{1,0:T(8,128)S(1)}, u32[]{:S(2)}, u32[]{:S(2)}) collective-permute-start(f32[64,128]{1,0:T(8,128)S(1)} %add_add_fusion.mine_ref), channel_id=1, source_target_pairs={{0,4},{1,5},{2,6},{3,7},{4,0},{5,1},{6,2},{7,3},{8,12},{9,13},{10,... | collective-permute-start | bytes 98312 | tf_op jit(solution)/shard_map/ppermute | solution.py:372

commit v11 on v8

--- a/solution.py
+++ b/solution.py
@@ -39,17 +39,22 @@
 
     @pl.loop(0, groups * slabs // 4 // MERGES)
     def _(i):
-        for j in range(MERGES):
-            slot = i * MERGES + j
-            v = [turned[slot, pl.ds(t, SUB, stride=TILES), :] for t in range(TILES)]
+        every = [
+            [turned[i * MERGES + j, pl.ds(t, SUB, stride=TILES), :] for t in range(TILES)]
+            for j in range(MERGES)
+        ]
+        for v in every:
             for p in (0, 2):
                 low, upper = v[p], v[p + 1]
                 moved = jnp.take_along_axis(jnp.where(odd, low, upper), swapped, axis=1)
                 v[p], v[p + 1] = jnp.where(odd, moved, low), jnp.where(odd, upper, moved)
+        for v in every:
             for p in (0, 1):
                 low, upper = v[p], v[p + 2]
                 moved = pltpu.roll(jnp.where(high, low, upper), LANES // 2, 1)
                 v[p], v[p + 2] = jnp.where(high, moved, low), jnp.where(high, upper, moved)
+        for j, v in enumerate(every):
+            slot = i * MERGES + j
             for s in range(4):
                 out_ref[slot * 4 // slabs, slot * 4 % slabs + s] = v[s]
 

time: 79.3 us -> 79.3 us (level)
  no operation moved by 1% of the time
where the time goes in v11:
time: 79.3 us; the launch traced here: 78.3 us
  waiting for transfers between devices  33.9 us (43%)
  starting transfers between devices  27.5 us (35%)
  Pallas kernels  11.6 us (15%)
  matrix products  5.05 us (6%)
    all_to_all x1, waiting for transfers between devices, per_device(): recv = lax.all_to_all(packed, ('cols', 'sites'), 0, 0, tiled=True)  25.1 us
    all_to_all x1, starting transfers between devices, per_device(): recv = lax.all_to_all(packed, ('cols', 'sites'), 0, 0, tiled=True)  14.7 us
    ppermute x7, starting transfers between devices, moved(): return lax.ppermute(values, 'sites', [(i, i ^ flip) for i in range(count)])  9.24 us
    ppermute x7, waiting for transfers between devices, moved(): return lax.ppermute(values, 'sites', [(i, i ^ flip) for i in range(count)])  6.39 us
    pallas_call x1, Pallas kernels, inner_moments(): pl.pallas_call(inner_kernel, in_specs=[vm] * 3, out_specs=[vm] * 2, out_s...  4.47 us
    dot_general x1, matrix products, per_device(): left = jnp.dot(left, to_place, preferred_element_type=jnp.bfloat16)  4.46 us
    pallas_call x1, Pallas kernels, pack(): pl.pallas_call(pack_kernel, grid=(groups // step,), in_specs=[pl.BlockSpe...  4.32 us
    ppermute x1, waiting for transfers between devices, per_device(): across = lax.ppermute(jnp.where(lower_slab, low, high), 'sites', to_chip)  2.46 us
  transfers between devices with their start and end apart: 10, of which 7 were waited for; matrix products, arithmetic and copies ran while one was open for 6% of the time, Pallas kernels for 7%

profile of v11, /device:TPU:2, one launch (start us, length us, event | category | flops | bytes accessed | tf_op | source)
XLA Modules:
  0.0 78.3 jit_solution(10174576085068273062)
XLA Ops:
  0.0 4.3 %pack.1 = f32[8,32,8,128]{3,2,1,0:T(8,128)} custom-call(f32[32,8,32,32]{3,2,1,0:T(8,128)} %bitcast.18), custom_call_target="tpu_custom_call" | custom-call | tf_op jit(solution)/shard_map/pack/pallas_call | solution.py:65
  4.3 14.7 %all-to-all-start = ((f32[256,8,128]{2,1,0:T(8,128)}), f32[256,8,128]{2,1,0:T(8,128)S(1)}, u32[]{:S(2)}, u32[]{:S(2)}) async-start(f32[256,8,128]{2,1,0:T(8,128)} %bitcast.19), calls=%async_computation | async-start | bytes 2097152 | tf_op jit(solution)/shard_map/all_to_all | solution.py:345
  19.1 0.6 convolution_bitcast_fusion
  19.7 4.5 %fusion.2.left_ref = bf16[16,128,512]{2,1,0:T(8,128)(2,1)S(1)} fusion(bf16[128,16,512]{2,1,0:T(8,128)(2,1)} %bitcast.22, s32[512]{0:T(512)S(1)} %get-tuple-element.25, s32[512]{0:T(512)S(1)} %get-tuple-element.28, s32[512]{0:T(512)S(1)} %get-tuple-element.26, s32[512]{0:T(512)S(1)} %get-tuple-element.27, pred[512]{0:T(512)(128)(4,1)S(1)} %get-tuple-element.29, ...), kind=kOutput, calls=%fused_computation.2 | convolution fusion | flops 1075052544 | bytes 4203520 | tf_op jit(solution)/shard_map/dot_general | solution.py:351
  24.2 25.1 %all-to-all-done.recv_ref = f32[256,8,128]{2,1,0:T(8,128)S(1)} async-done(((f32[256,8,128]{2,1,0:T(8,128)}), f32[256,8,128]{2,1,0:T(8,128)S(1)}, u32[]{:S(2)}, u32[]{:S(2)}) %all-to-all-start) | async-done | bytes 1048608 | tf_op jit(solution)/shard_map/all_to_all | solution.py:345
  49.3 1.5 %collective-permute-start.1 = (f32[66,8,128]{2,1,0:T(8,128)S(1)}, f32[66,8,128]{2,1,0:T(8,128)S(1)}, u32[]{:S(2)}, u32[]{:S(2)}) collective-permute-start(f32[66,8,128]{2,1,0:T(8,128)S(1)} %get-tuple-element.21), channel_id=1, source_target_pairs={{0,1},{1,0},{2,3},{3,2},{4,5},{5,4},{6,7},{7,6},{8,9},{9,8},{10,11... | collective-permute-start | bytes 811016 | tf_op jit(solution)/shard_map/ppermute | solution.py:367
  50.8 2.0 %collective-permute-start = (f32[66,8,128]{2,1,0:T(8,128)S(1)}, f32[66,8,128]{2,1,0:T(8,128)S(1)}, u32[]{:S(2)}, u32[]{:S(2)}) collective-permute-start(f32[66,8,128]{2,1,0:T(8,128)S(1)} %get-tuple-element.22), channel_id=1, source_target_pairs={{0,31},{1,2},{2,1},{3,4},{4,3},{5,6},{6,5},{7,8},{8,7},{9,10},{10,... | collective-permute-start | bytes 811016 | tf_op jit(solution)/shard_map/ppermute | solution.py:366
  52.8 4.5 %inner_moments.1 = (f32[128,128]{1,0:T(8,128)S(1)}, f32[4,2,2,2,2,4,8,128]{7,6,5,4,3,2,1,0:T(8,128)S(1)}) custom-call(f32[256,8,128]{2,1,0:T(8,128)S(1)} %all-to-all-done.recv_ref, f32[16,4,128]{2,1,0:T(4,128)S(1)} %reshape.28.pres_ref, bf16[16,128,512]{2,1,0:T(8,128)(2,1)S(1)} %fusion.2.left_ref), custom_call_target="tpu_custom_call" | custom-call | flops 1000000000 | bytes 10000000 | tf_op jit(solution)/shard_map/inner_moments/pallas_call | solution.py:282
  57.3 0.0 collective-permute-done.1.src_ref
  57.3 1.1 %edge_sibling.1.sum_ref = f32[128,128]{1,0:T(8,128)S(1)} custom-call(s32[1]{0:T(128)} %bitcast.core_ref, f32[66,8,128]{2,1,0:T(8,128)S(1)} %collective-permute-done.1.src_ref, f32[16,4,128]{2,1,0:T(4,128)S(1)} %reshape.28.pres_ref, bf16[16,128,512]{2,1,0:T(8,128)(2,1)S(1)} %fusion.2.left_ref, f32[128,128]{1,0:T(8,128)S(1)} %get-tuple-element.17.sum_ref, ...), custom_call_target="tpu_custom_call" | custom-call | flops 100000000 | bytes 1000000 | tf_op jit(solution)/shard_map/edge_sibling/pallas_call | solution.py:303
  58.4 2.5 %collective-permute-done.src_ref = f32[66,8,128]{2,1,0:T(8,128)S(1)} collective-permute-done((f32[66,8,128]{2,1,0:T(8,128)S(1)}, f32[66,8,128]{2,1,0:T(8,128)S(1)}, u32[]{:S(2)}, u32[]{:S(2)}) %collective-permute-start) | collective-permute-done | bytes 270368 | tf_op jit(solution)/shard_map/ppermute | solution.py:366
  60.8 1.0 %edge_across.1 = f32[64,128]{1,0:T(8,128)S(1)} custom-call(s32[1]{0:T(128)} %bitcast.core_ref, f32[66,8,128]{2,1,0:T(8,128)S(1)} %collective-permute-done.src_ref, f32[16,4,128]{2,1,0:T(4,128)S(1)} %reshape.28.pres_ref, bf16[16,128,512]{2,1,0:T(8,128)(2,1)S(1)} %fusion.2.left_ref, f32[128,128]{1,0:T(8,128)S(1)} %edge_sibling.1.sum_ref, ...), custom_call_target="tpu_custom_call" | custom-call | flops 100000000 | bytes 1000000 | tf_op jit(solution)/shard_map/edge_across/pallas_call | solution.py:303
  61.9 0.1 collective-permute-start.2
  62.0 1.2 %collective-permute-done.2 = f32[64,128]{1,0:T(8,128)S(1)} collective-permute-done((f32[64,128]{1,0:T(8,128)S(1)}, f32[64,128]{1,0:T(8,128)S(1)}, u32[]{:S(2)}, u32[]{:S(2)}) %collective-permute-start.2) | collective-permute-done | bytes 32800 | tf_op jit(solution)/shard_map/ppermute | solution.py:373
  63.2 0.0 collective-permute-start.5
  63.2 1.7 %collective-permute-start.4 = (f32[64,128]{1,0:T(8,128)S(1)}, f32[64,128]{1,0:T(8,128)S(1)}, u32[]{:S(2)}, u32[]{:S(2)}) collective-permute-start(f32[64,128]{1,0:T(8,128)S(1)} %add.35), channel_id=1, source_target_pairs={{0,8},{1,9},{2,10},{3,11},{4,12},{5,13},{6,14},{7,15},{8,0},{9,1},... | collective-permute-start | bytes 98312 | tf_op jit(solution)/shard_map/ppermute | solution.py:373
  64.8 1.8 %collective-permute-start.3 = (f32[64,128]{1,0:T(8,128)S(1)}, f32[64,128]{1,0:T(8,128)S(1)}, u32[]{:S(2)}, u32[]{:S(2)}) collective-permute-start(f32[64,128]{1,0:T(8,128)S(1)} %add.35), channel_id=1, source_target_pairs={{0,2},{1,3},{2,0},{3,1},{4,6},{5,7},{6,4},{7,5},{8,10},{9,11},{10,... | collective-permute-start | bytes 98312 | tf_op jit(solution)/shard_map/ppermute | solution.py:373
  66.7 1.4 %collective-permute-done.5 = f32[64,128]{1,0:T(8,128)S(1)} collective-permute-done((f32[64,128]{1,0:T(8,128)S(1)}, f32[64,128]{1,0:T(8,128)S(1)}, u32[]{:S(2)}, u32[]{:S(2)}) %collective-permute-start.5) | collective-permute-done | bytes 32800 | tf_op jit(solution)/shard_map/ppermute | solution.py:373
  68.0 0.7 collective-permute-done.3
  68.8 3.7 %collective-permute-start.8 = (f32[64,128]{1,0:T(8,128)S(1)}, f32[64,128]{1,0:T(8,128)S(1)}, u32[]{:S(2)}, u32[]{:S(2)}) collective-permute-start(f32[64,128]{1,0:T(8,128)S(1)} %add_add_fusion.mine_ref), channel_id=1, source_target_pairs={{0,28},{1,29},{2,30},{3,31},{4,24},{5,25},{6,26},{7,27},{8,20},{9,... | collective-permute-start | bytes 98312 | tf_op jit(solution)/shard_map/ppermute | solution.py:373
  72.4 2.0 %collective-permute-start.6 = (f32[64,128]{1,0:T(8,128)S(1)}, f32[64,128]{1,0:T(8,128)S(1)}, u32[]{:S(2)}, u32[]{:S(2)}) collective-permute-start(f32[64,128]{1,0:T(8,128)S(1)} %add_add_fusion.mine_ref), channel_id=1, source_target_pairs={{0,4},{1,5},{2,6},{3,7},{4,0},{5,1},{6,2},{7,3},{8,12},{9,13},{10,... | collective-permute-start | bytes 98312 | tf_op jit(solution)/shard_map/ppermute | solution.py:373
  74.5 1.3 %collective-permute-done.8.other_ref = f32[64,128]{1,0:T(8,128)S(1)} collective-permute-done((f32[64,128]{1,0:T(8,128)S(1)}, f32[64,128]{1,0:T(8,128)S(1)}, u32[]{:S(2)}, u32[]{:S(2)}) %collective-permute-start.8) | collective-permute-done | bytes 32800 | tf_op jit(solution)/shard_map/ppermute | solution.py:373
  75.8 1.8 %collective-permute-done.7.one_ref = f32[64,128]{1,0:T(8,128)S(1)} collective-permute-done((f32[64,128]{1,0:T(8,128)S(1)}, f32[64,128]{1,0:T(8,128)S(1)}, u32[]{:S(2)}, u32[]{:S(2)}) %collective-permute-start.7) | collective-permute-done | bytes 32800 | tf_op jit(solution)/shard_map/ppermute | solution.py:373
  77.6 0.7 last_sum.1
  (14 shorter events, 0.1 us)
Async XLA Ops:
  4.3 14.8 %copy-start = (s32[16,512]{1,0:T(8,128)S(1)}, s32[16,512]{1,0:T(8,128)}, u32[]{:S(2)}) copy-start(s32[16,512]{1,0:T(8,128)} %param.5) | copy-start | bytes 98308
  4.3 44.9 %all-to-all-start = ((f32[256,8,128]{2,1,0:T(8,128)}), f32[256,8,128]{2,1,0:T(8,128)S(1)}, u32[]{:S(2)}, u32[]{:S(2)}) async-start(f32[256,8,128]{2,1,0:T(8,128)} %bitcast.19), calls=%async_computation | async-start | bytes 2097152 | tf_op jit(solution)/shard_map/all_to_all | solution.py:345
  49.3 8.0 %collective-permute-start.1 = (f32[66,8,128]{2,1,0:T(8,128)S(1)}, f32[66,8,128]{2,1,0:T(8,128)S(1)}, u32[]{:S(2)}, u32[]{:S(2)}) collective-permute-start(f32[66,8,128]{2,1,0:T(8,128)S(1)} %get-tuple-element.21), channel_id=1, source_target_pairs={{0,1},{1,0},{2,3},{3,2},{4,5},{5,4},{6,7},{7,6},{8,9},{9,8},{10,11... | collective-permute-start | bytes 811016 | tf_op jit(solution)/shard_map/ppermute | solution.py:367
  50.8 10.0 %collective-permute-start = (f32[66,8,128]{2,1,0:T(8,128)S(1)}, f32[66,8,128]{2,1,0:T(8,128)S(1)}, u32[]{:S(2)}, u32[]{:S(2)}) collective-permute-start(f32[66,8,128]{2,1,0:T(8,128)S(1)} %get-tuple-element.22), channel_id=1, source_target_pairs={{0,31},{1,2},{2,1},{3,4},{4,3},{5,6},{6,5},{7,8},{8,7},{9,10},{10,... | collective-permute-start | bytes 811016 | tf_op jit(solution)/shard_map/ppermute | solution.py:366
  61.9 1.3 %collective-permute-start.2 = (f32[64,128]{1,0:T(8,128)S(1)}, f32[64,128]{1,0:T(8,128)S(1)}, u32[]{:S(2)}, u32[]{:S(2)}) collective-permute-start(f32[64,128]{1,0:T(8,128)S(1)} %edge_across.1), channel_id=1, source_target_pairs={{0,1},{1,0},{2,3},{3,2},{4,5},{5,4},{6,7},{7,6},{8,9},{9,8},{10,11... | collective-permute-start | bytes 98312 | tf_op jit(solution)/shard_map/ppermute | solution.py:373
  63.2 4.9 %collective-permute-start.5 = (f32[64,128]{1,0:T(8,128)S(1)}, f32[64,128]{1,0:T(8,128)S(1)}, u32[]{:S(2)}, u32[]{:S(2)}) collective-permute-start(f32[64,128]{1,0:T(8,128)S(1)} %add.35), channel_id=1, source_target_pairs={{0,10},{1,11},{2,8},{3,9},{4,14},{5,15},{6,12},{7,13},{8,2},{9,3},... | collective-permute-start | bytes 98312 | tf_op jit(solution)/shard_map/ppermute | solution.py:373
  63.2 4.8 %collective-permute-start.4 = (f32[64,128]{1,0:T(8,128)S(1)}, f32[64,128]{1,0:T(8,128)S(1)}, u32[]{:S(2)}, u32[]{:S(2)}) collective-permute-start(f32[64,128]{1,0:T(8,128)S(1)} %add.35), channel_id=1, source_target_pairs={{0,8},{1,9},{2,10},{3,11},{4,12},{5,13},{6,14},{7,15},{8,0},{9,1},... | collective-permute-start | bytes 98312 | tf_op jit(solution)/shard_map/ppermute | solution.py:373
  64.8 3.9 %collective-permute-start.3 = (f32[64,128]{1,0:T(8,128)S(1)}, f32[64,128]{1,0:T(8,128)S(1)}, u32[]{:S(2)}, u32[]{:S(2)}) collective-permute-start(f32[64,128]{1,0:T(8,128)S(1)} %add.35), channel_id=1, source_target_pairs={{0,2},{1,3},{2,0},{3,1},{4,6},{5,7},{6,4},{7,5},{8,10},{9,11},{10,... | collective-permute-start | bytes 98312 | tf_op jit(solution)/shard_map/ppermute | solution.py:373
  68.8 7.0 %collective-permute-start.8 = (f32[64,128]{1,0:T(8,128)S(1)}, f32[64,128]{1,0:T(8,128)S(1)}, u32[]{:S(2)}, u32[]{:S(2)}) collective-permute-start(f32[64,128]{1,0:T(8,128)S(1)} %add_add_fusion.mine_ref), channel_id=1, source_target_pairs={{0,28},{1,29},{2,30},{3,31},{4,24},{5,25},{6,26},{7,27},{8,20},{9,... | collective-permute-start | bytes 98312 | tf_op jit(solution)/shard_map/ppermute | solution.py:373
  72.4 5.1 %collective-permute-start.7 = (f32[64,128]{1,0:T(8,128)S(1)}, f32[64,128]{1,0:T(8,128)S(1)}, u32[]{:S(2)}, u32[]{:S(2)}) collective-permute-start(f32[64,128]{1,0:T(8,128)S(1)} %add_add_fusion.mine_ref), channel_id=1, source_target_pairs={{0,24},{1,25},{2,26},{3,27},{4,28},{5,29},{6,30},{7,31},{8,16},{9,... | collective-permute-start | bytes 98312 | tf_op jit(solution)/shard_map/ppermute | solution.py:373
  72.4 5.1 %collective-permute-start.6 = (f32[64,128]{1,0:T(8,128)S(1)}, f32[64,128]{1,0:T(8,128)S(1)}, u32[]{:S(2)}, u32[]{:S(2)}) collective-permute-start(f32[64,128]{1,0:T(8,128)S(1)} %add_add_fusion.mine_ref), channel_id=1, source_target_pairs={{0,4},{1,5},{2,6},{3,7},{4,0},{5,1},{6,2},{7,3},{8,12},{9,13},{10,... | collective-permute-start | bytes 98312 | tf_op jit(solution)/shard_map/ppermute | solution.py:373
